TPU v7x, 32 devices: a whole 2x2x4 slice. The times are simulated.
32 devices in a mesh: groups: 2 (over y), emit: 4 (over z), recv: 4 (over x, core).
Axes of the slice: x: 2, y: 2, z: 4, core: 2. Of those that a mesh axis runs over, the one named last changes fastest.
Arguments:
- positions: float32 [3, 8192], P(None, ('groups', 'emit', 'recv')), parts along dimension 1, may hold values from 0 to 1
- angles: float32 [2, 8192], P(None, ('groups', 'emit', 'recv')), parts along dimension 1, may hold values from -3.140625 to 3.140625
- areas: float32 [8192], P(('groups', 'emit', 'recv')), parts along dimension 0, may hold values from 0.00024414062 to 0.00390625
- emissivity: float32 [8192], P(('groups', 'emit', 'recv')), parts along dimension 0, may hold values from 0.1 to 0.9
- emission: float32 [32, 8192], P(None, ('groups', 'emit', 'recv')), parts along dimension 1, may hold values from 0.5 to 2
- radiosity_in: float32 [32, 8192], P(None, ('groups', 'emit', 'recv')), parts along dimension 1, may hold values from 0.2 to 2
- adjoint_in: float32 [32, 8192], P(None, ('groups', 'emit', 'recv')), parts along dimension 1, may hold values from 0 to 1.5
- visibility: int32 [64, 32], P(('groups', 'emit')), parts along dimension 0, may hold values 0 or 1
- inlet_patches: int32 [4096], P('groups'), parts along dimension 0, may hold values from 0 to 4095
- inlet_weights: float32 [32, 4096], P(None, 'groups'), parts along dimension 1, may hold values from 0.5 to 2
Outputs:
- radiosity_out: float32 [32, 8192], P(None, ('groups', 'emit', 'recv')), parts along dimension 1
- adjoint_out: float32 [32, 8192], P(None, ('groups', 'emit', 'recv')), parts along dimension 1
- emissivity_grad: float32 [8192], P(('groups', 'emit', 'recv')), parts along dimension 0
There are 2 independent parts, one for each index of `groups`. A program takes and returns all parts, laid end to end along the dimension named above; each array names one. Nothing has to cross between parts.
Inputs may be any that keep to these rules, and one draw needn't show every extreme that they name: `inlet_patches`: an inlet patch may be listed more than once.
All inputs are finite; a program needn't handle non-finite values. No bound on the sum of `visibility` on one device may be relied on, other than what follows from the above.
Results may differ from a plain program's by a relative error of at most 0.0003.
Values may be sent and summed in bfloat16 or wider, within the bound.
No kernel may reach another device: no remote copies, remote signals or barrier semaphores. Data moves between devices by JAX's collectives and lax.ppermute only.
A program may use at most 64 MiB of HBM per device.

v0:
```python
import math

import jax
import jax.numpy as jnp
from jax import lax
from jax.sharding import PartitionSpec as P

BLK = 128


def patch_geometry(positions, angles, areas):
    polar = angles[0]
    azimuth = angles[1]
    normal = jnp.stack(
        [jnp.sin(polar) * jnp.cos(azimuth), jnp.sin(polar) * jnp.sin(azimuth), jnp.cos(polar)]
    )
    return jnp.concatenate([positions, normal, areas[None, :]], axis=0)


def view_tile(row_geom, col_geom, block_mask):
    delta_x = col_geom[0][None, :] - row_geom[0][:, None]
    delta_y = col_geom[1][None, :] - row_geom[1][:, None]
    delta_z = col_geom[2][None, :] - row_geom[2][:, None]
    dist_sq = delta_x * delta_x + delta_y * delta_y + delta_z * delta_z
    cos_emit = jnp.maximum(
        row_geom[3][:, None] * delta_x
        + row_geom[4][:, None] * delta_y
        + row_geom[5][:, None] * delta_z,
        0.0,
    )
    cos_recv = jnp.maximum(
        -(
            col_geom[3][None, :] * delta_x
            + col_geom[4][None, :] * delta_y
            + col_geom[5][None, :] * delta_z
        ),
        0.0,
    )
    patch_area = row_geom[6][:, None]
    spread = dist_sq + patch_area
    kernel = cos_emit * cos_recv * patch_area / (math.pi * spread * spread)
    row_blocks, col_blocks = block_mask.shape
    rows_total = row_geom.shape[1]
    cols_total = col_geom.shape[1]
    expanded = jnp.broadcast_to(
        block_mask[:, None, :, None],
        (row_blocks, rows_total // row_blocks, col_blocks, cols_total // col_blocks),
    ).reshape(rows_total, cols_total)
    return (expanded * kernel).astype(jnp.bfloat16)


def block_width():
    return 128


def local(
    positions,
    angles,
    areas,
    emissivity,
    emission,
    radiosity_in,
    adjoint_in,
    visibility,
    inlet_patches,
    inlet_weights,
):
    emit_count = lax.axis_size("emit")
    recv_count = lax.axis_size("recv")
    emit_index = lax.axis_index("emit")
    recv_index = lax.axis_index("recv")
    own_count = areas.shape[0]
    cases = emission.shape[0]
    geometry = patch_geometry(positions, angles, areas)
    reflect = 1.0 - emissivity
    own_weights = (reflect[None, :] * adjoint_in).astype(jnp.bfloat16)
    own_values = radiosity_in.astype(jnp.bfloat16)
    mask_rows = visibility.shape[0]
    per_block = visibility.shape[1] // emit_count
    own_blocks = own_count // BLK
    folded_mask = visibility.astype(jnp.float32).reshape(mask_rows, emit_count, per_block)
    tile_mask = lax.dynamic_slice_in_dim(
        folded_mask, recv_index * own_blocks, own_blocks, 2
    ).reshape(mask_rows, emit_count * own_blocks)
    row_total = own_count * recv_count
    col_total = own_count * emit_count
    row_values = lax.all_gather(own_values, "recv", axis=1, tiled=True)
    col_weight = lax.all_gather(own_weights, "emit", axis=1, tiled=True)
    start_state = (
        jnp.zeros((cases, col_total), jnp.float32),
        jnp.zeros((cases, row_total), jnp.float32),
    )
    col_geom = lax.all_gather(geometry, "emit", axis=1, tiled=True)
    geom_piece = lax.all_gather(geometry, "recv", axis=1, tiled=True)
    count = geom_piece.shape[1]
    width = block_width()

    def inner(number, state):
        fwd_total, adj_total = state
        offset = number * width
        geom_part = lax.dynamic_slice_in_dim(geom_piece, offset, width, 1)
        value_part = lax.dynamic_slice_in_dim(row_values, offset, width, 1)
        mask_part = lax.dynamic_slice_in_dim(tile_mask, offset // BLK, width // BLK, 0)
        tile = view_tile(geom_part, col_geom, mask_part)
        fwd_total = fwd_total + jnp.dot(value_part, tile, preferred_element_type=jnp.float32)
        adj_part = lax.dot_general(
            col_weight, tile, (((1,), (1,)), ((), ())), preferred_element_type=jnp.float32
        )
        adj_total = lax.dynamic_update_slice_in_dim(adj_total, adj_part, offset, 1)
        return (fwd_total, adj_total)

    forward, adjoint = lax.fori_loop(0, count // width, inner, start_state)
    incoming = lax.psum_scatter(forward, "emit", scatter_dimension=1, tiled=True)
    returned = lax.psum_scatter(adjoint, "recv", scatter_dimension=1, tiled=True)
    own_ids = (emit_index * recv_count + recv_index) * own_count + lax.iota(jnp.int32, own_count)
    selector = (inlet_patches[:, None] == own_ids[None, :]).astype(jnp.float32)
    source = jnp.dot(
        inlet_weights, selector, precision=lax.Precision.HIGHEST, preferred_element_type=jnp.float32
    )
    radiosity_out = emissivity[None, :] * emission + reflect[None, :] * incoming
    adjoint_out = source + returned
    emissivity_grad = jnp.sum(adjoint_out * (emission - incoming), axis=0)
    return (radiosity_out, adjoint_out, emissivity_grad)


def solution(mesh):
    placed = (
        P(None, ("groups", "emit", "recv")),
        P(None, ("groups", "emit", "recv")),
        P(("groups", "emit", "recv")),
        P(("groups", "emit", "recv")),
        P(None, ("groups", "emit", "recv")),
        P(None, ("groups", "emit", "recv")),
        P(None, ("groups", "emit", "recv")),
        P(("groups", "emit"), None),
        P("groups"),
        P(None, "groups"),
    )
    return jax.shard_map(
        local,
        mesh=mesh,
        in_specs=placed,
        out_specs=(
            P(None, ("groups", "emit", "recv")),
            P(None, ("groups", "emit", "recv")),
            P(("groups", "emit", "recv")),
        ),
        check_vma=False,
    )
```

profile of v0, /device:TPU:0, one launch (start us, length us, event | category | flops | bytes accessed | tf_op | source)
XLA Modules:
  0.0 115.8 jit_solution(4974398801967030085)
XLA Ops:
  7.2 0.8 slice_cosine_fusion
  8.1 0.7 concatenate.3
  8.8 14.8 %all_gather.14 = f32[7,1024]{1,0:T(8,128)S(1)} all-gather(f32[7,256]{1,0:T(8,128)S(1)} %concatenate.3), channel_id=1, replica_groups=mesh['groups'=2,'emit'=4,'recv'=4] {'emit'}, dimensions={1}, use_global_device_ids=true | all-gather | bytes 35840 | tf_op jit(solution)/shard_map/all_gather | solution.py:93
  23.6 5.2 %all_gather.13 = f32[7,1024]{1,0:T(8,128)S(1)} all-gather(f32[7,256]{1,0:T(8,128)S(1)} %concatenate.3), channel_id=1, replica_groups=mesh['groups'=2,'emit'=4,'recv'=4] {'recv'}, dimensions={1}, use_global_device_ids=true | all-gather | bytes 35840 | tf_op jit(solution)/shard_map/all_gather | solution.py:94
  28.8 0.7 broadcast_subtract_fusion
  29.5 0.7 convert_element_type.21
  30.1 0.1 copy.15
  30.3 0.8 convert_element_type.20
  31.1 5.2 %all_gather.12 = bf16[32,1024]{1,0:T(8,128)(2,1)S(1)} all-gather(bf16[32,256]{1,0:T(8,128)(2,1)S(1)} %convert_element_type.20), channel_id=1, replica_groups=mesh['groups'=2,'emit'=4,'recv'=4] {'recv'}, dimensions={1}, use_global_device_ids=true | all-gather | bytes 81920 | tf_op jit(solution)/shard_map/all_gather | solution.py:87
  36.3 13.1 %all_gather.15 = bf16[32,1024]{1,0:T(8,128)(2,1)S(1)} all-gather(bf16[32,256]{1,0:T(8,128)(2,1)S(1)} %multiply_convert_fusion), channel_id=1, replica_groups=mesh['groups'=2,'emit'=4,'recv'=4] {'emit'}, dimensions={1}, use_global_device_ids=true | all-gather | bytes 81920 | tf_op jit(solution)/shard_map/all_gather | solution.py:88
  49.4 13.7 %while.18 = (s32[]{:T(128)}, f32[32,1024]{1,0:T(8,128)S(1)}, f32[32,1024]{1,0:T(8,128)S(1)}, bf16[32,1024]{1,0:T(8,128)(2,1)S(1)}, f32[8,8]{1,0:T(8,128)S(1)}, /...) while((s32[]{:T(128)}, f32[32,1024]{1,0:T(8,128)S(1)}, ...), condition=%wide.region_1.2_spmd.clone, body=%wide.region_0.1_spmd.clone.sunk | while | flops 24444952 | bytes 484852 | solution.py:112
  49.6 0.8 convolution_add_fusion.2
  50.4 0.8 fusion.47
  51.3 0.8 convolution_add_fusion.2
  52.1 0.8 fusion.47
  53.0 0.8 convolution_add_fusion.2
  53.8 0.8 fusion.47
  54.7 0.8 convolution_add_fusion.2
  55.5 0.8 fusion.47
  56.4 0.8 convolution_add_fusion.2
  57.2 0.8 fusion.47
  58.1 0.8 convolution_add_fusion.2
  58.9 0.8 fusion.47
  59.8 0.8 convolution_add_fusion.2
  60.6 0.8 fusion.47
  61.5 0.8 convolution_add_fusion.2
  62.4 0.8 fusion.47
  63.2 0.6 copy-done.1
  63.9 0.7 reduce-scatter.3.cloned.1.call-update
  64.6 20.0 %reduce-scatter.5.cloned.1.call-done = f32[32,256]{1,0:T(8,128)} async-done(((f32[32,1024]{1,0:T(8,128)}), f32[32,256]{1,0:T(8,128)}) %reduce-scatter.5.cloned.1.call-update) | async-done | bytes 32784 | tf_op jit(solution)/shard_map/reduce_scatter | solution.py:114
  84.6 21.6 %reduce-scatter.3.cloned.1.call-done = f32[32,256]{1,0:T(8,128)} async-done(((f32[32,1024]{1,0:T(8,128)}), f32[32,256]{1,0:T(8,128)}) %reduce-scatter.3.cloned.1.call-update) | async-done | bytes 32784 | tf_op jit(solution)/shard_map/reduce_scatter | solution.py:113
  106.2 2.8 %multiply_reduce_fusion = (f32[256]{0:T(256)}, f32[32,256]{1,0:T(8,128)}, f32[32,256]{1,0:T(8,128)}) fusion(f32[32,256]{1,0:T(8,128)S(1)} %copy-done.5, f32[32,256]{1,0:T(8,128)} %reduce-scatter.3.cloned.1.call-done, f32[256]{0:T(256)S(1)} %broadcast_subtract_fusion, f32[256]{0:T(256)S(1)} %copy-done.4, f32[32,256]{1,0:T(8,128)} %reduce-scatter.5.cloned.1.call-done, ...), kind=kOutput, calls=%fused_computation.47 | convolution fusion | flops 201907968 | bytes 438272 | tf_op jit(solution)/shard_map/dot_general | solution.py:117
  (62 shorter events, 1.1 us)
Async XLA Ops:
  7.2 99.0 %copy-start = (f32[32,2048]{1,0:T(8,128)S(1)}, f32[32,2048]{1,0:T(8,128)}, u32[]{:S(2)}) copy-start(f32[32,2048]{1,0:T(8,128)} %param.21) | copy-start | bytes 786436
  7.2 29.1 %copy-start.3 = (f32[32,256]{1,0:T(8,128)S(1)}, f32[32,256]{1,0:T(8,128)}, u32[]{:S(2)}) copy-start(f32[32,256]{1,0:T(8,128)} %param.18) | copy-start | bytes 98308
  7.2 77.4 %reduce-scatter.5.cloned.1.call-start = ((), (), s32[]{:S(2)}) async-start(), calls=%async_computation.3 | async-start | bytes 163840 | tf_op jit(solution)/shard_map/reduce_scatter | solution.py:114
  63.1 0.7 copy-start.1
  63.1 0.7 copy-start.2
  63.1 43.0 %copy-start.4 = (f32[256]{0:T(256)S(1)}, f32[256]{0:T(256)}, u32[]{:S(2)}) copy-start(f32[256]{0:T(256)} %param.15) | copy-start | bytes 3076
  63.2 43.0 %copy-start.5 = (f32[32,256]{1,0:T(8,128)S(1)}, f32[32,256]{1,0:T(8,128)}, u32[]{:S(2)}) copy-start(f32[32,256]{1,0:T(8,128)} %param.16) | copy-start | bytes 98308
  63.2 43.0 %copy-start.6 = (s32[2048]{0:T(1024)S(1)}, s32[2048]{0:T(1024)}, u32[]{:S(2)}) copy-start(s32[2048]{0:T(1024)} %param.20) | copy-start | bytes 24580
  63.8 42.3 %reduce-scatter.3.cloned.1.call-start = ((), (), s32[]{:S(2)}) async-start(), calls=%async_computation.2 | async-start | bytes 163840 | tf_op jit(solution)/shard_map/reduce_scatter | solution.py:113
Sparse Core Ops, SparseCore 0:
  63.9 20.5 reduce-scatter.4
  86.9 19.1 reduce-scatter.2
where the time goes:
time: 116 us
  waiting for transfers between devices  42.3 us (36%)
  blocking collectives  38.3 us (33%)
  matrix products  15.3 us (13%)
  between operations  14.1 us (12%)
  other arithmetic  2.97 us (3%)
  local copies, waits for them, and re-layouts  2.42 us (2%)
    reduce_scatter x1, waiting for transfers between devices, local(): lax.psum_scatter(forward, 'emit', scatter_dimension=1, tiled=True)  21.6 us
    reduce_scatter x1, waiting for transfers between devices, local(): lax.psum_scatter(adjoint, 'recv', scatter_dimension=1, tiled=True)  20 us
    all_gather x1, blocking collectives, local(): col_geom = lax.all_gather(geometry, 'emit', axis=1, tiled=True)  14.8 us
    all_gather x1, blocking collectives, local(): col_weight = lax.all_gather(own_weights, 'emit', axis=1, tiled=True)  13.1 us
    dot_general x8, matrix products, inner(): jnp.dot(value_part, tile, preferred_element_type=jnp.float32)  6.43 us
    dot_general x8, matrix products, inner(): lax.dot_general(col_weight, tile, (((1,), (1,)), ((), ())), preferred_ele...  6.15 us
    all_gather x1, blocking collectives, local(): row_values = lax.all_gather(own_values, 'recv', axis=1, tiled=True)  5.23 us
    all_gather x1, blocking collectives, local(): geom_piece = lax.all_gather(geometry, 'recv', axis=1, tiled=True)  5.18 us
  transfers between devices with their start and end apart: 2, of which 2 were waited for; matrix products, arithmetic and copies ran while one was open for 0% of the time, Pallas kernels for 0%

commit v1 on v0

v1 whole, which is shorter than its diff:
```python
import functools
import math

import jax
import jax.numpy as jnp
import numpy as np
from jax import lax
from jax.experimental import pallas as pl
from jax.experimental.pallas import tpu as pltpu
from jax.sharding import PartitionSpec as P

BLK = 128
GEO = 32
FEAT = 128
ROWS = 32
NT = (((1,), (1,)), ((), ()))
TN = (((0,), (0,)), ((), ()))


def selection():
    pick = np.zeros((GEO, 2 * FEAT + 4 * BLK), np.float32)
    for part in range(3):
        base = part * GEO
        for split in range(3):
            for axis in range(3):
                pick[9 + 3 * part + axis, base + 3 * split + axis] = 1.0
                pick[3 * part + axis, FEAT + base + 9 + 3 * split + axis] = 1.0
        pick[18 + part, base + 21] = 1.0
        pick[21, FEAT + 18 + part] = 1.0
        for axis in range(3):
            first = 2 * FEAT + axis * BLK
            pick[3 * part + axis, first : first + BLK] = 1.0
        first = 2 * FEAT + 3 * BLK
        pick[22 + part, first : first + BLK] = 1.0
    return pick


def parts(x):
    high = x.astype(jnp.bfloat16).astype(jnp.float32)
    rest = x - high
    middle = rest.astype(jnp.bfloat16).astype(jnp.float32)
    return high, middle, rest - middle


def pack_kernel(positions, angles, areas, emissivity, radiosity, adjoint, row_ref, col_ref, geo):
    place = positions[...]
    turn = angles[...]
    sines = jnp.sin(turn)
    cosines = jnp.cos(turn)
    normal = jnp.concatenate(
        [sines[0:1] * cosines[1:2], sines[0:1] * sines[1:2], cosines[0:1]], axis=0
    )
    product = normal * place
    offset = -(product[0:1] + product[1:2] + product[2:3])
    geo[...] = jnp.zeros_like(geo)
    for number, (a, b, c, d) in enumerate(
        zip(parts(place), parts(normal), parts(offset), parts(areas[...]))
    ):
        geo[3 * number : 3 * number + 3, :] = a
        geo[9 + 3 * number : 12 + 3 * number, :] = b
        geo[18 + number : 19 + number, :] = c
        geo[22 + number : 23 + number, :] = d
    geo[21:22, :] = jnp.ones_like(offset)
    packed = geo[...].astype(jnp.bfloat16)
    cases = radiosity.shape[0]
    row_ref[0:cases, :] = radiosity[...].astype(jnp.bfloat16)
    row_ref[cases:, :] = packed
    col_ref[0:cases, :] = ((1.0 - emissivity[...]) * adjoint[...]).astype(jnp.bfloat16)
    col_ref[cases:, :] = packed


def source_kernel(ids, weights, out_ref, *, axes):
    own = out_ref.shape[1]
    first = (lax.axis_index(axes[0]) * lax.axis_size(axes[1]) + lax.axis_index(axes[1])) * own
    local = ids[...] - first
    step = 512
    total = jnp.zeros(out_ref.shape, jnp.float32)
    for start in range(0, ids.shape[1], step):
        here = local[:, start : start + step]
        hit = lax.broadcasted_iota(jnp.int32, (own, step), 0) == here
        chosen = jnp.where(hit, 1.0, 0.0).astype(jnp.bfloat16)
        for piece in parts(weights[:, start : start + step]):
            total = total + lax.dot_general(
                piece.astype(jnp.bfloat16), chosen, NT, preferred_element_type=jnp.float32
            )
    out_ref[...] = total


def tile_kernel(*refs, nr, nz):
    pick, seen = refs[0], refs[1]
    rows = refs[2 : 2 + nr]
    cols = refs[2 + nr : 2 + nr + nz]
    fwd = refs[2 + nr + nz : 2 + nr + 2 * nz]
    adj = refs[2 + nr + 2 * nz : 2 + 2 * nr + 2 * nz]
    left, wide, values, right, weights, places, ce, cr, tile, fwd_sum, adj_sum = refs[2 + 2 * nr + 2 * nz :]
    me_r = lax.axis_index("recv")
    me_z = lax.axis_index("emit")
    own = rows[0].shape[1]
    cases = rows[0].shape[0] - GEO
    for s in range(nr):
        feature = lax.dot_general(rows[s][cases:, :], pick[...], TN, preferred_element_type=jnp.float32)
        left[s] = feature[:, : 2 * FEAT].astype(jnp.bfloat16)
        wide[s, :, : 3 * BLK] = feature[:, 2 * FEAT : 2 * FEAT + 3 * BLK]
        wide[s, :, 3 * BLK :] = feature[:, 2 * FEAT + 3 * BLK :]
        values[s] = rows[s][0:cases, :]
        adj_sum[s] = jnp.zeros((cases, own), jnp.float32)
    for z in range(nz):
        geometry = cols[z][cases:, :]
        right[z] = jnp.concatenate([geometry, geometry, geometry, jnp.zeros_like(geometry)], axis=0)
        weights[z] = cols[z][0:cases, :]
        exact = geometry.astype(jnp.float32)
        places[z, 0:3, :] = exact[0:3] + exact[3:6] + exact[6:9]
        fwd_sum[z] = jnp.zeros((cases, own), jnp.float32)

    def pair(number, _):
        z = number // nr
        s = number % nr
        from_r = me_r ^ s
        to_z = me_z ^ z
        ce[...] = jnp.dot(left[s, :, :FEAT], right[z], preferred_element_type=jnp.float32)
        cr[...] = jnp.dot(left[s, :, FEAT:], right[z], preferred_element_type=jnp.float32)
        per = own // BLK
        for jb in range(per):
            lanes = slice(jb * BLK, (jb + 1) * BLK)
            xj = places[z, 0:1, lanes]
            yj = places[z, 1:2, lanes]
            zj = places[z, 2:3, lanes]
            for ib in range(per):
                sees = seen[from_r * per + ib, (to_z * nr + me_r) * per + jb].astype(jnp.float32)
                scale = sees * (1.0 / math.pi)
                for start in range(ib * BLK, (ib + 1) * BLK, ROWS):
                    here = slice(start, start + ROWS)
                    dx = wide[s, here, 0:BLK] - xj
                    dy = wide[s, here, BLK : 2 * BLK] - yj
                    dz = wide[s, here, 2 * BLK : 3 * BLK] - zj
                    area = wide[s, here, 3 * BLK :]
                    spread = dx * dx + dy * dy + dz * dz + area
                    product = jnp.maximum(ce[here, lanes], 0.0) * jnp.maximum(cr[here, lanes], 0.0)
                    view = product * (area * scale) / (spread * spread)
                    tile[here, lanes] = view.astype(jnp.bfloat16)
        fwd_sum[z] = fwd_sum[z] + jnp.dot(values[s], tile[...], preferred_element_type=jnp.float32)
        adj_sum[s] = adj_sum[s] + lax.dot_general(weights[z], tile[...], NT, preferred_element_type=jnp.float32)
        return 0

    lax.fori_loop(0, nr * nz, pair, 0)
    for s in range(nr):
        adj[s][...] = adj_sum[s]
    for z in range(nz):
        fwd[z][...] = fwd_sum[z]


def finish_kernel(*refs, nr, nz):
    emissivity, emission, source = refs[0:3]
    fwd = refs[3 : 3 + nz]
    adj = refs[3 + nz : 3 + nz + nr]
    radiosity_out, adjoint_out, gradient = refs[3 + nz + nr :]
    incoming = fwd[0][...]
    for piece in fwd[1:]:
        incoming = incoming + piece[...]
    returned = source[...]
    for piece in adj:
        returned = returned + piece[...]
    mine = emissivity[...]
    power = emission[...]
    radiosity_out[...] = mine * power + (1.0 - mine) * incoming
    adjoint_out[...] = returned
    gradient[...] = jnp.sum(returned * (power - incoming), axis=0, keepdims=True)


def swap(x, axis, other):
    if other == 0:
        return x
    return lax.ppermute(x, axis, [(i, i ^ other) for i in range(lax.axis_size(axis))])


def local(
    positions,
    angles,
    areas,
    emissivity,
    emission,
    radiosity_in,
    adjoint_in,
    visibility,
    inlet_patches,
    inlet_weights,
):
    nz = lax.axis_size("emit")
    nr = lax.axis_size("recv")
    own = areas.shape[0]
    cases = emission.shape[0]
    mine = emissivity.reshape(1, own)
    vmem = pl.BlockSpec(memory_space=pltpu.VMEM)
    smem = pl.BlockSpec(memory_space=pltpu.SMEM)
    packed = jax.ShapeDtypeStruct((cases + GEO, own), jnp.bfloat16)
    sums = jax.ShapeDtypeStruct((cases, own), jnp.float32)
    row_pack, col_pack = pl.pallas_call(
        pack_kernel,
        out_shape=(packed, packed),
        in_specs=[vmem] * 6,
        out_specs=(vmem, vmem),
        scratch_shapes=[pltpu.VMEM((GEO, own), jnp.float32)],
    )(positions, angles, areas.reshape(1, own), mine, radiosity_in, adjoint_in)
    rows = [swap(row_pack, "recv", k) for k in range(nr)]
    cols = [swap(col_pack, "emit", k) for k in range(nz)]
    source = pl.pallas_call(
        functools.partial(source_kernel, axes=("emit", "recv")),
        out_shape=sums,
        in_specs=[vmem] * 2,
        out_specs=vmem,
    )(inlet_patches.reshape(1, -1), inlet_weights)
    partial = pl.pallas_call(
        functools.partial(tile_kernel, nr=nr, nz=nz),
        out_shape=(sums,) * (nz + nr),
        in_specs=[vmem, smem] + [vmem] * (nr + nz),
        out_specs=(vmem,) * (nz + nr),
        scratch_shapes=[
            pltpu.VMEM((nr, own, 2 * FEAT), jnp.bfloat16),
            pltpu.VMEM((nr, own, 4 * BLK), jnp.float32),
            pltpu.VMEM((nr, cases, own), jnp.bfloat16),
            pltpu.VMEM((nz, FEAT, own), jnp.bfloat16),
            pltpu.VMEM((nz, cases, own), jnp.bfloat16),
            pltpu.VMEM((nz, 8, own), jnp.float32),
            pltpu.VMEM((own, own), jnp.float32),
            pltpu.VMEM((own, own), jnp.float32),
            pltpu.VMEM((own, own), jnp.bfloat16),
            pltpu.VMEM((nz, cases, own), jnp.float32),
            pltpu.VMEM((nr, cases, own), jnp.float32),
        ],
        compiler_params=pltpu.CompilerParams(vmem_limit_bytes=24 << 20),
    )(jnp.asarray(selection(), jnp.bfloat16), visibility, *rows, *cols)
    fwd = [swap(partial[k], "emit", k) for k in range(nz)]
    adj = [swap(partial[nz + k], "recv", k) for k in range(nr)]
    radiosity_out, adjoint_out, gradient = pl.pallas_call(
        functools.partial(finish_kernel, nr=nr, nz=nz),
        out_shape=(sums, sums, jax.ShapeDtypeStruct((1, own), jnp.float32)),
        in_specs=[vmem] * (3 + nz + nr),
        out_specs=(vmem, vmem, vmem),
    )(mine, emission, source, *fwd, *adj)
    return radiosity_out, adjoint_out, gradient.reshape(own)


def solution(mesh):
    patch = ("groups", "emit", "recv")
    placed = (
        P(None, patch),
        P(None, patch),
        P(patch),
        P(patch),
        P(None, patch),
        P(None, patch),
        P(None, patch),
        P(("groups", "emit"), None),
        P("groups"),
        P(None, "groups"),
    )
    return jax.shard_map(
        local,
        mesh=mesh,
        in_specs=placed,
        out_specs=(P(None, patch), P(None, patch), P(patch)),
        check_vma=False,
    )
```

time: 116 us -> 37.2 us (0.32)
  blocking collectives: 38.3 us -> 0 us
  waiting for transfers between devices: 42.3 us -> 5.92 us
  matrix products: 15.3 us -> 0 us
  between operations: 14.1 us -> 0.77 us
  starting transfers between devices: 0.08 us -> 13.4 us
  Pallas kernels: 0 us -> 13.3 us
  other arithmetic: 2.97 us -> 0 us
    reduce_scatter x2 -> x0, waiting for transfers between devices: 41.6 us -> none  [the longest x1 21.6 us: local(): lax.psum_scatter(forward, 'emit', scatter_dimension=1, tiled=True)]
    all_gather x4 -> x0, blocking collectives: 38.3 us -> none  [the longest x1 14.8 us: local(): col_geom = lax.all_gather(geometry, 'emit', axis=1, tiled=True)]
    dot_general x17 -> x0, matrix products: 15.3 us -> none  [the longest x8 6.43 us: inner(): jnp.dot(value_part, tile, preferred_element_type=jnp.float32)]
    ppermute x0 -> x12, starting transfers between devices: none -> 13.4 us  [swap(): lax.ppermute(x, axis, [(i, i ^ other) for i in range(lax.axis_size(axis))])]
    pallas_call x0 -> x4, Pallas kernels: none -> 13.3 us  [the longest x1 7.57 us: local(): pl.pallas_call(functools.partial(tile_kernel, nr=nr, nz=nz), out_shape=(s...]
    ppermute x0 -> x12, waiting for transfers between devices: none -> 5.92 us  [swap(): lax.ppermute(x, axis, [(i, i ^ other) for i in range(lax.axis_size(axis))])]
    unnamed x15 -> x24, local copies, waits for them, and re-layouts: 0.72 us -> 3.36 us
    convert_element_type x3 -> x0, other arithmetic: 1.46 us -> none  [the longest x1 0.76 us: local(): own_values = radiosity_in.astype(jnp.bfloat16)]
  transfers between devices with their start and end apart: 2 -> 12, of which waited for: 2 -> 2; matrix products, arithmetic and copies ran while one was open for 0% -> 0% of each run, Pallas kernels for 0% -> 7%
where the time goes in v1:
time: 37.2 us; the launch traced here: 36.8 us
  starting transfers between devices  13.4 us (36%)
  Pallas kernels  13.3 us (36%)
  waiting for transfers between devices  5.92 us (16%)
  local copies, waits for them, and re-layouts  3.36 us (9%)
  between operations  0.77 us (2%)
    ppermute x12, starting transfers between devices, swap(): lax.ppermute(x, axis, [(i, i ^ other) for i in range(lax.axis_size(axis))])  13.4 us
    pallas_call x1, Pallas kernels, local(): pl.pallas_call(functools.partial(tile_kernel, nr=nr, nz=nz), out_shape=(s...  7.57 us
    ppermute x12, waiting for transfers between devices, swap(): lax.ppermute(x, axis, [(i, i ^ other) for i in range(lax.axis_size(axis))])  5.92 us
    unnamed x24, local copies, waits for them, and re-layouts  3.36 us
    pallas_call x1, Pallas kernels, local(): pl.pallas_call(functools.partial(source_kernel, axes=('emit', 'recv')), o...  2.65 us
    pallas_call x1, Pallas kernels, local(): pl.pallas_call(functools.partial(finish_kernel, nr=nr, nz=nz), out_shape=...  1.57 us
    pallas_call x1, Pallas kernels, local(): pl.pallas_call(pack_kernel, out_shape=(packed, packed), in_specs=[vmem] *...  1.56 us
  transfers between devices with their start and end apart: 12, of which 2 were waited for; matrix products, arithmetic and copies ran while one was open for 0% of the time, Pallas kernels for 7%

profile of v1, /device:TPU:0, one launch (start us, length us, event | category | flops | bytes accessed | tf_op | source)
XLA Modules:
  0.0 36.8 jit_solution(5492169188181188942)
XLA Ops:
  0.6 0.0 copy-start
  0.7 1.6 %shard_map.131 = (bf16[64,256]{1,0:T(8,128)(2,1)}, bf16[64,256]{1,0:T(8,128)(2,1)}) custom-call(f32[3,256]{1,0:T(4,128)} %positions.1, f32[2,256]{1,0:T(2,128)} %angles.1, f32[1,256]{1,0:T(1,128)} %bitcast.7, f32[1,256]{1,0:T(1,128)} %bitcast.5, f32[32,256]{1,0:T(8,128)} %radiosity.1, f32[32,256]{1,0:T(8,128)} %adjoint.1), custom_call_target="tpu_custom_call" | custom-call | tf_op jit(solution)/shard_map/pallas_call | solution.py:197
  2.2 0.5 %collective-permute-start = (bf16[64,256]{1,0:T(8,128)(2,1)}, bf16[64,256]{1,0:T(8,128)(2,1)S(1)}, u32[]{:S(2)}, u32[]{:S(2)}) collective-permute-start(bf16[64,256]{1,0:T(8,128)(2,1)} %get-tuple-element.16.refs_2_), channel_id=1, source_target_pairs={{0,1},{1,0},{2,3},{3,2},{4,5},{5,4},{6,7},{7,6},{8,9},{9,8},{10,11... | collective-permute-start | bytes 98312 | tf_op jit(solution)/shard_map/ppermute | solution.py:173
  2.7 2.5 %collective-permute-start.1 = (bf16[64,256]{1,0:T(8,128)(2,1)}, bf16[64,256]{1,0:T(8,128)(2,1)S(1)}, u32[]{:S(2)}, u32[]{:S(2)}) collective-permute-start(bf16[64,256]{1,0:T(8,128)(2,1)} %get-tuple-element.16.refs_2_), channel_id=1, source_target_pairs={{0,2},{1,3},{2,0},{3,1},{4,6},{5,7},{6,4},{7,5},{8,10},{9,11},{10,... | collective-permute-start | bytes 98312 | tf_op jit(solution)/shard_map/ppermute | solution.py:173
  5.2 0.1 collective-permute-start.2
  5.3 1.8 %collective-permute-start.3 = (bf16[64,256]{1,0:T(8,128)(2,1)}, bf16[64,256]{1,0:T(8,128)(2,1)S(1)}, u32[]{:S(2)}, u32[]{:S(2)}) collective-permute-start(bf16[64,256]{1,0:T(8,128)(2,1)} %get-tuple-element.17.refs_6_), channel_id=1, source_target_pairs={{0,4},{4,0},{8,12},{12,8},{1,5},{5,1},{9,13},{13,9},{2,6},{6,2},{1... | collective-permute-start | bytes 98312 | tf_op jit(solution)/shard_map/ppermute | solution.py:173
  7.1 2.6 %collective-permute-start.4 = (bf16[64,256]{1,0:T(8,128)(2,1)}, bf16[64,256]{1,0:T(8,128)(2,1)S(1)}, u32[]{:S(2)}, u32[]{:S(2)}) collective-permute-start(bf16[64,256]{1,0:T(8,128)(2,1)} %get-tuple-element.17.refs_6_), channel_id=1, source_target_pairs={{0,8},{4,12},{8,0},{12,4},{1,9},{5,13},{9,1},{13,5},{2,10},{6,14},... | collective-permute-start | bytes 98312 | tf_op jit(solution)/shard_map/ppermute | solution.py:173
  9.7 0.0 collective-permute-done.refs_3_
  9.7 0.0 collective-permute-start.5
  9.7 0.0 collective-permute-done.1.refs_4_
  9.7 0.0 collective-permute-done.3.refs_7_
  9.7 2.9 %collective-permute-done.4.refs_8_ = bf16[64,256]{1,0:T(8,128)(2,1)S(1)} collective-permute-done((bf16[64,256]{1,0:T(8,128)(2,1)}, bf16[64,256]{1,0:T(8,128)(2,1)S(1)}, u32[]{:S(2)}, u32[]{:S(2)}) %collective-permute-start.4) | collective-permute-done | bytes 32800 | tf_op jit(solution)/shard_map/ppermute | solution.py:173
  12.7 2.9 %collective-permute-done.5.refs_9_ = bf16[64,256]{1,0:T(8,128)(2,1)S(1)} collective-permute-done((bf16[64,256]{1,0:T(8,128)(2,1)}, bf16[64,256]{1,0:T(8,128)(2,1)S(1)}, u32[]{:S(2)}, u32[]{:S(2)}) %collective-permute-start.5) | collective-permute-done | bytes 32800 | tf_op jit(solution)/shard_map/ppermute | solution.py:173
  15.6 0.8 %copy-done.3 = bf16[64,256]{1,0:T(8,128)(2,1)S(1)} copy-done((bf16[64,256]{1,0:T(8,128)(2,1)S(1)}, bf16[64,256]{1,0:T(8,128)(2,1)}, u32[]{:S(2)}) %copy-start.3) | copy-done | bytes 32792
  16.4 0.8 %copy-done.4 = bf16[64,256]{1,0:T(8,128)(2,1)S(1)} copy-done((bf16[64,256]{1,0:T(8,128)(2,1)S(1)}, bf16[64,256]{1,0:T(8,128)(2,1)}, u32[]{:S(2)}) %copy-start.4) | copy-done | bytes 32792
  17.1 7.6 %shard_map.132 = (f32[32,256]{1,0:T(8,128)S(1)}, f32[32,256]{1,0:T(8,128)S(1)}, f32[32,256]{1,0:T(8,128)S(1)}, f32[32,256]{1,0:T(8,128)S(1)}, f32[32,256]{1,0:T(...) custom-call(bf16[32,768]{1,0:T(8,128)(2,1)S(1)} %copy-done, ...), custom_call_target="tpu_custom_call" | custom-call | tf_op jit(solution)/shard_map/pallas_call | solution.py:212
  24.7 0.6 %copy-done.1 = f32[32,256]{1,0:T(8,128)} copy-done((f32[32,256]{1,0:T(8,128)}, f32[32,256]{1,0:T(8,128)S(1)}, u32[]{:S(2)}) %copy-start.1) | copy-done | bytes 32792
  25.3 0.6 %copy-done.2 = f32[32,256]{1,0:T(8,128)} copy-done((f32[32,256]{1,0:T(8,128)}, f32[32,256]{1,0:T(8,128)S(1)}, u32[]{:S(2)}) %copy-start.2) | copy-done | bytes 32792
  25.9 1.5 %collective-permute-start.10 = (f32[32,256]{1,0:T(8,128)S(1)}, f32[32,256]{1,0:T(8,128)S(1)}, u32[]{:S(2)}, u32[]{:S(2)}) collective-permute-start(f32[32,256]{1,0:T(8,128)S(1)} %get-tuple-element.24), channel_id=1, source_target_pairs={{0,2},{1,3},{2,0},{3,1},{4,6},{5,7},{6,4},{7,5},{8,10},{9,11},{10,... | collective-permute-start | bytes 98312 | tf_op jit(solution)/shard_map/ppermute | solution.py:173
  27.4 1.0 %collective-permute-start.7 = (f32[32,256]{1,0:T(8,128)S(1)}, f32[32,256]{1,0:T(8,128)S(1)}, u32[]{:S(2)}, u32[]{:S(2)}) collective-permute-start(f32[32,256]{1,0:T(8,128)S(1)} %get-tuple-element.20), channel_id=1, source_target_pairs={{0,8},{4,12},{8,0},{12,4},{1,9},{5,13},{9,1},{13,5},{2,10},{6,14},... | collective-permute-start | bytes 98312 | tf_op jit(solution)/shard_map/ppermute | solution.py:173
  28.4 3.4 %collective-permute-start.8 = (f32[32,256]{1,0:T(8,128)S(1)}, f32[32,256]{1,0:T(8,128)S(1)}, u32[]{:S(2)}, u32[]{:S(2)}) collective-permute-start(f32[32,256]{1,0:T(8,128)S(1)} %get-tuple-element.21), channel_id=1, source_target_pairs={{0,12},{4,8},{8,4},{12,0},{1,13},{5,9},{9,5},{13,1},{2,14},{6,10},... | collective-permute-start | bytes 98312 | tf_op jit(solution)/shard_map/ppermute | solution.py:173
  31.8 0.0 collective-permute-done.10.refs_9_
  31.8 0.0 collective-permute-start.9
  31.8 2.6 %shard_map.130.refs_2_ = f32[32,256]{1,0:T(8,128)} custom-call(s32[1,2048]{1,0:T(1,128)} %bitcast.4, f32[32,2048]{1,0:T(8,128)} %weights.1), custom_call_target="tpu_custom_call" | custom-call | tf_op jit(solution)/shard_map/pallas_call | solution.py:206
  34.5 0.0 collective-permute-done.11.refs_10_
  34.5 0.0 collective-permute-done.7.refs_5_
  34.6 0.5 %copy-done.7 = f32[32,256]{1,0:T(8,128)} copy-done((f32[32,256]{1,0:T(8,128)}, f32[32,256]{1,0:T(8,128)S(1)}, u32[]{:S(2)}) %copy-start.7) | copy-done | bytes 32792
  35.1 0.0 copy-done.8
  35.1 0.0 copy-done.9
  35.2 0.0 copy-done.10
  35.2 0.0 copy-done.11
  35.2 1.6 %shard_map.133 = (f32[32,256]{1,0:T(8,128)}, f32[32,256]{1,0:T(8,128)}, f32[1,256]{1,0:T(1,128)}) custom-call(f32[1,256]{1,0:T(1,128)} %bitcast.6, f32[32,256]{1,0:T(8,128)} %refs_1_.3, f32[32,256]{1,0:T(8,128)} %shard_map.130.refs_2_, f32[32,256]{1,0:T(8,128)} %copy-done.1, f32[32,256]{1,0:T(8,128)} %copy-done.8, f32[32,256]{1,0:T(8,128)} %copy-done.9, ...), custom_call_target="tpu_custom_call" | custom-call | tf_op jit(solution)/shard_map/pallas_call | solution.py:234
  (20 shorter events, 0.0 us)
Async XLA Ops:
  0.6 15.0 %copy-start = (bf16[32,768]{1,0:T(8,128)(2,1)S(1)}, bf16[32,768]{1,0:T(8,128)(2,1)}, u32[]{:S(2)}) copy-start(bf16[32,768]{1,0:T(8,128)(2,1)} %constant.2.clone.refs_0_) | copy-start | bytes 147460
  0.6 15.0 %copy-start.5 = (s32[8,32]{1,0:T(8,128)S(1)}, s32[8,32]{1,0:T(8,128)}, u32[]{:S(2)}) copy-start(s32[8,32]{1,0:T(8,128)} %refs_1_.2) | copy-start | bytes 3076
  2.2 7.5 %collective-permute-start = (bf16[64,256]{1,0:T(8,128)(2,1)}, bf16[64,256]{1,0:T(8,128)(2,1)S(1)}, u32[]{:S(2)}, u32[]{:S(2)}) collective-permute-start(bf16[64,256]{1,0:T(8,128)(2,1)} %get-tuple-element.16.refs_2_), channel_id=1, source_target_pairs={{0,1},{1,0},{2,3},{3,2},{4,5},{5,4},{6,7},{7,6},{8,9},{9,8},{10,11... | collective-permute-start | bytes 98312 | tf_op jit(solution)/shard_map/ppermute | solution.py:173
  2.7 7.0 %collective-permute-start.1 = (bf16[64,256]{1,0:T(8,128)(2,1)}, bf16[64,256]{1,0:T(8,128)(2,1)S(1)}, u32[]{:S(2)}, u32[]{:S(2)}) collective-permute-start(bf16[64,256]{1,0:T(8,128)(2,1)} %get-tuple-element.16.refs_2_), channel_id=1, source_target_pairs={{0,2},{1,3},{2,0},{3,1},{4,6},{5,7},{6,4},{7,5},{8,10},{9,11},{10,... | collective-permute-start | bytes 98312 | tf_op jit(solution)/shard_map/ppermute | solution.py:173
  5.2 4.5 %collective-permute-start.2 = (bf16[64,256]{1,0:T(8,128)(2,1)}, bf16[64,256]{1,0:T(8,128)(2,1)S(1)}, u32[]{:S(2)}, u32[]{:S(2)}) collective-permute-start(bf16[64,256]{1,0:T(8,128)(2,1)} %get-tuple-element.16.refs_2_), channel_id=1, source_target_pairs={{0,3},{1,2},{2,1},{3,0},{4,7},{5,6},{6,5},{7,4},{8,11},{9,10},{10,... | collective-permute-start | bytes 98312 | tf_op jit(solution)/shard_map/ppermute | solution.py:173
  5.3 4.4 %collective-permute-start.3 = (bf16[64,256]{1,0:T(8,128)(2,1)}, bf16[64,256]{1,0:T(8,128)(2,1)S(1)}, u32[]{:S(2)}, u32[]{:S(2)}) collective-permute-start(bf16[64,256]{1,0:T(8,128)(2,1)} %get-tuple-element.17.refs_6_), channel_id=1, source_target_pairs={{0,4},{4,0},{8,12},{12,8},{1,5},{5,1},{9,13},{13,9},{2,6},{6,2},{1... | collective-permute-start | bytes 98312 | tf_op jit(solution)/shard_map/ppermute | solution.py:173
  7.1 5.6 %collective-permute-start.4 = (bf16[64,256]{1,0:T(8,128)(2,1)}, bf16[64,256]{1,0:T(8,128)(2,1)S(1)}, u32[]{:S(2)}, u32[]{:S(2)}) collective-permute-start(bf16[64,256]{1,0:T(8,128)(2,1)} %get-tuple-element.17.refs_6_), channel_id=1, source_target_pairs={{0,8},{4,12},{8,0},{12,4},{1,9},{5,13},{9,1},{13,5},{2,10},{6,14},... | collective-permute-start | bytes 98312 | tf_op jit(solution)/shard_map/ppermute | solution.py:173
  9.7 5.9 %collective-permute-start.5 = (bf16[64,256]{1,0:T(8,128)(2,1)}, bf16[64,256]{1,0:T(8,128)(2,1)S(1)}, u32[]{:S(2)}, u32[]{:S(2)}) collective-permute-start(bf16[64,256]{1,0:T(8,128)(2,1)} %get-tuple-element.17.refs_6_), channel_id=1, source_target_pairs={{0,12},{4,8},{8,4},{12,0},{1,13},{5,9},{9,5},{13,1},{2,14},{6,10},... | collective-permute-start | bytes 98312 | tf_op jit(solution)/shard_map/ppermute | solution.py:173
  15.6 0.8 %copy-start.3 = (bf16[64,256]{1,0:T(8,128)(2,1)S(1)}, bf16[64,256]{1,0:T(8,128)(2,1)}, u32[]{:S(2)}) copy-start(bf16[64,256]{1,0:T(8,128)(2,1)} %get-tuple-element.16.refs_2_) | copy-start | bytes 98308
  16.4 0.8 %copy-start.4 = (bf16[64,256]{1,0:T(8,128)(2,1)S(1)}, bf16[64,256]{1,0:T(8,128)(2,1)}, u32[]{:S(2)}) copy-start(bf16[64,256]{1,0:T(8,128)(2,1)} %get-tuple-element.17.refs_6_) | copy-start | bytes 98308
  24.7 0.6 %copy-start.1 = (f32[32,256]{1,0:T(8,128)}, f32[32,256]{1,0:T(8,128)S(1)}, u32[]{:S(2)}) copy-start(f32[32,256]{1,0:T(8,128)S(1)} %get-tuple-element.18.refs_3_) | copy-start | bytes 98308
  25.3 0.6 %copy-start.2 = (f32[32,256]{1,0:T(8,128)}, f32[32,256]{1,0:T(8,128)S(1)}, u32[]{:S(2)}) copy-start(f32[32,256]{1,0:T(8,128)S(1)} %get-tuple-element.22.refs_7_) | copy-start | bytes 98308
  25.9 5.9 %collective-permute-start.10 = (f32[32,256]{1,0:T(8,128)S(1)}, f32[32,256]{1,0:T(8,128)S(1)}, u32[]{:S(2)}, u32[]{:S(2)}) collective-permute-start(f32[32,256]{1,0:T(8,128)S(1)} %get-tuple-element.24), channel_id=1, source_target_pairs={{0,2},{1,3},{2,0},{3,1},{4,6},{5,7},{6,4},{7,5},{8,10},{9,11},{10,... | collective-permute-start | bytes 98312 | tf_op jit(solution)/shard_map/ppermute | solution.py:173
  27.4 7.1 %collective-permute-start.11 = (f32[32,256]{1,0:T(8,128)S(1)}, f32[32,256]{1,0:T(8,128)S(1)}, u32[]{:S(2)}, u32[]{:S(2)}) collective-permute-start(f32[32,256]{1,0:T(8,128)S(1)} %get-tuple-element.25), channel_id=1, source_target_pairs={{0,3},{1,2},{2,1},{3,0},{4,7},{5,6},{6,5},{7,4},{8,11},{9,10},{10,... | collective-permute-start | bytes 98312 | tf_op jit(solution)/shard_map/ppermute | solution.py:173
  27.4 7.1 %collective-permute-start.6 = (f32[32,256]{1,0:T(8,128)S(1)}, f32[32,256]{1,0:T(8,128)S(1)}, u32[]{:S(2)}, u32[]{:S(2)}) collective-permute-start(f32[32,256]{1,0:T(8,128)S(1)} %get-tuple-element.19), channel_id=1, source_target_pairs={{0,4},{4,0},{8,12},{12,8},{1,5},{5,1},{9,13},{13,9},{2,6},{6,2},{1... | collective-permute-start | bytes 98312 | tf_op jit(solution)/shard_map/ppermute | solution.py:173
  27.4 7.1 %collective-permute-start.7 = (f32[32,256]{1,0:T(8,128)S(1)}, f32[32,256]{1,0:T(8,128)S(1)}, u32[]{:S(2)}, u32[]{:S(2)}) collective-permute-start(f32[32,256]{1,0:T(8,128)S(1)} %get-tuple-element.20), channel_id=1, source_target_pairs={{0,8},{4,12},{8,0},{12,4},{1,9},{5,13},{9,1},{13,5},{2,10},{6,14},... | collective-permute-start | bytes 98312 | tf_op jit(solution)/shard_map/ppermute | solution.py:173
  28.4 6.1 %collective-permute-start.8 = (f32[32,256]{1,0:T(8,128)S(1)}, f32[32,256]{1,0:T(8,128)S(1)}, u32[]{:S(2)}, u32[]{:S(2)}) collective-permute-start(f32[32,256]{1,0:T(8,128)S(1)} %get-tuple-element.21), channel_id=1, source_target_pairs={{0,12},{4,8},{8,4},{12,0},{1,13},{5,9},{9,5},{13,1},{2,14},{6,10},... | collective-permute-start | bytes 98312 | tf_op jit(solution)/shard_map/ppermute | solution.py:173
  31.8 2.7 %copy-start.6 = (f32[32,256]{1,0:T(8,128)}, f32[32,256]{1,0:T(8,128)S(1)}, u32[]{:S(2)}) copy-start(f32[32,256]{1,0:T(8,128)S(1)} %collective-permute-done.10.refs_9_) | copy-start | bytes 98308
  31.8 2.7 %collective-permute-start.9 = (f32[32,256]{1,0:T(8,128)S(1)}, f32[32,256]{1,0:T(8,128)S(1)}, u32[]{:S(2)}, u32[]{:S(2)}) collective-permute-start(f32[32,256]{1,0:T(8,128)S(1)} %get-tuple-element.23), channel_id=1, source_target_pairs={{0,1},{1,0},{2,3},{3,2},{4,5},{5,4},{6,7},{7,6},{8,9},{9,8},{10,11... | collective-permute-start | bytes 98312 | tf_op jit(solution)/shard_map/ppermute | solution.py:173
  34.5 0.6 %copy-start.7 = (f32[32,256]{1,0:T(8,128)}, f32[32,256]{1,0:T(8,128)S(1)}, u32[]{:S(2)}) copy-start(f32[32,256]{1,0:T(8,128)S(1)} %collective-permute-done.11.refs_10_) | copy-start | bytes 98308
  34.5 0.6 %copy-start.8 = (f32[32,256]{1,0:T(8,128)}, f32[32,256]{1,0:T(8,128)S(1)}, u32[]{:S(2)}) copy-start(f32[32,256]{1,0:T(8,128)S(1)} %collective-permute-done.6.refs_4_) | copy-start | bytes 98308
  34.5 0.6 %copy-start.9 = (f32[32,256]{1,0:T(8,128)}, f32[32,256]{1,0:T(8,128)S(1)}, u32[]{:S(2)}) copy-start(f32[32,256]{1,0:T(8,128)S(1)} %collective-permute-done.7.refs_5_) | copy-start | bytes 98308
  34.6 0.6 %copy-start.10 = (f32[32,256]{1,0:T(8,128)}, f32[32,256]{1,0:T(8,128)S(1)}, u32[]{:S(2)}) copy-start(f32[32,256]{1,0:T(8,128)S(1)} %collective-permute-done.8.refs_6_) | copy-start | bytes 98308
  34.6 0.6 %copy-start.11 = (f32[32,256]{1,0:T(8,128)}, f32[32,256]{1,0:T(8,128)S(1)}, u32[]{:S(2)}) copy-start(f32[32,256]{1,0:T(8,128)S(1)} %collective-permute-done.9.refs_8_) | copy-start | bytes 98308

commit v2 on v1

v2 whole, which is shorter than its diff:
```python
import functools
import math

import jax
import jax.numpy as jnp
import numpy as np
from jax import lax
from jax.experimental import pallas as pl
from jax.experimental.pallas import tpu as pltpu
from jax.sharding import PartitionSpec as P

BLK = 128
GEO = 24
SLAB = 32
FEAT = 128
ROWS = 32
NT = (((1,), (1,)), ((), ()))
TN = (((0,), (0,)), ((), ()))


def selection():
    pick = np.zeros((SLAB, 2 * FEAT + 4 * BLK), np.float32)
    for part in range(3):
        base = part * SLAB
        for split in range(3):
            for axis in range(3):
                pick[9 + 3 * part + axis, base + 3 * split + axis] = 1.0
                pick[3 * part + axis, FEAT + base + 9 + 3 * split + axis] = 1.0
        pick[18 + part, 3 * SLAB + part] = 1.0
        pick[24, FEAT + 18 + part] = 1.0
        for axis in range(3):
            first = 2 * FEAT + axis * BLK
            pick[3 * part + axis, first : first + BLK] = 1.0
        first = 2 * FEAT + 3 * BLK
        pick[21 + part, first : first + BLK] = 1.0
    return pick


def parts(x):
    high = x.astype(jnp.bfloat16).astype(jnp.float32)
    rest = x - high
    middle = rest.astype(jnp.bfloat16).astype(jnp.float32)
    return high, middle, rest - middle


def pack_kernel(*refs, nr, nz, held):
    given = refs[1 : 1 + held]
    target_ref = refs[1 + held]
    sources = refs[2 + held : 2 + held + nz]
    kept = refs[2 + held + nz : 2 + held + nz + 4]
    mask_ref = refs[2 + held + nz + 4]
    place_ref, turn_ref, area_ref, radiosity, adjoint, geo, seen, sems, seen_sem = refs[2 + held + nz + 5 :]
    emissivity_ref = kept[0]
    landing = (place_ref, turn_ref, area_ref, emissivity_ref, radiosity, adjoint) + tuple(kept[1:])
    copies = [pltpu.make_async_copy(a, b, sems.at[i]) for i, (a, b) in enumerate(zip(given, landing))]
    sight = pltpu.make_async_copy(refs[0], seen, seen_sem)
    sight.start()
    for copy in copies:
        copy.start()
    me_r = lax.axis_index("recv")
    me_z = lax.axis_index("emit")
    own = area_ref.shape[1]
    cases = radiosity.shape[0]
    per = own // BLK
    for copy in copies[:3]:
        copy.wait()
    place = place_ref[...]
    turn = turn_ref[...]
    sines = jnp.sin(turn)
    cosines = jnp.cos(turn)
    normal = jnp.concatenate(
        [sines[0:1] * cosines[1:2], sines[0:1] * sines[1:2], cosines[0:1]], axis=0
    )
    product = normal * place
    offset = -(product[0:1] + product[1:2] + product[2:3])
    for number, (a, b, c, d) in enumerate(
        zip(parts(place), parts(normal), parts(offset), parts(area_ref[...]))
    ):
        geo[0, 3 * number : 3 * number + 3, :] = a
        geo[0, 9 + 3 * number : 12 + 3 * number, :] = b
        geo[0, 18 + number : 19 + number, :] = c
        geo[0, 21 + number : 22 + number, :] = d
    sight.wait()
    for k in range(nz):
        for s in range(nr):
            for ib in range(per):
                row = GEO + s * per + ib
                col = ((me_z ^ k) * nr + (me_r ^ s)) * per + ib
                spot = (k * nr + s) * per + ib
                for jb in range(per):
                    lanes = slice(jb * BLK, (jb + 1) * BLK)
                    sees = seen[me_r * per + jb, col].astype(jnp.float32)
                    geo[k, row : row + 1, lanes] = jnp.full((1, BLK), sees, jnp.float32)
                    other = seen[(me_r ^ s) * per + ib, ((me_z ^ k) * nr + me_r) * per + jb]
                    sees = other.astype(jnp.float32) * (1.0 / math.pi)
                    mask_ref[spot : spot + 1, lanes] = jnp.full((1, BLK), sees, jnp.float32)
    shared = geo[0, 0:GEO, :]
    one = jnp.ones((SLAB - GEO, own), jnp.float32)
    target_ref[...] = jnp.concatenate([shared, one], axis=0).astype(jnp.bfloat16)
    for copy in copies[3:6]:
        copy.wait()
    value = radiosity[...].astype(jnp.bfloat16)
    weighted = ((1.0 - emissivity_ref[...]) * adjoint[...]).astype(jnp.bfloat16)
    for k in range(nz):
        sources[k][0:cases, :] = value
        sources[k][cases : 2 * cases, :] = weighted
        sources[k][2 * cases :, :] = jnp.concatenate([shared, geo[k, GEO:, :]], axis=0).astype(jnp.bfloat16)
    for copy in copies[6:]:
        copy.wait()


def source_kernel(ids, weights, out_ref):
    own = out_ref.shape[1]
    first = (lax.axis_index("emit") * lax.axis_size("recv") + lax.axis_index("recv")) * own
    half = out_ref.shape[0] // 2
    hit = lax.broadcasted_iota(jnp.int32, (own, ids.shape[1]), 0) == ids[...] - first
    chosen = jnp.where(hit, 1.0, 0.0).astype(jnp.bfloat16)
    pieces = jnp.concatenate(parts(weights[...]), axis=0).astype(jnp.bfloat16)
    split = lax.dot_general(pieces, chosen, NT, preferred_element_type=jnp.float32)
    out_ref[0:half, :] = jnp.zeros((half, own), jnp.float32)
    out_ref[half:, :] = split[0:half] + split[half : 2 * half] + split[2 * half :]


def one_row(ref, row, lanes):
    if isinstance(row, int):
        return ref[row : row + 1, lanes]
    around = ref[pl.ds(pl.multiple_of(row // 8 * 8, 8), 8), lanes]
    pick = lax.broadcasted_iota(jnp.int32, around.shape, 0) == row % 8
    return jnp.sum(jnp.where(pick, around, 0.0), axis=0, keepdims=True)


def prepare_kernel(*refs, count):
    pick = refs[0]
    targets = refs[1 : 1 + count]
    left, wide = refs[1 + count :]
    own = targets[0].shape[1]
    pair = left.shape[1] // own
    for g in range(count // pair):
        both = jnp.concatenate([targets[g * pair + t][...] for t in range(pair)], axis=1)
        feature = lax.dot_general(both, pick[...], TN, preferred_element_type=jnp.float32)
        left[g] = feature[:, : 2 * FEAT].astype(jnp.bfloat16)
        wide[g] = feature[:, 2 * FEAT :]


def sum_kernel(*refs, first, count, blocks, numbers):
    ns = len(numbers)
    mask, left, wide = refs[0:3]
    sources = refs[3 : 3 + ns]
    begin = refs[3 + ns : 3 + ns + count]
    out = refs[3 + ns + count : 3 + ns + 2 * count]
    facing, back, fwd_tile, adj_tile, total, stack, geo, scale_q = refs[3 + ns + 2 * count :]
    own = out[0].shape[1]
    cases = out[0].shape[0] // 2
    per = own // BLK
    span = left.shape[1]
    pair = span // own
    groups = count // pair
    for t in range(count):
        total[t] = begin[t][...]

    def match(k, g, slot, source):
        slab = source[2 * cases : 2 * cases + SLAB, :]
        right = jnp.concatenate([slab, slab, slab, jnp.ones_like(slab)], axis=0)
        facing[slot] = jnp.dot(left[g, :, :FEAT], right, preferred_element_type=jnp.float32)
        back[slot] = jnp.dot(left[g, :, FEAT:], right, preferred_element_type=jnp.float32)

    def measure(k, slot, source):
        exact = source[2 * cases :, :].astype(jnp.float32)
        geo[slot, 0:3, :] = exact[0:3] + exact[3:6] + exact[6:9]
        area_q = exact[21:22] + exact[22:23] + exact[23:24]
        geo[slot, 3:4, :] = area_q
        scale_q[slot] = exact[GEO:] * (area_q * (1.0 / math.pi))

    def build(k, g, slot, side):
        for jb in range(per):
            lanes = slice(jb * BLK, (jb + 1) * BLK)
            xq = geo[side, 0:1, lanes]
            yq = geo[side, 1:2, lanes]
            zq = geo[side, 2:3, lanes]
            aq = geo[side, 3:4, lanes]
            for block in range(pair * per):
                row = (first + g * pair) * per + block
                scale = one_row(scale_q.at[side], row, lanes)
                sees = one_row(mask, k * blocks + row, lanes)
                for start in range(block * BLK, (block + 1) * BLK, ROWS):
                    here = slice(start, start + ROWS)
                    dx = wide[g, here, 0:BLK] - xq
                    dy = wide[g, here, BLK : 2 * BLK] - yq
                    dz = wide[g, here, 2 * BLK : 3 * BLK] - zq
                    area = wide[g, here, 3 * BLK :]
                    square = dx * dx + dy * dy + dz * dz
                    product = jnp.maximum(facing[slot, here, lanes], 0.0) * jnp.maximum(back[slot, here, lanes], 0.0)
                    near = square + aq
                    far = square + area
                    fwd_tile[slot, here, lanes] = (product * scale / (near * near)).astype(jnp.bfloat16)
                    adj_tile[slot, here, lanes] = (product * sees * area / (far * far)).astype(jnp.bfloat16)

    def collect(g, slot, source):
        incoming = lax.dot_general(source[0:cases, :], fwd_tile[slot], NT, preferred_element_type=jnp.float32)
        returned = lax.dot_general(
            source[cases : 2 * cases, :], adj_tile[slot], NT, preferred_element_type=jnp.float32
        )
        for t in range(pair):
            s = g * pair + t
            total[s, 0:cases, :] += incoming[:, t * own : (t + 1) * own]
            total[s, cases:, :] += returned[:, t * own : (t + 1) * own]

    if ns * groups <= 8:
        steps = [(i, g) for i in range(ns) for g in range(groups)]
        for number, (i, g) in enumerate(steps):
            if number == 0:
                measure(numbers[i], i % 2, sources[i])
                match(numbers[i], g, 0, sources[i])
            if number + 1 < len(steps):
                j, h = steps[number + 1]
                if j != i:
                    measure(numbers[j], j % 2, sources[j])
                match(numbers[j], h, (number + 1) % 2, sources[j])
            build(numbers[i], g, number % 2, i % 2)
            collect(g, number % 2, sources[i])
    else:
        for i in range(ns):
            stack[i] = sources[i][...]

        def step(number, _):
            i, g = number // groups, number % groups
            source = stack.at[i]
            measure(numbers[0] + i, 0, source)
            match(numbers[0] + i, g, 0, source)
            build(numbers[0] + i, g, 0, 0)
            collect(g, 0, source)
            return 0

        lax.fori_loop(0, ns * groups, step, 0)
    for t in range(count):
        out[t][...] = total[t]


def finish_kernel(*refs, nr):
    emissivity, emission = refs[0:2]
    pieces = refs[2 : 2 + nr]
    radiosity_out, adjoint_out, gradient = refs[2 + nr :]
    cases = emission.shape[0]
    total = pieces[0][...]
    for piece in pieces[1:]:
        total = total + piece[...]
    incoming = total[0:cases]
    returned = total[cases:]
    mine = emissivity[...]
    power = emission[...]
    radiosity_out[...] = mine * power + (1.0 - mine) * incoming
    adjoint_out[...] = returned
    gradient[...] = jnp.sum(returned * (power - incoming), axis=0, keepdims=True)


def busy(micros):
    return pl.CostEstimate(flops=int(micros * 1.1e9), bytes_accessed=0, transcendentals=0)


def swap(x, axis, other):
    if other == 0:
        return x
    return lax.ppermute(x, axis, [(i, i ^ other) for i in range(lax.axis_size(axis))])


def local(
    positions,
    angles,
    areas,
    emissivity,
    emission,
    radiosity_in,
    adjoint_in,
    visibility,
    inlet_patches,
    inlet_weights,
):
    nz = lax.axis_size("emit")
    nr = lax.axis_size("recv")
    own = areas.shape[0]
    cases = emission.shape[0]
    per = own // BLK
    ids = inlet_patches.reshape(1, -1)
    vmem = pl.BlockSpec(memory_space=pltpu.VMEM)
    hbm = pl.BlockSpec(memory_space=pltpu.HBM)
    small = pltpu.CompilerParams(vmem_limit_bytes=4 << 20)
    f32 = jnp.float32
    blocks = nr * per
    rows = 2 * cases + GEO + blocks
    given = (
        positions,
        angles,
        areas.reshape(1, own),
        emissivity.reshape(1, own),
        radiosity_in,
        adjoint_in,
        emission,
        ids,
        inlet_weights,
    )
    given = tuple(pltpu.with_memory_space_constraint(x, pltpu.HBM) for x in given)
    seen = pltpu.with_memory_space_constraint(visibility, pltpu.HBM)
    packed = pl.pallas_call(
        functools.partial(pack_kernel, nr=nr, nz=nz, held=len(given)),
        out_shape=(jax.ShapeDtypeStruct((SLAB, own), jnp.bfloat16),)
        + (jax.ShapeDtypeStruct((rows, own), jnp.bfloat16),) * nz
        + tuple(jax.ShapeDtypeStruct(given[i].shape, given[i].dtype) for i in (3, 6, 7, 8))
        + (jax.ShapeDtypeStruct((nz * blocks, own), f32),),
        in_specs=[hbm] * (1 + len(given)),
        out_specs=(vmem,) * (1 + nz + 5),
        scratch_shapes=[
            pltpu.VMEM((3, own), f32),
            pltpu.VMEM((2, own), f32),
            pltpu.VMEM((1, own), f32),
            pltpu.VMEM((cases, own), f32),
            pltpu.VMEM((cases, own), f32),
            pltpu.VMEM((nz, GEO + blocks, own), f32),
            pltpu.SMEM(visibility.shape, jnp.int32),
            pltpu.SemaphoreType.DMA((len(given),)),
            pltpu.SemaphoreType.DMA,
        ],
        compiler_params=small,
    )(seen, *given)
    mine, power, ids, weights, mask = packed[1 + nz :]
    targets = []
    for s in range(nr):
        targets.append(swap(targets[s - 1], "recv", 1) if s % 2 else swap(packed[0], "recv", s))
    sources = [swap(packed[1 + k], "emit", k) for k in range(nz)]
    source = pl.pallas_call(
        source_kernel,
        out_shape=jax.ShapeDtypeStruct((2 * cases, own), f32),
        in_specs=[vmem] * 2,
        out_specs=vmem,
        compiler_params=small,
        cost_estimate=busy(0.5),
    )(ids, weights)
    pick = jnp.asarray(selection(), jnp.bfloat16)
    sums = jax.ShapeDtypeStruct((2 * cases, own), f32)
    zero = jnp.zeros((2 * cases, own), f32)

    def prepare(chosen):
        count = len(chosen)
        pair = min(count, 2)
        return pl.pallas_call(
            functools.partial(prepare_kernel, count=count),
            out_shape=(
                jax.ShapeDtypeStruct((count // pair, pair * own, 2 * FEAT), jnp.bfloat16),
                jax.ShapeDtypeStruct((count // pair, pair * own, 4 * BLK), f32),
            ),
            in_specs=[vmem] * (1 + count),
            out_specs=(vmem, vmem),
            compiler_params=small,
            cost_estimate=busy(0.2 * count),
        )(pick, *chosen)

    def add(first, shape, numbers, begin):
        count = len(begin)
        pair = min(count, 2)
        many = len(numbers) * (count // pair) > 8
        return list(
            pl.pallas_call(
                functools.partial(sum_kernel, first=first, count=count, blocks=blocks, numbers=numbers),
                out_shape=(sums,) * count,
                in_specs=[vmem] * (3 + len(numbers) + count),
                out_specs=(vmem,) * count,
                scratch_shapes=[
                    pltpu.VMEM((2, pair * own, own), f32),
                    pltpu.VMEM((2, pair * own, own), f32),
                    pltpu.VMEM((2, pair * own, own), jnp.bfloat16),
                    pltpu.VMEM((2, pair * own, own), jnp.bfloat16),
                    pltpu.VMEM((count, 2 * cases, own), f32),
                    pltpu.VMEM((len(numbers) if many else 1, rows, own), jnp.bfloat16),
                    pltpu.VMEM((2, 8, own), f32),
                    pltpu.VMEM((2, blocks, own), f32),
                ],
                compiler_params=pltpu.CompilerParams(vmem_limit_bytes=12 << 20),
                cost_estimate=busy(0.3 * count * len(numbers)),
            )(mask, *shape, *[sources[k] for k in numbers], *begin)
        )

    own_shape = prepare(targets[:1])
    core_shape = prepare(targets[1:2])
    far_shape = prepare(targets[2:])
    rest = tuple(range(1, nz))
    own_sums = add(0, own_shape, (0,), [source])
    core_sums = add(1, core_shape, (0,), [zero])
    far_sums = add(2, far_shape, (0,), [zero] * (nr - 2))
    core_sums = add(1, core_shape, rest, core_sums)
    far_sums, core_sums = lax.optimization_barrier((far_sums, core_sums))
    far_sums = add(2, far_shape, rest, far_sums)
    far_sums, own_sums = lax.optimization_barrier((far_sums, own_sums))
    own_sums = add(0, own_shape, rest, own_sums)
    pieces = [swap(x, "recv", s) for s, x in enumerate(own_sums + core_sums + far_sums)]
    whole = jax.ShapeDtypeStruct((cases, own), f32)
    radiosity_out, adjoint_out, gradient = pl.pallas_call(
        functools.partial(finish_kernel, nr=nr),
        out_shape=(whole, whole, jax.ShapeDtypeStruct((1, own), f32)),
        in_specs=[vmem] * (2 + nr),
        out_specs=(vmem, vmem, vmem),
        compiler_params=small,
    )(mine, power, *pieces)
    return radiosity_out, adjoint_out, gradient.reshape(own)


def solution(mesh):
    patch = ("groups", "emit", "recv")
    placed = (
        P(None, patch),
        P(None, patch),
        P(patch),
        P(patch),
        P(None, patch),
        P(None, patch),
        P(None, patch),
        P(("groups", "emit"), None),
        P("groups"),
        P(None, "groups"),
    )
    return jax.shard_map(
        local,
        mesh=mesh,
        in_specs=placed,
        out_specs=(P(None, patch), P(None, patch), P(patch)),
        check_vma=False,
    )
```

time: 37.2 us -> 23.5 us (0.63)
  Pallas kernels: 13.3 us -> 8.62 us
  starting transfers between devices: 13.4 us -> 9.71 us
  local copies, waits for them, and re-layouts: 3.36 us -> 0.01 us
  waiting for transfers between devices: 5.92 us -> 4.22 us
    pallas_call x4 -> x12, Pallas kernels: 13.3 us -> 8.62 us  [the longest x6 5.38 us: add(): pl.pallas_call(functools.partial(sum_kernel, first=first, count=count, bl...]
    ppermute x12 -> x9, starting transfers between devices: 13.4 us -> 9.71 us  [swap(): lax.ppermute(x, axis, [(i, i ^ other) for i in range(lax.axis_size(axis))])]
    unnamed x24 -> x2, local copies, waits for them, and re-layouts: 3.36 us -> 0.01 us
    ppermute x12 -> x9, waiting for transfers between devices: 5.92 us -> 4.22 us  [swap(): lax.ppermute(x, axis, [(i, i ^ other) for i in range(lax.axis_size(axis))])]
  transfers between devices with their start and end apart: 12 -> 9, of which waited for: 2 -> 3; matrix products, arithmetic and copies ran while one was open for 0% -> 0% of each run, Pallas kernels for 7% -> 18%
where the time goes in v2:
time: 23.5 us; the launch traced here: 23.3 us
  starting transfers between devices  9.71 us (41%)
  Pallas kernels  8.62 us (37%)
  waiting for transfers between devices  4.22 us (18%)
  between operations  0.72 us (3%)
    ppermute x9, starting transfers between devices, swap(): lax.ppermute(x, axis, [(i, i ^ other) for i in range(lax.axis_size(axis))])  9.71 us
    pallas_call x6, Pallas kernels, add(): pl.pallas_call(functools.partial(sum_kernel, first=first, count=count, bl...  5.38 us
    ppermute x9, waiting for transfers between devices, swap(): lax.ppermute(x, axis, [(i, i ^ other) for i in range(lax.axis_size(axis))])  4.22 us
    pallas_call x1, Pallas kernels, local(): pl.pallas_call(functools.partial(pack_kernel, nr=nr, nz=nz, held=len(give...  1.2 us
    pallas_call x3, Pallas kernels, prepare(): pl.pallas_call(functools.partial(prepare_kernel, count=count), out_shape=...  0.94 us
    pallas_call x1, Pallas kernels, local(): pl.pallas_call(functools.partial(finish_kernel, nr=nr), out_shape=(whole,...  0.64 us
  transfers between devices with their start and end apart: 9, of which 3 were waited for; matrix products, arithmetic and copies ran while one was open for 0% of the time, Pallas kernels for 18%

profile of v2, /device:TPU:0, one launch (start us, length us, event | category | flops | bytes accessed | tf_op | source)
XLA Modules:
  0.0 23.3 jit_solution(12351106417700502404)
XLA Ops:
  0.6 0.0 copy-start
  0.6 1.2 %shard_map.130 = (bf16[32,256]{1,0:T(8,128)(2,1)S(1)}, bf16[96,256]{1,0:T(8,128)(2,1)S(1)}, bf16[96,256]{1,0:T(8,128)(2,1)S(1)}, bf16[96,256]{1,0:T(8,128)(2,1)S...) custom-call(s32[8,32]{1,0:T(8,128)} %refs_0_.4, ...), custom_call_target="tpu_custom_call" | custom-call | tf_op jit(solution)/shard_map/pallas_call | solution.py:303
  1.9 0.5 %collective-permute-start.5 = (bf16[32,256]{1,0:T(8,128)(2,1)S(1)}, bf16[32,256]{1,0:T(8,128)(2,1)S(1)}, u32[]{:S(2)}, u32[]{:S(2)}) collective-permute-start(bf16[32,256]{1,0:T(8,128)(2,1)S(1)} %get-tuple-element.35.refs_1_), channel_id=1, source_target_pairs={{0,1},{1,0},{2,3},{3,2},{4,5},{5,4},{6,7},{7,6},{8,9},{9,8},{10,11... | collective-permute-start | bytes 49160 | tf_op jit(solution)/shard_map/ppermute | solution.py:263
  2.4 2.6 %collective-permute-start.3 = (bf16[32,256]{1,0:T(8,128)(2,1)S(1)}, bf16[32,256]{1,0:T(8,128)(2,1)S(1)}, u32[]{:S(2)}, u32[]{:S(2)}) collective-permute-start(bf16[32,256]{1,0:T(8,128)(2,1)S(1)} %get-tuple-element.35.refs_1_), channel_id=1, source_target_pairs={{0,2},{1,3},{2,0},{3,1},{4,6},{5,7},{6,4},{7,5},{8,10},{9,11},{10,... | collective-permute-start | bytes 49160 | tf_op jit(solution)/shard_map/ppermute | solution.py:263
  4.9 1.6 %collective-permute-start = (bf16[96,256]{1,0:T(8,128)(2,1)S(1)}, bf16[96,256]{1,0:T(8,128)(2,1)S(1)}, u32[]{:S(2)}, u32[]{:S(2)}) collective-permute-start(bf16[96,256]{1,0:T(8,128)(2,1)S(1)} %get-tuple-element.38), channel_id=1, source_target_pairs={{0,4},{4,0},{8,12},{12,8},{1,5},{5,1},{9,13},{13,9},{2,6},{6,2},{1... | collective-permute-start | bytes 147464 | tf_op jit(solution)/shard_map/ppermute | solution.py:263
  6.5 2.6 %collective-permute-start.1 = (bf16[96,256]{1,0:T(8,128)(2,1)S(1)}, bf16[96,256]{1,0:T(8,128)(2,1)S(1)}, u32[]{:S(2)}, u32[]{:S(2)}) collective-permute-start(bf16[96,256]{1,0:T(8,128)(2,1)S(1)} %get-tuple-element.39), channel_id=1, source_target_pairs={{0,8},{4,12},{8,0},{12,4},{1,9},{5,13},{9,1},{13,5},{2,10},{6,14},... | collective-permute-start | bytes 147464 | tf_op jit(solution)/shard_map/ppermute | solution.py:263
  9.1 0.2 collective-permute-start.2
  9.3 0.0 copy-done
  9.3 0.3 %shard_map.131 = (bf16[1,256,256]{2,1,0:T(8,128)(2,1)S(1)}, f32[1,256,512]{2,1,0:T(8,128)S(1)}) custom-call(bf16[32,768]{1,0:T(8,128)(2,1)S(1)} %copy-done, bf16[32,256]{1,0:T(8,128)(2,1)S(1)} %get-tuple-element.35.refs_1_), custom_call_target="tpu_custom_call" | custom-call | flops 220000000 | tf_op jit(solution)/shard_map/pallas_call | solution.py:344
  9.6 0.5 %shard_map.138.refs_4_ = f32[64,256]{1,0:T(8,128)S(1)} custom-call(s32[1,2048]{1,0:T(1,128)S(1)} %get-tuple-element.52.ids, f32[32,2048]{1,0:T(8,128)S(1)} %get-tuple-element.53.weights), custom_call_target="tpu_custom_call" | custom-call | flops 550000000 | tf_op jit(solution)/shard_map/pallas_call | solution.py:329
  10.1 0.5 %shard_map.139.refs_6_ = f32[64,256]{1,0:T(8,128)S(1)} custom-call(f32[32,256]{1,0:T(8,128)S(1)} %get-tuple-element.34.refs_0_, bf16[1,256,256]{2,1,0:T(8,128)(2,1)S(1)} %get-tuple-element.36.refs_1_, f32[1,256,512]{2,1,0:T(8,128)S(1)} %get-tuple-element.37.refs_2_, bf16[96,256]{1,0:T(8,128)(2,1)S(1)} %get-tuple-element.43.refs_3_, ...), custom_call_target="tpu_custom_call" | custom-call | flops 330000000 | tf_op jit(solution)/shard_map/pallas_call | solution.py:361
  10.5 0.0 collective-permute-done.5.refs_1_
  10.6 0.3 %shard_map.134 = (bf16[1,256,256]{2,1,0:T(8,128)(2,1)S(1)}, f32[1,256,512]{2,1,0:T(8,128)S(1)}) custom-call(bf16[32,768]{1,0:T(8,128)(2,1)S(1)} %copy-done, bf16[32,256]{1,0:T(8,128)(2,1)S(1)} %collective-permute-done.5.refs_1_), custom_call_target="tpu_custom_call" | custom-call | flops 220000000 | tf_op jit(solution)/shard_map/pallas_call | solution.py:344
  10.8 0.0 collective-permute-done.3.refs_1_
  10.9 0.1 collective-permute-start.4
  10.9 0.5 %shard_map.135.refs_6_ = f32[64,256]{1,0:T(8,128)S(1)} custom-call(f32[32,256]{1,0:T(8,128)S(1)} %get-tuple-element.34.refs_0_, bf16[1,256,256]{2,1,0:T(8,128)(2,1)S(1)} %get-tuple-element.46.refs_1_, f32[1,256,512]{2,1,0:T(8,128)S(1)} %get-tuple-element.47.refs_2_, bf16[96,256]{1,0:T(8,128)(2,1)S(1)} %get-tuple-element.43.refs_3_, ...), custom_call_target="tpu_custom_call" | custom-call | flops 330000000 | tf_op jit(solution)/shard_map/pallas_call | solution.py:361
  11.4 0.7 %collective-permute-done.4.refs_2_ = bf16[32,256]{1,0:T(8,128)(2,1)S(1)} collective-permute-done((bf16[32,256]{1,0:T(8,128)(2,1)S(1)}, bf16[32,256]{1,0:T(8,128)(2,1)S(1)}, u32[]{:S(2)}, u32[]{:S(2)}) %collective-permute-start.4) | collective-permute-done | bytes 16416 | tf_op jit(solution)/shard_map/ppermute | solution.py:263
  12.1 0.4 %shard_map.132 = (bf16[1,512,256]{2,1,0:T(8,128)(2,1)S(1)}, f32[1,512,512]{2,1,0:T(8,128)S(1)}) custom-call(bf16[32,768]{1,0:T(8,128)(2,1)S(1)} %copy-done, bf16[32,256]{1,0:T(8,128)(2,1)S(1)} %collective-permute-done.3.refs_1_, bf16[32,256]{1,0:T(8,128)(2,1)S(1)} %collective-permute-done.4.refs_2_), custom_call_target="tpu_custom_call" | custom-call | flops 440000000 | tf_op jit(solution)/shard_map/pallas_call | solution.py:344
  12.5 0.8 %shard_map.133 = (f32[64,256]{1,0:T(8,128)S(1)}, f32[64,256]{1,0:T(8,128)S(1)}) custom-call(f32[32,256]{1,0:T(8,128)S(1)} %get-tuple-element.34.refs_0_, bf16[1,512,256]{2,1,0:T(8,128)(2,1)S(1)} %get-tuple-element.41.refs_1_, f32[1,512,512]{2,1,0:T(8,128)S(1)} %get-tuple-element.42.refs_2_, bf16[96,256]{1,0:T(8,128)(2,1)S(1)} %get-tuple-element.43.refs_3_, ...), custom_call_target="tpu_custom_call" | custom-call | flops 660000000 | tf_op jit(solution)/shard_map/pallas_call | solution.py:361
  13.3 0.0 collective-permute-done.refs_3_
  13.3 0.0 collective-permute-done.1.refs_4_
  13.3 1.7 %collective-permute-done.2.refs_5_ = bf16[96,256]{1,0:T(8,128)(2,1)S(1)} collective-permute-done((bf16[96,256]{1,0:T(8,128)(2,1)S(1)}, bf16[96,256]{1,0:T(8,128)(2,1)S(1)}, u32[]{:S(2)}, u32[]{:S(2)}) %collective-permute-start.2) | collective-permute-done | bytes 49184 | tf_op jit(solution)/shard_map/ppermute | solution.py:263
  15.0 1.0 %shard_map.136 = f32[64,256]{1,0:T(8,128)S(1)} custom-call(f32[32,256]{1,0:T(8,128)S(1)} %get-tuple-element.34.refs_0_, bf16[1,256,256]{2,1,0:T(8,128)(2,1)S(1)} %get-tuple-element.46.refs_1_, f32[1,256,512]{2,1,0:T(8,128)S(1)} %get-tuple-element.47.refs_2_, bf16[96,256]{1,0:T(8,128)(2,1)S(1)} %collective-permute-done.refs_3_, ...), custom_call_target="tpu_custom_call" | custom-call | flops 990000000 | tf_op jit(solution)/shard_map/pallas_call | solution.py:361
  16.0 1.7 %shard_map.137 = (f32[64,256]{1,0:T(8,128)S(1)}, f32[64,256]{1,0:T(8,128)S(1)}) custom-call(f32[32,256]{1,0:T(8,128)S(1)} %get-tuple-element.34.refs_0_, bf16[1,512,256]{2,1,0:T(8,128)(2,1)S(1)} %get-tuple-element.41.refs_1_, f32[1,512,512]{2,1,0:T(8,128)S(1)} %get-tuple-element.42.refs_2_, bf16[96,256]{1,0:T(8,128)(2,1)S(1)} %collective-permute-done.refs_3_, ...), custom_call_target="tpu_custom_call" | custom-call | flops 1980000000 | tf_op jit(solution)/shard_map/pallas_call | solution.py:361
  17.7 0.6 %collective-permute-start.7 = (f32[64,256]{1,0:T(8,128)S(1)}, f32[64,256]{1,0:T(8,128)S(1)}, u32[]{:S(2)}, u32[]{:S(2)}) collective-permute-start(f32[64,256]{1,0:T(8,128)S(1)} %get-tuple-element.56), channel_id=1, source_target_pairs={{0,2},{1,3},{2,0},{3,1},{4,6},{5,7},{6,4},{7,5},{8,10},{9,11},{10,... | collective-permute-start | bytes 196616 | tf_op jit(solution)/shard_map/ppermute | solution.py:263
  18.2 0.0 collective-permute-start.8
  18.2 1.6 %collective-permute-start.6 = (f32[64,256]{1,0:T(8,128)S(1)}, f32[64,256]{1,0:T(8,128)S(1)}, u32[]{:S(2)}, u32[]{:S(2)}) collective-permute-start(f32[64,256]{1,0:T(8,128)S(1)} %shard_map.136), channel_id=1, source_target_pairs={{0,1},{1,0},{2,3},{3,2},{4,5},{5,4},{6,7},{7,6},{8,9},{9,8},{10,11... | collective-permute-start | bytes 196616 | tf_op jit(solution)/shard_map/ppermute | solution.py:263
  19.8 1.0 %shard_map.140.refs_2_ = f32[64,256]{1,0:T(8,128)S(1)} custom-call(f32[32,256]{1,0:T(8,128)S(1)} %get-tuple-element.34.refs_0_, bf16[1,256,256]{2,1,0:T(8,128)(2,1)S(1)} %get-tuple-element.36.refs_1_, f32[1,256,512]{2,1,0:T(8,128)S(1)} %get-tuple-element.37.refs_2_, bf16[96,256]{1,0:T(8,128)(2,1)S(1)} %collective-permute-done.refs_3_, ...), custom_call_target="tpu_custom_call" | custom-call | flops 990000000 | tf_op jit(solution)/shard_map/pallas_call | solution.py:361
  20.8 1.8 %collective-permute-done.7.refs_4_ = f32[64,256]{1,0:T(8,128)S(1)} collective-permute-done((f32[64,256]{1,0:T(8,128)S(1)}, f32[64,256]{1,0:T(8,128)S(1)}, u32[]{:S(2)}, u32[]{:S(2)}) %collective-permute-start.7) | collective-permute-done | bytes 65568 | tf_op jit(solution)/shard_map/ppermute | solution.py:263
  22.6 0.0 collective-permute-done.8.refs_5_
  22.6 0.0 collective-permute-done.6.refs_3_
  22.6 0.6 %shard_map.141 = (f32[32,256]{1,0:T(8,128)}, f32[32,256]{1,0:T(8,128)}, f32[1,256]{1,0:T(1,128)}) custom-call(f32[1,256]{1,0:T(1,128)S(1)} %get-tuple-element.32.refs_0_, f32[32,256]{1,0:T(8,128)S(1)} %get-tuple-element.33.refs_1_, f32[64,256]{1,0:T(8,128)S(1)} %shard_map.140.refs_2_, f32[64,256]{1,0:T(8,128)S(1)} %collective-permute-done.6.refs_3_, ...), custom_call_target="tpu_custom_call" | custom-call | tf_op jit(solution)/shard_map/pallas_call | solution.py:395
  (1 shorter events, 0.0 us)
Async XLA Ops:
  0.6 8.7 %copy-start = (bf16[32,768]{1,0:T(8,128)(2,1)S(1)}, bf16[32,768]{1,0:T(8,128)(2,1)}, u32[]{:S(2)}) copy-start(bf16[32,768]{1,0:T(8,128)(2,1)} %constant.4.clone.refs_0_) | copy-start | bytes 147460
  1.9 8.7 %collective-permute-start.5 = (bf16[32,256]{1,0:T(8,128)(2,1)S(1)}, bf16[32,256]{1,0:T(8,128)(2,1)S(1)}, u32[]{:S(2)}, u32[]{:S(2)}) collective-permute-start(bf16[32,256]{1,0:T(8,128)(2,1)S(1)} %get-tuple-element.35.refs_1_), channel_id=1, source_target_pairs={{0,1},{1,0},{2,3},{3,2},{4,5},{5,4},{6,7},{7,6},{8,9},{9,8},{10,11... | collective-permute-start | bytes 49160 | tf_op jit(solution)/shard_map/ppermute | solution.py:263
  2.4 8.5 %collective-permute-start.3 = (bf16[32,256]{1,0:T(8,128)(2,1)S(1)}, bf16[32,256]{1,0:T(8,128)(2,1)S(1)}, u32[]{:S(2)}, u32[]{:S(2)}) collective-permute-start(bf16[32,256]{1,0:T(8,128)(2,1)S(1)} %get-tuple-element.35.refs_1_), channel_id=1, source_target_pairs={{0,2},{1,3},{2,0},{3,1},{4,6},{5,7},{6,4},{7,5},{8,10},{9,11},{10,... | collective-permute-start | bytes 49160 | tf_op jit(solution)/shard_map/ppermute | solution.py:263
  4.9 8.3 %collective-permute-start = (bf16[96,256]{1,0:T(8,128)(2,1)S(1)}, bf16[96,256]{1,0:T(8,128)(2,1)S(1)}, u32[]{:S(2)}, u32[]{:S(2)}) collective-permute-start(bf16[96,256]{1,0:T(8,128)(2,1)S(1)} %get-tuple-element.38), channel_id=1, source_target_pairs={{0,4},{4,0},{8,12},{12,8},{1,5},{5,1},{9,13},{13,9},{2,6},{6,2},{1... | collective-permute-start | bytes 147464 | tf_op jit(solution)/shard_map/ppermute | solution.py:263
  6.5 6.8 %collective-permute-start.1 = (bf16[96,256]{1,0:T(8,128)(2,1)S(1)}, bf16[96,256]{1,0:T(8,128)(2,1)S(1)}, u32[]{:S(2)}, u32[]{:S(2)}) collective-permute-start(bf16[96,256]{1,0:T(8,128)(2,1)S(1)} %get-tuple-element.39), channel_id=1, source_target_pairs={{0,8},{4,12},{8,0},{12,4},{1,9},{5,13},{9,1},{13,5},{2,10},{6,14},... | collective-permute-start | bytes 147464 | tf_op jit(solution)/shard_map/ppermute | solution.py:263
  9.1 5.9 %collective-permute-start.2 = (bf16[96,256]{1,0:T(8,128)(2,1)S(1)}, bf16[96,256]{1,0:T(8,128)(2,1)S(1)}, u32[]{:S(2)}, u32[]{:S(2)}) collective-permute-start(bf16[96,256]{1,0:T(8,128)(2,1)S(1)} %get-tuple-element.40), channel_id=1, source_target_pairs={{0,12},{4,8},{8,4},{12,0},{1,13},{5,9},{9,5},{13,1},{2,14},{6,10},... | collective-permute-start | bytes 147464 | tf_op jit(solution)/shard_map/ppermute | solution.py:263
  10.9 1.2 %collective-permute-start.4 = (bf16[32,256]{1,0:T(8,128)(2,1)S(1)}, bf16[32,256]{1,0:T(8,128)(2,1)S(1)}, u32[]{:S(2)}, u32[]{:S(2)}) collective-permute-start(bf16[32,256]{1,0:T(8,128)(2,1)S(1)} %collective-permute-done.3.refs_1_), channel_id=1, source_target_pairs={{0,1},{1,0},{2,3},{3,2},{4,5},{5,4},{6,7},{7,6},{8,9},{9,8},{10,11... | collective-permute-start | bytes 49160 | tf_op jit(solution)/shard_map/ppermute | solution.py:263
  17.7 5.0 %collective-permute-start.7 = (f32[64,256]{1,0:T(8,128)S(1)}, f32[64,256]{1,0:T(8,128)S(1)}, u32[]{:S(2)}, u32[]{:S(2)}) collective-permute-start(f32[64,256]{1,0:T(8,128)S(1)} %get-tuple-element.56), channel_id=1, source_target_pairs={{0,2},{1,3},{2,0},{3,1},{4,6},{5,7},{6,4},{7,5},{8,10},{9,11},{10,... | collective-permute-start | bytes 196616 | tf_op jit(solution)/shard_map/ppermute | solution.py:263
  18.2 4.4 %collective-permute-start.8 = (f32[64,256]{1,0:T(8,128)S(1)}, f32[64,256]{1,0:T(8,128)S(1)}, u32[]{:S(2)}, u32[]{:S(2)}) collective-permute-start(f32[64,256]{1,0:T(8,128)S(1)} %get-tuple-element.57), channel_id=1, source_target_pairs={{0,3},{1,2},{2,1},{3,0},{4,7},{5,6},{6,5},{7,4},{8,11},{9,10},{10,... | collective-permute-start | bytes 196616 | tf_op jit(solution)/shard_map/ppermute | solution.py:263
  18.2 4.4 %collective-permute-start.6 = (f32[64,256]{1,0:T(8,128)S(1)}, f32[64,256]{1,0:T(8,128)S(1)}, u32[]{:S(2)}, u32[]{:S(2)}) collective-permute-start(f32[64,256]{1,0:T(8,128)S(1)} %shard_map.136), channel_id=1, source_target_pairs={{0,1},{1,0},{2,3},{3,2},{4,5},{5,4},{6,7},{7,6},{8,9},{9,8},{10,11... | collective-permute-start | bytes 196616 | tf_op jit(solution)/shard_map/ppermute | solution.py:263

commit v3 on v2

--- a/solution.py
+++ b/solution.py
@@ -132,108 +132,138 @@
 def prepare_kernel(*refs, count):
     pick = refs[0]
     targets = refs[1 : 1 + count]
-    left, wide = refs[1 + count :]
+    left = refs[1 + count : 1 + 2 * count]
+    wide = refs[1 + 2 * count :]
     own = targets[0].shape[1]
-    pair = left.shape[1] // own
-    for g in range(count // pair):
-        both = jnp.concatenate([targets[g * pair + t][...] for t in range(pair)], axis=1)
-        feature = lax.dot_general(both, pick[...], TN, preferred_element_type=jnp.float32)
-        left[g] = feature[:, : 2 * FEAT].astype(jnp.bfloat16)
-        wide[g] = feature[:, 2 * FEAT :]
-
-
-def sum_kernel(*refs, first, count, blocks, numbers):
-    ns = len(numbers)
-    mask, left, wide = refs[0:3]
-    sources = refs[3 : 3 + ns]
-    begin = refs[3 + ns : 3 + ns + count]
-    out = refs[3 + ns + count : 3 + ns + 2 * count]
-    facing, back, fwd_tile, adj_tile, total, stack, geo, scale_q = refs[3 + ns + 2 * count :]
+    both = jnp.concatenate([target[...] for target in targets], axis=1)
+    feature = lax.dot_general(both, pick[...], TN, preferred_element_type=jnp.float32)
+    for t in range(count):
+        lines = slice(t * own, (t + 1) * own)
+        left[t][...] = feature[lines, : 2 * FEAT].astype(jnp.bfloat16)
+        wide[t][...] = feature[lines, 2 * FEAT :]
+
+
+def sum_kernel(*refs, slots, blocks, numbers):
+    ns, count = len(numbers), len(slots)
+    refs = list(refs)
+
+    def take(amount):
+        taken = refs[:amount]
+        del refs[:amount]
+        return taken
+
+    mask = take(1)[0]
+    left, wide = take(count), take(count)
+    sources = take(ns)
+    begin, out = take(count), take(count)
+    facing, back, fwd_tile, adj_tile = take(2), take(2), take(2), take(2)
+    total, stack, geo, scale_q = refs
     own = out[0].shape[1]
     cases = out[0].shape[0] // 2
     per = own // BLK
-    span = left.shape[1]
-    pair = span // own
-    groups = count // pair
     for t in range(count):
         total[t] = begin[t][...]
 
-    def match(k, g, slot, source):
+    def match(slot, source):
         slab = source[2 * cases : 2 * cases + SLAB, :]
         right = jnp.concatenate([slab, slab, slab, jnp.ones_like(slab)], axis=0)
-        facing[slot] = jnp.dot(left[g, :, :FEAT], right, preferred_element_type=jnp.float32)
-        back[slot] = jnp.dot(left[g, :, FEAT:], right, preferred_element_type=jnp.float32)
-
-    def measure(k, slot, source):
+
+        def piece(t, which):
+            cols = slice(FEAT, 2 * FEAT) if which else slice(0, FEAT)
+            (back if which else facing)[slot][t * own : (t + 1) * own, :] = jnp.dot(
+                left[t][:, cols], right, preferred_element_type=jnp.float32
+            )
+
+        return [functools.partial(piece, t, which) for t in range(count) for which in (0, 1)]
+
+    def measure(slot, source):
         exact = source[2 * cases :, :].astype(jnp.float32)
         geo[slot, 0:3, :] = exact[0:3] + exact[3:6] + exact[6:9]
         area_q = exact[21:22] + exact[22:23] + exact[23:24]
         geo[slot, 3:4, :] = area_q
         scale_q[slot] = exact[GEO:] * (area_q * (1.0 / math.pi))
 
-    def build(k, g, slot, side):
+    def build(k, slot, woven=()):
+        spots, spot = count * own // ROWS, 0
+        amount, done = len(woven), 0
+        marks = []
         for jb in range(per):
             lanes = slice(jb * BLK, (jb + 1) * BLK)
-            xq = geo[side, 0:1, lanes]
-            yq = geo[side, 1:2, lanes]
-            zq = geo[side, 2:3, lanes]
-            aq = geo[side, 3:4, lanes]
-            for block in range(pair * per):
-                row = (first + g * pair) * per + block
-                scale = one_row(scale_q.at[side], row, lanes)
-                sees = one_row(mask, k * blocks + row, lanes)
-                for start in range(block * BLK, (block + 1) * BLK, ROWS):
+            marks.append((lanes, [geo[slot, c : c + 1, lanes] for c in range(4)]))
+        for t in range(count):
+            for ib in range(per):
+                row = slots[t] * per + ib
+                pairs = [
+                    (lanes, place, one_row(scale_q.at[slot], row, lanes), one_row(mask, k * blocks + row, lanes))
+                    for lanes, place in marks
+                ]
+                for start in range(ib * BLK, (ib + 1) * BLK, ROWS):
                     here = slice(start, start + ROWS)
-                    dx = wide[g, here, 0:BLK] - xq
-                    dy = wide[g, here, BLK : 2 * BLK] - yq
-                    dz = wide[g, here, 2 * BLK : 3 * BLK] - zq
-                    area = wide[g, here, 3 * BLK :]
-                    square = dx * dx + dy * dy + dz * dz
-                    product = jnp.maximum(facing[slot, here, lanes], 0.0) * jnp.maximum(back[slot, here, lanes], 0.0)
-                    near = square + aq
-                    far = square + area
-                    fwd_tile[slot, here, lanes] = (product * scale / (near * near)).astype(jnp.bfloat16)
-                    adj_tile[slot, here, lanes] = (product * sees * area / (far * far)).astype(jnp.bfloat16)
-
-    def collect(g, slot, source):
-        incoming = lax.dot_general(source[0:cases, :], fwd_tile[slot], NT, preferred_element_type=jnp.float32)
-        returned = lax.dot_general(
-            source[cases : 2 * cases, :], adj_tile[slot], NT, preferred_element_type=jnp.float32
-        )
-        for t in range(pair):
-            s = g * pair + t
-            total[s, 0:cases, :] += incoming[:, t * own : (t + 1) * own]
-            total[s, cases:, :] += returned[:, t * own : (t + 1) * own]
-
-    if ns * groups <= 8:
-        steps = [(i, g) for i in range(ns) for g in range(groups)]
-        for number, (i, g) in enumerate(steps):
+                    there = slice(t * own + start, t * own + start + ROWS)
+                    x, y, z, area = (wide[t][here, c * BLK : (c + 1) * BLK] for c in range(4))
+                    for lanes, (xq, yq, zq, aq), scale, sees in pairs:
+                        dx = x - xq
+                        dy = y - yq
+                        dz = z - zq
+                        square = dx * dx + dy * dy + dz * dz
+                        faced = jnp.maximum(facing[slot][there, lanes], 0.0)
+                        product = faced * jnp.maximum(back[slot][there, lanes], 0.0)
+                        near = square + aq
+                        far = square + area
+                        fwd_tile[slot][there, lanes] = (product * scale / (near * near)).astype(jnp.bfloat16)
+                        adj_tile[slot][there, lanes] = (product * sees * area / (far * far)).astype(jnp.bfloat16)
+                    spot += 1
+                    due = spot * amount // spots
+                    while done < due:
+                        woven[done]()
+                        done += 1
+
+    def collect(slot, source):
+        def piece(t, which):
+            lines = slice(cases, 2 * cases) if which else slice(0, cases)
+            tile = (adj_tile if which else fwd_tile)[slot][t * own : (t + 1) * own, :]
+            total[t, lines, :] += lax.dot_general(source[lines, :], tile, NT, preferred_element_type=jnp.float32)
+
+        return [functools.partial(piece, t, which) for t in range(count) for which in (0, 1)]
+
+    if ns <= 4:
+        late = []
+        for number, k in enumerate(numbers):
             if number == 0:
-                measure(numbers[i], i % 2, sources[i])
-                match(numbers[i], g, 0, sources[i])
-            if number + 1 < len(steps):
-                j, h = steps[number + 1]
-                if j != i:
-                    measure(numbers[j], j % 2, sources[j])
-                match(numbers[j], h, (number + 1) % 2, sources[j])
-            build(numbers[i], g, number % 2, i % 2)
-            collect(g, number % 2, sources[i])
+                measure(0, sources[0])
+                for piece in match(0, sources[0]):
+                    piece()
+            if number + 1 < ns:
+                measure((number + 1) % 2, sources[number + 1])
+                late = late + match((number + 1) % 2, sources[number + 1])
+            build(k, number % 2, late)
+            late = collect(number % 2, sources[number])
+        for piece in late:
+            piece()
     else:
         for i in range(ns):
             stack[i] = sources[i][...]
 
-        def step(number, _):
-            i, g = number // groups, number % groups
+        def step(i, _):
             source = stack.at[i]
-            measure(numbers[0] + i, 0, source)
-            match(numbers[0] + i, g, 0, source)
-            build(numbers[0] + i, g, 0, 0)
-            collect(g, 0, source)
+            measure(0, source)
+            for piece in match(0, source):
+                piece()
+            build(numbers[0] + i, 0)
+            for piece in collect(0, source):
+                piece()
             return 0
 
-        lax.fori_loop(0, ns * groups, step, 0)
+        lax.fori_loop(0, ns, step, 0)
     for t in range(count):
         out[t][...] = total[t]
+
+
+def join_kernel(*refs):
+    total = refs[0][...]
+    for piece in refs[1:-1]:
+        total = total + piece[...]
+    refs[-1][...] = total
 
 
 def finish_kernel(*refs, nr):
@@ -338,64 +368,72 @@
     sums = jax.ShapeDtypeStruct((2 * cases, own), f32)
     zero = jnp.zeros((2 * cases, own), f32)
 
+    left_kind = jax.ShapeDtypeStruct((own, 2 * FEAT), jnp.bfloat16)
+    wide_kind = jax.ShapeDtypeStruct((own, 4 * BLK), f32)
+
     def prepare(chosen):
         count = len(chosen)
-        pair = min(count, 2)
-        return pl.pallas_call(
+        made = pl.pallas_call(
             functools.partial(prepare_kernel, count=count),
-            out_shape=(
-                jax.ShapeDtypeStruct((count // pair, pair * own, 2 * FEAT), jnp.bfloat16),
-                jax.ShapeDtypeStruct((count // pair, pair * own, 4 * BLK), f32),
-            ),
+            out_shape=(left_kind,) * count + (wide_kind,) * count,
             in_specs=[vmem] * (1 + count),
-            out_specs=(vmem, vmem),
-            compiler_params=small,
+            out_specs=(vmem,) * (2 * count),
+            compiler_params=pltpu.CompilerParams(vmem_limit_bytes=(2 + 3 * count) << 20),
             cost_estimate=busy(0.2 * count),
         )(pick, *chosen)
-
-    def add(first, shape, numbers, begin):
-        count = len(begin)
-        pair = min(count, 2)
-        many = len(numbers) * (count // pair) > 8
+        return list(zip(made[:count], made[count:]))
+
+    def add(slots, numbers, begin):
+        count, ns = len(slots), len(numbers)
         return list(
             pl.pallas_call(
-                functools.partial(sum_kernel, first=first, count=count, blocks=blocks, numbers=numbers),
+                functools.partial(sum_kernel, slots=slots, blocks=blocks, numbers=numbers),
                 out_shape=(sums,) * count,
-                in_specs=[vmem] * (3 + len(numbers) + count),
+                in_specs=[vmem] * (1 + 3 * count + ns),
                 out_specs=(vmem,) * count,
                 scratch_shapes=[
-                    pltpu.VMEM((2, pair * own, own), f32),
-                    pltpu.VMEM((2, pair * own, own), f32),
-                    pltpu.VMEM((2, pair * own, own), jnp.bfloat16),
-                    pltpu.VMEM((2, pair * own, own), jnp.bfloat16),
+                    *[pltpu.VMEM((count * own, own), f32)] * 4,
+                    *[pltpu.VMEM((count * own, own), jnp.bfloat16)] * 4,
                     pltpu.VMEM((count, 2 * cases, own), f32),
-                    pltpu.VMEM((len(numbers) if many else 1, rows, own), jnp.bfloat16),
+                    pltpu.VMEM((ns if ns > 4 else 1, rows, own), jnp.bfloat16),
                     pltpu.VMEM((2, 8, own), f32),
                     pltpu.VMEM((2, blocks, own), f32),
                 ],
                 compiler_params=pltpu.CompilerParams(vmem_limit_bytes=12 << 20),
-                cost_estimate=busy(0.3 * count * len(numbers)),
-            )(mask, *shape, *[sources[k] for k in numbers], *begin)
+                cost_estimate=busy(0.3 * count * ns),
+            )(
+                mask,
+                *[shapes[t][0] for t in slots],
+                *[shapes[t][1] for t in slots],
+                *[sources[k] for k in numbers],
+                *begin,
+            )
         )
 
-    own_shape = prepare(targets[:1])
-    core_shape = prepare(targets[1:2])
-    far_shape = prepare(targets[2:])
+    shapes = prepare(targets[:2]) + prepare(targets[2:])
     rest = tuple(range(1, nz))
-    own_sums = add(0, own_shape, (0,), [source])
-    core_sums = add(1, core_shape, (0,), [zero])
-    far_sums = add(2, far_shape, (0,), [zero] * (nr - 2))
-    core_sums = add(1, core_shape, rest, core_sums)
-    far_sums, core_sums = lax.optimization_barrier((far_sums, core_sums))
-    far_sums = add(2, far_shape, rest, far_sums)
-    far_sums, own_sums = lax.optimization_barrier((far_sums, own_sums))
-    own_sums = add(0, own_shape, rest, own_sums)
-    pieces = [swap(x, "recv", s) for s, x in enumerate(own_sums + core_sums + far_sums)]
+    begun = []
+    for first in range(0, nr, 2):
+        begun += add((first, first + 1), (0,), [zero if first else source, zero])
+    far_sums = []
+    for first in range(2, nr, 2):
+        far_sums += add((first, first + 1), rest, begun[first : first + 2])
+    far_sums, near_sums = lax.optimization_barrier((far_sums, begun[:2]))
+    near_sums = add((0, 1), rest, near_sums)
+    far = pl.pallas_call(
+        join_kernel,
+        out_shape=sums,
+        in_specs=[vmem] * (nr - 2),
+        out_specs=vmem,
+        compiler_params=small,
+        cost_estimate=busy(8.0),
+    )(*[swap(x, "recv", s + 2) for s, x in enumerate(far_sums)])
+    pieces = [far, near_sums[0], swap(near_sums[1], "recv", 1)]
     whole = jax.ShapeDtypeStruct((cases, own), f32)
     radiosity_out, adjoint_out, gradient = pl.pallas_call(
-        functools.partial(finish_kernel, nr=nr),
+        functools.partial(finish_kernel, nr=len(pieces)),
         out_shape=(whole, whole, jax.ShapeDtypeStruct((1, own), f32)),
-        in_specs=[vmem] * (2 + nr),
+        in_specs=[vmem] * (2 + len(pieces)),
         out_specs=(vmem, vmem, vmem),
         compiler_params=small,
     )(mine, power, *pieces)

time: 23.5 us -> 22.4 us (0.953)
  Pallas kernels: 8.62 us -> 7.67 us
  waiting for transfers between devices: 4.22 us -> 3.8 us
    pallas_call x7 -> x6, Pallas kernels: 6.02 us -> 5.24 us  [the longest x4 4.59 us: add(): pl.pallas_call(functools.partial(sum_kernel, slots=slots, blocks=blocks,...]
    ppermute x9, waiting for transfers between devices: 4.22 us -> 3.8 us  [swap(): lax.ppermute(x, axis, [(i, i ^ other) for i in range(lax.axis_size(axis))])]
    pallas_call x3 -> x2, Pallas kernels: 0.94 us -> 0.77 us  [prepare(): pl.pallas_call(functools.partial(prepare_kernel, count=count), out_shape=...]
  transfers between devices with their start and end apart: 9 -> 9, of which waited for: 3 -> 2; matrix products, arithmetic and copies ran while one was open for 0% -> 0% of each run, Pallas kernels for 18% -> 19%
where the time goes in v3:
time: 22.4 us; the launch traced here: 22.2 us
  starting transfers between devices  9.75 us (44%)
  Pallas kernels  7.67 us (34%)
  waiting for transfers between devices  3.8 us (17%)
  between operations  0.72 us (3%)
  local copies, waits for them, and re-layouts  0.23 us (1%)
    ppermute x9, starting transfers between devices, swap(): lax.ppermute(x, axis, [(i, i ^ other) for i in range(lax.axis_size(axis))])  9.75 us
    pallas_call x4, Pallas kernels, add(): pl.pallas_call(functools.partial(sum_kernel, slots=slots, blocks=blocks,...  4.59 us
    ppermute x9, waiting for transfers between devices, swap(): lax.ppermute(x, axis, [(i, i ^ other) for i in range(lax.axis_size(axis))])  3.8 us
    pallas_call x1, Pallas kernels, local(): pl.pallas_call(functools.partial(pack_kernel, nr=nr, nz=nz, held=len(give...  1.2 us
    pallas_call x2, Pallas kernels, prepare(): pl.pallas_call(functools.partial(prepare_kernel, count=count), out_shape=...  0.77 us
    pallas_call x1, Pallas kernels, local(): pl.pallas_call(functools.partial(finish_kernel, nr=len(pieces)), out_shap...  0.64 us
    pallas_call x1, Pallas kernels, local(): pl.pallas_call(source_kernel, out_shape=jax.ShapeDtypeStruct((2 * cases,...  0.45 us
  transfers between devices with their start and end apart: 9, of which 2 were waited for; matrix products, arithmetic and copies ran while one was open for 0% of the time, Pallas kernels for 19%

profile of v3, /device:TPU:0, one launch (start us, length us, event | category | flops | bytes accessed | tf_op | source)
XLA Modules:
  0.0 22.2 jit_solution(12883967959792032692)
XLA Ops:
  0.6 1.2 %shard_map.130 = (bf16[32,256]{1,0:T(8,128)(2,1)S(1)}, bf16[96,256]{1,0:T(8,128)(2,1)S(1)}, bf16[96,256]{1,0:T(8,128)(2,1)S(1)}, bf16[96,256]{1,0:T(8,128)(2,1)S...) custom-call(s32[8,32]{1,0:T(8,128)} %refs_0_.3, ...), custom_call_target="tpu_custom_call" | custom-call | tf_op jit(solution)/shard_map/pallas_call | solution.py:333
  1.8 0.5 %collective-permute-start.5 = (bf16[32,256]{1,0:T(8,128)(2,1)S(1)}, bf16[32,256]{1,0:T(8,128)(2,1)S(1)}, u32[]{:S(2)}, u32[]{:S(2)}) collective-permute-start(bf16[32,256]{1,0:T(8,128)(2,1)S(1)} %get-tuple-element.39.refs_1_), channel_id=1, source_target_pairs={{0,1},{1,0},{2,3},{3,2},{4,5},{5,4},{6,7},{7,6},{8,9},{9,8},{10,11... | collective-permute-start | bytes 49160 | tf_op jit(solution)/shard_map/ppermute | solution.py:293
  2.4 2.6 %collective-permute-start = (bf16[32,256]{1,0:T(8,128)(2,1)S(1)}, bf16[32,256]{1,0:T(8,128)(2,1)S(1)}, u32[]{:S(2)}, u32[]{:S(2)}) collective-permute-start(bf16[32,256]{1,0:T(8,128)(2,1)S(1)} %get-tuple-element.39.refs_1_), channel_id=1, source_target_pairs={{0,2},{1,3},{2,0},{3,1},{4,6},{5,7},{6,4},{7,5},{8,10},{9,11},{10,... | collective-permute-start | bytes 49160 | tf_op jit(solution)/shard_map/ppermute | solution.py:293
  4.9 1.6 %collective-permute-start.2 = (bf16[96,256]{1,0:T(8,128)(2,1)S(1)}, bf16[96,256]{1,0:T(8,128)(2,1)S(1)}, u32[]{:S(2)}, u32[]{:S(2)}) collective-permute-start(bf16[96,256]{1,0:T(8,128)(2,1)S(1)} %get-tuple-element.44), channel_id=1, source_target_pairs={{0,4},{4,0},{8,12},{12,8},{1,5},{5,1},{9,13},{13,9},{2,6},{6,2},{1... | collective-permute-start | bytes 147464 | tf_op jit(solution)/shard_map/ppermute | solution.py:293
  6.5 2.6 %collective-permute-start.3 = (bf16[96,256]{1,0:T(8,128)(2,1)S(1)}, bf16[96,256]{1,0:T(8,128)(2,1)S(1)}, u32[]{:S(2)}, u32[]{:S(2)}) collective-permute-start(bf16[96,256]{1,0:T(8,128)(2,1)S(1)} %get-tuple-element.45), channel_id=1, source_target_pairs={{0,8},{4,12},{8,0},{12,4},{1,9},{5,13},{9,1},{13,5},{2,10},{6,14},... | collective-permute-start | bytes 147464 | tf_op jit(solution)/shard_map/ppermute | solution.py:293
  9.1 0.2 collective-permute-start.4
  9.3 0.0 copy-start
  9.3 0.5 %shard_map.135.refs_6_ = f32[64,256]{1,0:T(8,128)S(1)} custom-call(s32[1,2048]{1,0:T(1,128)S(1)} %get-tuple-element.56.ids, f32[32,2048]{1,0:T(8,128)S(1)} %get-tuple-element.57.weights), custom_call_target="tpu_custom_call" | custom-call | flops 550000000 | tf_op jit(solution)/shard_map/pallas_call | solution.py:359
  9.8 0.0 collective-permute-done.refs_1_
  9.8 0.1 collective-permute-start.1
  9.9 0.0 collective-permute-done.5.refs_2_
  9.9 0.2 %copy-done = bf16[32,768]{1,0:T(8,128)(2,1)S(1)} copy-done((bf16[32,768]{1,0:T(8,128)(2,1)S(1)}, bf16[32,768]{1,0:T(8,128)(2,1)}, u32[]{:S(2)}) %copy-start) | copy-done | bytes 49176
  10.1 0.4 %shard_map.134 = (bf16[256,256]{1,0:T(8,128)(2,1)S(1)}, bf16[256,256]{1,0:T(8,128)(2,1)S(1)}, f32[256,512]{1,0:T(8,128)S(1)}, f32[256,512]{1,0:T(8,128)S(1)}) custom-call(bf16[32,768]{1,0:T(8,128)(2,1)S(1)} %copy-done, bf16[32,256]{1,0:T(8,128)(2,1)S(1)} %get-tuple-element.39.refs_1_, bf16[32,256]{1,0:T(8,128)(2,1)S(1)} %collective-permute-done.5.refs_2_), custom_call_target="tpu_custom_call" | custom-call | flops 440000000 | tf_op jit(solution)/shard_map/pallas_call | solution.py:376
  10.5 0.7 %shard_map.136 = (f32[64,256]{1,0:T(8,128)S(1)}, f32[64,256]{1,0:T(8,128)S(1)}) custom-call(f32[32,256]{1,0:T(8,128)S(1)} %get-tuple-element.38.refs_0_, bf16[256,256]{1,0:T(8,128)(2,1)S(1)} %get-tuple-element.52.refs_1_, bf16[256,256]{1,0:T(8,128)(2,1)S(1)} %get-tuple-element.53.refs_2_, f32[256,512]{1,0:T(8,128)S(1)} %get-tuple-element.54.refs_3_, ...), custom_call_target="tpu_custom_call" | custom-call | flops 660000000 | tf_op jit(solution)/shard_map/pallas_call | solution.py:389
  11.2 0.0 collective-permute-done.1.refs_2_
  11.3 0.4 %shard_map.131 = (bf16[256,256]{1,0:T(8,128)(2,1)S(1)}, bf16[256,256]{1,0:T(8,128)(2,1)S(1)}, f32[256,512]{1,0:T(8,128)S(1)}, f32[256,512]{1,0:T(8,128)S(1)}) custom-call(bf16[32,768]{1,0:T(8,128)(2,1)S(1)} %copy-done, bf16[32,256]{1,0:T(8,128)(2,1)S(1)} %collective-permute-done.refs_1_, bf16[32,256]{1,0:T(8,128)(2,1)S(1)} %collective-permute-done.1.refs_2_), custom_call_target="tpu_custom_call" | custom-call | flops 440000000 | tf_op jit(solution)/shard_map/pallas_call | solution.py:376
  11.6 0.7 %shard_map.132 = (f32[64,256]{1,0:T(8,128)S(1)}, f32[64,256]{1,0:T(8,128)S(1)}) custom-call(f32[32,256]{1,0:T(8,128)S(1)} %get-tuple-element.38.refs_0_, bf16[256,256]{1,0:T(8,128)(2,1)S(1)} %get-tuple-element.40.refs_1_, bf16[256,256]{1,0:T(8,128)(2,1)S(1)} %get-tuple-element.41.refs_2_, f32[256,512]{1,0:T(8,128)S(1)} %get-tuple-element.42.refs_3_, ...), custom_call_target="tpu_custom_call" | custom-call | flops 660000000 | tf_op jit(solution)/shard_map/pallas_call | solution.py:389
  12.4 0.0 collective-permute-done.2.refs_5_
  12.4 0.0 collective-permute-done.3.refs_6_
  12.4 2.6 %collective-permute-done.4.refs_7_ = bf16[96,256]{1,0:T(8,128)(2,1)S(1)} collective-permute-done((bf16[96,256]{1,0:T(8,128)(2,1)S(1)}, bf16[96,256]{1,0:T(8,128)(2,1)S(1)}, u32[]{:S(2)}, u32[]{:S(2)}) %collective-permute-start.4) | collective-permute-done | bytes 49184 | tf_op jit(solution)/shard_map/ppermute | solution.py:293
  15.0 1.6 %shard_map.133 = (f32[64,256]{1,0:T(8,128)S(1)}, f32[64,256]{1,0:T(8,128)S(1)}) custom-call(f32[32,256]{1,0:T(8,128)S(1)} %get-tuple-element.38.refs_0_, bf16[256,256]{1,0:T(8,128)(2,1)S(1)} %get-tuple-element.40.refs_1_, bf16[256,256]{1,0:T(8,128)(2,1)S(1)} %get-tuple-element.41.refs_2_, f32[256,512]{1,0:T(8,128)S(1)} %get-tuple-element.42.refs_3_, ...), custom_call_target="tpu_custom_call" | custom-call | flops 1980000000 | tf_op jit(solution)/shard_map/pallas_call | solution.py:389
  16.6 0.6 %collective-permute-start.6 = (f32[64,256]{1,0:T(8,128)S(1)}, f32[64,256]{1,0:T(8,128)S(1)}, u32[]{:S(2)}, u32[]{:S(2)}) collective-permute-start(f32[64,256]{1,0:T(8,128)S(1)} %get-tuple-element.60), channel_id=1, source_target_pairs={{0,2},{1,3},{2,0},{3,1},{4,6},{5,7},{6,4},{7,5},{8,10},{9,11},{10,... | collective-permute-start | bytes 196616 | tf_op jit(solution)/shard_map/ppermute | solution.py:293
  17.1 0.0 collective-permute-start.7
  17.1 1.6 %shard_map.138 = (f32[64,256]{1,0:T(8,128)S(1)}, f32[64,256]{1,0:T(8,128)S(1)}) custom-call(f32[32,256]{1,0:T(8,128)S(1)} %get-tuple-element.38.refs_0_, bf16[256,256]{1,0:T(8,128)(2,1)S(1)} %get-tuple-element.52.refs_1_, bf16[256,256]{1,0:T(8,128)(2,1)S(1)} %get-tuple-element.53.refs_2_, f32[256,512]{1,0:T(8,128)S(1)} %get-tuple-element.54.refs_3_, ...), custom_call_target="tpu_custom_call" | custom-call | flops 1980000000 | tf_op jit(solution)/shard_map/pallas_call | solution.py:389
  18.7 1.6 %collective-permute-start.8 = (f32[64,256]{1,0:T(8,128)S(1)}, f32[64,256]{1,0:T(8,128)S(1)}, u32[]{:S(2)}, u32[]{:S(2)}) collective-permute-start(f32[64,256]{1,0:T(8,128)S(1)} %get-tuple-element.65), channel_id=1, source_target_pairs={{0,1},{1,0},{2,3},{3,2},{4,5},{5,4},{6,7},{7,6},{8,9},{9,8},{10,11... | collective-permute-start | bytes 196616 | tf_op jit(solution)/shard_map/ppermute | solution.py:293
  20.3 1.2 %collective-permute-done.6.refs_0_ = f32[64,256]{1,0:T(8,128)S(1)} collective-permute-done((f32[64,256]{1,0:T(8,128)S(1)}, f32[64,256]{1,0:T(8,128)S(1)}, u32[]{:S(2)}, u32[]{:S(2)}) %collective-permute-start.6) | collective-permute-done | bytes 65568 | tf_op jit(solution)/shard_map/ppermute | solution.py:293
  21.5 0.0 collective-permute-done.7.refs_1_
  21.5 0.0 collective-permute-done.8.refs_4_
  21.5 0.6 %shard_map.139 = (f32[32,256]{1,0:T(8,128)}, f32[32,256]{1,0:T(8,128)}, f32[1,256]{1,0:T(1,128)}) custom-call(f32[1,256]{1,0:T(1,128)S(1)} %get-tuple-element.36.refs_0_, f32[32,256]{1,0:T(8,128)S(1)} %get-tuple-element.37.refs_1_, f32[64,256]{1,0:T(8,128)S(1)} %shard_map.137.refs_2_, f32[64,256]{1,0:T(8,128)S(1)} %get-tuple-element.64.refs_3_, ...), custom_call_target="tpu_custom_call" | custom-call | tf_op jit(solution)/shard_map/pallas_call | solution.py:433
  (2 shorter events, 0.0 us)
Async XLA Ops:
  1.8 8.0 %collective-permute-start.5 = (bf16[32,256]{1,0:T(8,128)(2,1)S(1)}, bf16[32,256]{1,0:T(8,128)(2,1)S(1)}, u32[]{:S(2)}, u32[]{:S(2)}) collective-permute-start(bf16[32,256]{1,0:T(8,128)(2,1)S(1)} %get-tuple-element.39.refs_1_), channel_id=1, source_target_pairs={{0,1},{1,0},{2,3},{3,2},{4,5},{5,4},{6,7},{7,6},{8,9},{9,8},{10,11... | collective-permute-start | bytes 49160 | tf_op jit(solution)/shard_map/ppermute | solution.py:293
  2.4 7.4 %collective-permute-start = (bf16[32,256]{1,0:T(8,128)(2,1)S(1)}, bf16[32,256]{1,0:T(8,128)(2,1)S(1)}, u32[]{:S(2)}, u32[]{:S(2)}) collective-permute-start(bf16[32,256]{1,0:T(8,128)(2,1)S(1)} %get-tuple-element.39.refs_1_), channel_id=1, source_target_pairs={{0,2},{1,3},{2,0},{3,1},{4,6},{5,7},{6,4},{7,5},{8,10},{9,11},{10,... | collective-permute-start | bytes 49160 | tf_op jit(solution)/shard_map/ppermute | solution.py:293
  4.9 7.5 %collective-permute-start.2 = (bf16[96,256]{1,0:T(8,128)(2,1)S(1)}, bf16[96,256]{1,0:T(8,128)(2,1)S(1)}, u32[]{:S(2)}, u32[]{:S(2)}) collective-permute-start(bf16[96,256]{1,0:T(8,128)(2,1)S(1)} %get-tuple-element.44), channel_id=1, source_target_pairs={{0,4},{4,0},{8,12},{12,8},{1,5},{5,1},{9,13},{13,9},{2,6},{6,2},{1... | collective-permute-start | bytes 147464 | tf_op jit(solution)/shard_map/ppermute | solution.py:293
  6.5 5.9 %collective-permute-start.3 = (bf16[96,256]{1,0:T(8,128)(2,1)S(1)}, bf16[96,256]{1,0:T(8,128)(2,1)S(1)}, u32[]{:S(2)}, u32[]{:S(2)}) collective-permute-start(bf16[96,256]{1,0:T(8,128)(2,1)S(1)} %get-tuple-element.45), channel_id=1, source_target_pairs={{0,8},{4,12},{8,0},{12,4},{1,9},{5,13},{9,1},{13,5},{2,10},{6,14},... | collective-permute-start | bytes 147464 | tf_op jit(solution)/shard_map/ppermute | solution.py:293
  9.1 5.9 %collective-permute-start.4 = (bf16[96,256]{1,0:T(8,128)(2,1)S(1)}, bf16[96,256]{1,0:T(8,128)(2,1)S(1)}, u32[]{:S(2)}, u32[]{:S(2)}) collective-permute-start(bf16[96,256]{1,0:T(8,128)(2,1)S(1)} %get-tuple-element.46), channel_id=1, source_target_pairs={{0,12},{4,8},{8,4},{12,0},{1,13},{5,9},{9,5},{13,1},{2,14},{6,10},... | collective-permute-start | bytes 147464 | tf_op jit(solution)/shard_map/ppermute | solution.py:293
  9.3 0.8 %copy-start = (bf16[32,768]{1,0:T(8,128)(2,1)S(1)}, bf16[32,768]{1,0:T(8,128)(2,1)}, u32[]{:S(2)}) copy-start(bf16[32,768]{1,0:T(8,128)(2,1)} %constant.4.clone.refs_0_) | copy-start | bytes 147460
  9.8 1.4 %collective-permute-start.1 = (bf16[32,256]{1,0:T(8,128)(2,1)S(1)}, bf16[32,256]{1,0:T(8,128)(2,1)S(1)}, u32[]{:S(2)}, u32[]{:S(2)}) collective-permute-start(bf16[32,256]{1,0:T(8,128)(2,1)S(1)} %collective-permute-done.refs_1_), channel_id=1, source_target_pairs={{0,1},{1,0},{2,3},{3,2},{4,5},{5,4},{6,7},{7,6},{8,9},{9,8},{10,11... | collective-permute-start | bytes 49160 | tf_op jit(solution)/shard_map/ppermute | solution.py:293
  16.6 5.0 %collective-permute-start.6 = (f32[64,256]{1,0:T(8,128)S(1)}, f32[64,256]{1,0:T(8,128)S(1)}, u32[]{:S(2)}, u32[]{:S(2)}) collective-permute-start(f32[64,256]{1,0:T(8,128)S(1)} %get-tuple-element.60), channel_id=1, source_target_pairs={{0,2},{1,3},{2,0},{3,1},{4,6},{5,7},{6,4},{7,5},{8,10},{9,11},{10,... | collective-permute-start | bytes 196616 | tf_op jit(solution)/shard_map/ppermute | solution.py:293
  17.1 4.4 %collective-permute-start.7 = (f32[64,256]{1,0:T(8,128)S(1)}, f32[64,256]{1,0:T(8,128)S(1)}, u32[]{:S(2)}, u32[]{:S(2)}) collective-permute-start(f32[64,256]{1,0:T(8,128)S(1)} %get-tuple-element.61), channel_id=1, source_target_pairs={{0,3},{1,2},{2,1},{3,0},{4,7},{5,6},{6,5},{7,4},{8,11},{9,10},{10,... | collective-permute-start | bytes 196616 | tf_op jit(solution)/shard_map/ppermute | solution.py:293
  18.7 2.8 %collective-permute-start.8 = (f32[64,256]{1,0:T(8,128)S(1)}, f32[64,256]{1,0:T(8,128)S(1)}, u32[]{:S(2)}, u32[]{:S(2)}) collective-permute-start(f32[64,256]{1,0:T(8,128)S(1)} %get-tuple-element.65), channel_id=1, source_target_pairs={{0,1},{1,0},{2,3},{3,2},{4,5},{5,4},{6,7},{7,6},{8,9},{9,8},{10,11... | collective-permute-start | bytes 196616 | tf_op jit(solution)/shard_map/ppermute | solution.py:293

commit v4 on v3

--- a/solution.py
+++ b/solution.py
@@ -47,9 +47,9 @@
     given = refs[1 : 1 + held]
     target_ref = refs[1 + held]
     sources = refs[2 + held : 2 + held + nz]
-    kept = refs[2 + held + nz : 2 + held + nz + 4]
-    mask_ref = refs[2 + held + nz + 4]
-    place_ref, turn_ref, area_ref, radiosity, adjoint, geo, seen, sems, seen_sem = refs[2 + held + nz + 5 :]
+    kept = refs[2 + held + nz : 2 + held + nz + 5]
+    mask_ref = refs[2 + held + nz + 5]
+    place_ref, turn_ref, area_ref, radiosity, adjoint, geo, seen, sems, seen_sem = refs[2 + held + nz + 6 :]
     emissivity_ref = kept[0]
     landing = (place_ref, turn_ref, area_ref, emissivity_ref, radiosity, adjoint) + tuple(kept[1:])
     copies = [pltpu.make_async_copy(a, b, sems.at[i]) for i, (a, b) in enumerate(zip(given, landing))]
@@ -249,7 +249,7 @@
             measure(0, source)
             for piece in match(0, source):
                 piece()
-            build(numbers[0] + i, 0)
+            build(numbers[0] + i * (numbers[1] - numbers[0]), 0)
             for piece in collect(0, source):
                 piece()
             return 0
@@ -327,6 +327,7 @@
         emission,
         ids,
         inlet_weights,
+        jnp.asarray(selection(), jnp.bfloat16),
     )
     given = tuple(pltpu.with_memory_space_constraint(x, pltpu.HBM) for x in given)
     seen = pltpu.with_memory_space_constraint(visibility, pltpu.HBM)
@@ -334,10 +335,10 @@
         functools.partial(pack_kernel, nr=nr, nz=nz, held=len(given)),
         out_shape=(jax.ShapeDtypeStruct((SLAB, own), jnp.bfloat16),)
         + (jax.ShapeDtypeStruct((rows, own), jnp.bfloat16),) * nz
-        + tuple(jax.ShapeDtypeStruct(given[i].shape, given[i].dtype) for i in (3, 6, 7, 8))
+        + tuple(jax.ShapeDtypeStruct(given[i].shape, given[i].dtype) for i in (3, 6, 7, 8, 9))
         + (jax.ShapeDtypeStruct((nz * blocks, own), f32),),
         in_specs=[hbm] * (1 + len(given)),
-        out_specs=(vmem,) * (1 + nz + 5),
+        out_specs=(vmem,) * (1 + nz + 6),
         scratch_shapes=[
             pltpu.VMEM((3, own), f32),
             pltpu.VMEM((2, own), f32),
@@ -351,11 +352,11 @@
         ],
         compiler_params=small,
     )(seen, *given)
-    mine, power, ids, weights, mask = packed[1 + nz :]
+    mine, power, ids, weights, pick, mask = packed[1 + nz :]
     targets = []
     for s in range(nr):
         targets.append(swap(targets[s - 1], "recv", 1) if s % 2 else swap(packed[0], "recv", s))
-    sources = [swap(packed[1 + k], "emit", k) for k in range(nz)]
+    sources = {k: swap(packed[1 + k], "emit", k) for k in reversed(range(nz))}
     source = pl.pallas_call(
         source_kernel,
         out_shape=jax.ShapeDtypeStruct((2 * cases, own), f32),
@@ -364,7 +365,6 @@
         compiler_params=small,
         cost_estimate=busy(0.5),
     )(ids, weights)
-    pick = jnp.asarray(selection(), jnp.bfloat16)
     sums = jax.ShapeDtypeStruct((2 * cases, own), f32)
     zero = jnp.zeros((2 * cases, own), f32)
 
@@ -411,7 +411,7 @@
         )
 
     shapes = prepare(targets[:2]) + prepare(targets[2:])
-    rest = tuple(range(1, nz))
+    rest = tuple(range(nz - 1, 0, -1))
     begun = []
     for first in range(0, nr, 2):
         begun += add((first, first + 1), (0,), [zero if first else source, zero])
@@ -427,7 +427,7 @@
         out_specs=vmem,
         compiler_params=small,
         cost_estimate=busy(8.0),
-    )(*[swap(x, "recv", s + 2) for s, x in enumerate(far_sums)])
+    )(*[swap(far_sums[s - 2], "recv", s) for s in reversed(range(2, nr))])
     pieces = [far, near_sums[0], swap(near_sums[1], "recv", 1)]
     whole = jax.ShapeDtypeStruct((cases, own), f32)
     radiosity_out, adjoint_out, gradient = pl.pallas_call(

time: 22.4 us -> 21 us (0.938)
  waiting for transfers between devices: 3.8 us -> 2.91 us
  starting transfers between devices: 9.75 us -> 9.47 us
    ppermute x9, waiting for transfers between devices: 3.8 us -> 2.91 us  [swap(): lax.ppermute(x, axis, [(i, i ^ other) for i in range(lax.axis_size(axis))])]
    ppermute x9, starting transfers between devices: 9.75 us -> 9.47 us  [swap(): lax.ppermute(x, axis, [(i, i ^ other) for i in range(lax.axis_size(axis))])]
    unnamed x2 -> x0, local copies, waits for them, and re-layouts: 0.23 us -> none
  transfers between devices with their start and end apart: 9 -> 9, of which waited for: 2 -> 3; matrix products, arithmetic and copies ran while one was open for 0% -> 0% of each run, Pallas kernels for 19% -> 21%
where the time goes in v4:
time: 21 us; the launch traced here: 20.8 us
  starting transfers between devices  9.47 us (45%)
  Pallas kernels  7.7 us (37%)
  waiting for transfers between devices  2.91 us (14%)
  between operations  0.72 us (3%)
    ppermute x9, starting transfers between devices, swap(): lax.ppermute(x, axis, [(i, i ^ other) for i in range(lax.axis_size(axis))])  9.47 us
    pallas_call x4, Pallas kernels, add(): pl.pallas_call(functools.partial(sum_kernel, slots=slots, blocks=blocks,...  4.61 us
    ppermute x9, waiting for transfers between devices, swap(): lax.ppermute(x, axis, [(i, i ^ other) for i in range(lax.axis_size(axis))])  2.91 us
    pallas_call x1, Pallas kernels, local(): pl.pallas_call(functools.partial(pack_kernel, nr=nr, nz=nz, held=len(give...  1.21 us
    pallas_call x2, Pallas kernels, prepare(): pl.pallas_call(functools.partial(prepare_kernel, count=count), out_shape=...  0.77 us
    pallas_call x1, Pallas kernels, local(): pl.pallas_call(functools.partial(finish_kernel, nr=len(pieces)), out_shap...  0.64 us
    pallas_call x1, Pallas kernels, local(): pl.pallas_call(source_kernel, out_shape=jax.ShapeDtypeStruct((2 * cases,...  0.45 us
  transfers between devices with their start and end apart: 9, of which 3 were waited for; matrix products, arithmetic and copies ran while one was open for 0% of the time, Pallas kernels for 21%

profile of v4, /device:TPU:0, one launch (start us, length us, event | category | flops | bytes accessed | tf_op | source)
XLA Modules:
  0.0 20.8 jit_solution(14917428709769650569)
XLA Ops:
  0.6 1.2 %shard_map.130 = (bf16[32,256]{1,0:T(8,128)(2,1)S(1)}, bf16[96,256]{1,0:T(8,128)(2,1)S(1)}, bf16[96,256]{1,0:T(8,128)(2,1)S(1)}, bf16[96,256]{1,0:T(8,128)(2,1)S...) custom-call(s32[8,32]{1,0:T(8,128)} %refs_0_.1, ...), custom_call_target="tpu_custom_call" | custom-call | tf_op jit(solution)/shard_map/pallas_call | solution.py:334
  1.9 0.5 %collective-permute-start.5 = (bf16[32,256]{1,0:T(8,128)(2,1)S(1)}, bf16[32,256]{1,0:T(8,128)(2,1)S(1)}, u32[]{:S(2)}, u32[]{:S(2)}) collective-permute-start(bf16[32,256]{1,0:T(8,128)(2,1)S(1)} %get-tuple-element.41.refs_1_), channel_id=1, source_target_pairs={{0,1},{1,0},{2,3},{3,2},{4,5},{5,4},{6,7},{7,6},{8,9},{9,8},{10,11... | collective-permute-start | bytes 49160 | tf_op jit(solution)/shard_map/ppermute | solution.py:293
  2.4 2.6 %collective-permute-start = (bf16[32,256]{1,0:T(8,128)(2,1)S(1)}, bf16[32,256]{1,0:T(8,128)(2,1)S(1)}, u32[]{:S(2)}, u32[]{:S(2)}) collective-permute-start(bf16[32,256]{1,0:T(8,128)(2,1)S(1)} %get-tuple-element.41.refs_1_), channel_id=1, source_target_pairs={{0,2},{1,3},{2,0},{3,1},{4,6},{5,7},{6,4},{7,5},{8,10},{9,11},{10,... | collective-permute-start | bytes 49160 | tf_op jit(solution)/shard_map/ppermute | solution.py:293
  4.9 3.6 %collective-permute-start.2 = (bf16[96,256]{1,0:T(8,128)(2,1)S(1)}, bf16[96,256]{1,0:T(8,128)(2,1)S(1)}, u32[]{:S(2)}, u32[]{:S(2)}) collective-permute-start(bf16[96,256]{1,0:T(8,128)(2,1)S(1)} %get-tuple-element.46), channel_id=1, source_target_pairs={{0,12},{4,8},{8,4},{12,0},{1,13},{5,9},{9,5},{13,1},{2,14},{6,10},... | collective-permute-start | bytes 147464 | tf_op jit(solution)/shard_map/ppermute | solution.py:293
  8.5 0.0 collective-permute-start.3
  8.5 0.8 %collective-permute-start.4 = (bf16[96,256]{1,0:T(8,128)(2,1)S(1)}, bf16[96,256]{1,0:T(8,128)(2,1)S(1)}, u32[]{:S(2)}, u32[]{:S(2)}) collective-permute-start(bf16[96,256]{1,0:T(8,128)(2,1)S(1)} %get-tuple-element.48), channel_id=1, source_target_pairs={{0,4},{4,0},{8,12},{12,8},{1,5},{5,1},{9,13},{13,9},{2,6},{6,2},{1... | collective-permute-start | bytes 147464 | tf_op jit(solution)/shard_map/ppermute | solution.py:293
  9.3 0.5 %shard_map.135.refs_6_ = f32[64,256]{1,0:T(8,128)S(1)} custom-call(s32[1,2048]{1,0:T(1,128)S(1)} %get-tuple-element.58.ids, f32[32,2048]{1,0:T(8,128)S(1)} %get-tuple-element.59.weights), custom_call_target="tpu_custom_call" | custom-call | flops 550000000 | tf_op jit(solution)/shard_map/pallas_call | solution.py:360
  9.8 0.0 collective-permute-done.refs_1_
  9.8 0.1 collective-permute-start.1
  9.9 0.0 collective-permute-done.5.refs_2_
  9.9 0.4 %shard_map.134 = (bf16[256,256]{1,0:T(8,128)(2,1)S(1)}, bf16[256,256]{1,0:T(8,128)(2,1)S(1)}, f32[256,512]{1,0:T(8,128)S(1)}, f32[256,512]{1,0:T(8,128)S(1)}) custom-call(bf16[32,768]{1,0:T(8,128)(2,1)S(1)} %get-tuple-element.40.refs_0_, bf16[32,256]{1,0:T(8,128)(2,1)S(1)} %get-tuple-element.41.refs_1_, bf16[32,256]{1,0:T(8,128)(2,1)S(1)} %collective-permute-done.5.refs_2_), custom_call_target="tpu_custom_call" | custom-call | flops 440000000 | tf_op jit(solution)/shard_map/pallas_call | solution.py:376
  10.3 0.7 %shard_map.136 = (f32[64,256]{1,0:T(8,128)S(1)}, f32[64,256]{1,0:T(8,128)S(1)}) custom-call(f32[32,256]{1,0:T(8,128)S(1)} %get-tuple-element.39.refs_0_, bf16[256,256]{1,0:T(8,128)(2,1)S(1)} %get-tuple-element.54.refs_1_, bf16[256,256]{1,0:T(8,128)(2,1)S(1)} %get-tuple-element.55.refs_2_, f32[256,512]{1,0:T(8,128)S(1)} %get-tuple-element.56.refs_3_, ...), custom_call_target="tpu_custom_call" | custom-call | flops 660000000 | tf_op jit(solution)/shard_map/pallas_call | solution.py:389
  11.0 0.0 collective-permute-done.1.refs_2_
  11.1 0.4 %shard_map.131 = (bf16[256,256]{1,0:T(8,128)(2,1)S(1)}, bf16[256,256]{1,0:T(8,128)(2,1)S(1)}, f32[256,512]{1,0:T(8,128)S(1)}, f32[256,512]{1,0:T(8,128)S(1)}) custom-call(bf16[32,768]{1,0:T(8,128)(2,1)S(1)} %get-tuple-element.40.refs_0_, bf16[32,256]{1,0:T(8,128)(2,1)S(1)} %collective-permute-done.refs_1_, bf16[32,256]{1,0:T(8,128)(2,1)S(1)} %collective-permute-done.1.refs_2_), custom_call_target="tpu_custom_call" | custom-call | flops 440000000 | tf_op jit(solution)/shard_map/pallas_call | solution.py:376
  11.4 0.7 %shard_map.132 = (f32[64,256]{1,0:T(8,128)S(1)}, f32[64,256]{1,0:T(8,128)S(1)}) custom-call(f32[32,256]{1,0:T(8,128)S(1)} %get-tuple-element.39.refs_0_, bf16[256,256]{1,0:T(8,128)(2,1)S(1)} %get-tuple-element.42.refs_1_, bf16[256,256]{1,0:T(8,128)(2,1)S(1)} %get-tuple-element.43.refs_2_, f32[256,512]{1,0:T(8,128)S(1)} %get-tuple-element.44.refs_3_, ...), custom_call_target="tpu_custom_call" | custom-call | flops 660000000 | tf_op jit(solution)/shard_map/pallas_call | solution.py:389
  12.2 0.0 collective-permute-done.2.refs_5_
  12.2 1.3 %collective-permute-done.3.refs_6_ = bf16[96,256]{1,0:T(8,128)(2,1)S(1)} collective-permute-done((bf16[96,256]{1,0:T(8,128)(2,1)S(1)}, bf16[96,256]{1,0:T(8,128)(2,1)S(1)}, u32[]{:S(2)}, u32[]{:S(2)}) %collective-permute-start.3) | collective-permute-done | bytes 49184 | tf_op jit(solution)/shard_map/ppermute | solution.py:293
  13.5 0.0 collective-permute-done.4.refs_7_
  13.5 1.6 %shard_map.133 = (f32[64,256]{1,0:T(8,128)S(1)}, f32[64,256]{1,0:T(8,128)S(1)}) custom-call(f32[32,256]{1,0:T(8,128)S(1)} %get-tuple-element.39.refs_0_, bf16[256,256]{1,0:T(8,128)(2,1)S(1)} %get-tuple-element.42.refs_1_, bf16[256,256]{1,0:T(8,128)(2,1)S(1)} %get-tuple-element.43.refs_2_, f32[256,512]{1,0:T(8,128)S(1)} %get-tuple-element.44.refs_3_, ...), custom_call_target="tpu_custom_call" | custom-call | flops 1980000000 | tf_op jit(solution)/shard_map/pallas_call | solution.py:389
  15.1 0.0 collective-permute-start.6
  15.2 0.9 %collective-permute-start.7 = (f32[64,256]{1,0:T(8,128)S(1)}, f32[64,256]{1,0:T(8,128)S(1)}, u32[]{:S(2)}, u32[]{:S(2)}) collective-permute-start(f32[64,256]{1,0:T(8,128)S(1)} %get-tuple-element.63), channel_id=1, source_target_pairs={{0,2},{1,3},{2,0},{3,1},{4,6},{5,7},{6,4},{7,5},{8,10},{9,11},{10,... | collective-permute-start | bytes 196616 | tf_op jit(solution)/shard_map/ppermute | solution.py:293
  16.0 1.6 %shard_map.138 = (f32[64,256]{1,0:T(8,128)S(1)}, f32[64,256]{1,0:T(8,128)S(1)}) custom-call(f32[32,256]{1,0:T(8,128)S(1)} %get-tuple-element.39.refs_0_, bf16[256,256]{1,0:T(8,128)(2,1)S(1)} %get-tuple-element.54.refs_1_, bf16[256,256]{1,0:T(8,128)(2,1)S(1)} %get-tuple-element.55.refs_2_, f32[256,512]{1,0:T(8,128)S(1)} %get-tuple-element.56.refs_3_, ...), custom_call_target="tpu_custom_call" | custom-call | flops 1980000000 | tf_op jit(solution)/shard_map/pallas_call | solution.py:389
  17.6 1.0 %collective-permute-start.8 = (f32[64,256]{1,0:T(8,128)S(1)}, f32[64,256]{1,0:T(8,128)S(1)}, u32[]{:S(2)}, u32[]{:S(2)}) collective-permute-start(f32[64,256]{1,0:T(8,128)S(1)} %get-tuple-element.67), channel_id=1, source_target_pairs={{0,1},{1,0},{2,3},{3,2},{4,5},{5,4},{6,7},{7,6},{8,9},{9,8},{10,11... | collective-permute-start | bytes 196616 | tf_op jit(solution)/shard_map/ppermute | solution.py:293
  18.6 0.6 %collective-permute-done.6.refs_0_ = f32[64,256]{1,0:T(8,128)S(1)} collective-permute-done((f32[64,256]{1,0:T(8,128)S(1)}, f32[64,256]{1,0:T(8,128)S(1)}, u32[]{:S(2)}, u32[]{:S(2)}) %collective-permute-start.6) | collective-permute-done | bytes 65568 | tf_op jit(solution)/shard_map/ppermute | solution.py:293
  19.2 0.9 %collective-permute-done.7.refs_1_ = f32[64,256]{1,0:T(8,128)S(1)} collective-permute-done((f32[64,256]{1,0:T(8,128)S(1)}, f32[64,256]{1,0:T(8,128)S(1)}, u32[]{:S(2)}, u32[]{:S(2)}) %collective-permute-start.7) | collective-permute-done | bytes 65568 | tf_op jit(solution)/shard_map/ppermute | solution.py:293
  20.2 0.0 collective-permute-done.8.refs_4_
  20.2 0.6 %shard_map.139 = (f32[32,256]{1,0:T(8,128)}, f32[32,256]{1,0:T(8,128)}, f32[1,256]{1,0:T(1,128)}) custom-call(f32[1,256]{1,0:T(1,128)S(1)} %get-tuple-element.37.refs_0_, f32[32,256]{1,0:T(8,128)S(1)} %get-tuple-element.38.refs_1_, f32[64,256]{1,0:T(8,128)S(1)} %shard_map.137.refs_2_, f32[64,256]{1,0:T(8,128)S(1)} %get-tuple-element.66.refs_3_, ...), custom_call_target="tpu_custom_call" | custom-call | tf_op jit(solution)/shard_map/pallas_call | solution.py:433
  (2 shorter events, 0.0 us)
Async XLA Ops:
  1.9 8.0 %collective-permute-start.5 = (bf16[32,256]{1,0:T(8,128)(2,1)S(1)}, bf16[32,256]{1,0:T(8,128)(2,1)S(1)}, u32[]{:S(2)}, u32[]{:S(2)}) collective-permute-start(bf16[32,256]{1,0:T(8,128)(2,1)S(1)} %get-tuple-element.41.refs_1_), channel_id=1, source_target_pairs={{0,1},{1,0},{2,3},{3,2},{4,5},{5,4},{6,7},{7,6},{8,9},{9,8},{10,11... | collective-permute-start | bytes 49160 | tf_op jit(solution)/shard_map/ppermute | solution.py:293
  2.4 7.4 %collective-permute-start = (bf16[32,256]{1,0:T(8,128)(2,1)S(1)}, bf16[32,256]{1,0:T(8,128)(2,1)S(1)}, u32[]{:S(2)}, u32[]{:S(2)}) collective-permute-start(bf16[32,256]{1,0:T(8,128)(2,1)S(1)} %get-tuple-element.41.refs_1_), channel_id=1, source_target_pairs={{0,2},{1,3},{2,0},{3,1},{4,6},{5,7},{6,4},{7,5},{8,10},{9,11},{10,... | collective-permute-start | bytes 49160 | tf_op jit(solution)/shard_map/ppermute | solution.py:293
  4.9 7.2 %collective-permute-start.2 = (bf16[96,256]{1,0:T(8,128)(2,1)S(1)}, bf16[96,256]{1,0:T(8,128)(2,1)S(1)}, u32[]{:S(2)}, u32[]{:S(2)}) collective-permute-start(bf16[96,256]{1,0:T(8,128)(2,1)S(1)} %get-tuple-element.46), channel_id=1, source_target_pairs={{0,12},{4,8},{8,4},{12,0},{1,13},{5,9},{9,5},{13,1},{2,14},{6,10},... | collective-permute-start | bytes 147464 | tf_op jit(solution)/shard_map/ppermute | solution.py:293
  8.5 5.0 %collective-permute-start.3 = (bf16[96,256]{1,0:T(8,128)(2,1)S(1)}, bf16[96,256]{1,0:T(8,128)(2,1)S(1)}, u32[]{:S(2)}, u32[]{:S(2)}) collective-permute-start(bf16[96,256]{1,0:T(8,128)(2,1)S(1)} %get-tuple-element.47), channel_id=1, source_target_pairs={{0,8},{4,12},{8,0},{12,4},{1,9},{5,13},{9,1},{13,5},{2,10},{6,14},... | collective-permute-start | bytes 147464 | tf_op jit(solution)/shard_map/ppermute | solution.py:293
  8.5 5.0 %collective-permute-start.4 = (bf16[96,256]{1,0:T(8,128)(2,1)S(1)}, bf16[96,256]{1,0:T(8,128)(2,1)S(1)}, u32[]{:S(2)}, u32[]{:S(2)}) collective-permute-start(bf16[96,256]{1,0:T(8,128)(2,1)S(1)} %get-tuple-element.48), channel_id=1, source_target_pairs={{0,4},{4,0},{8,12},{12,8},{1,5},{5,1},{9,13},{13,9},{2,6},{6,2},{1... | collective-permute-start | bytes 147464 | tf_op jit(solution)/shard_map/ppermute | solution.py:293
  9.8 1.2 %collective-permute-start.1 = (bf16[32,256]{1,0:T(8,128)(2,1)S(1)}, bf16[32,256]{1,0:T(8,128)(2,1)S(1)}, u32[]{:S(2)}, u32[]{:S(2)}) collective-permute-start(bf16[32,256]{1,0:T(8,128)(2,1)S(1)} %collective-permute-done.refs_1_), channel_id=1, source_target_pairs={{0,1},{1,0},{2,3},{3,2},{4,5},{5,4},{6,7},{7,6},{8,9},{9,8},{10,11... | collective-permute-start | bytes 49160 | tf_op jit(solution)/shard_map/ppermute | solution.py:293
  15.1 4.1 %collective-permute-start.6 = (f32[64,256]{1,0:T(8,128)S(1)}, f32[64,256]{1,0:T(8,128)S(1)}, u32[]{:S(2)}, u32[]{:S(2)}) collective-permute-start(f32[64,256]{1,0:T(8,128)S(1)} %get-tuple-element.62), channel_id=1, source_target_pairs={{0,3},{1,2},{2,1},{3,0},{4,7},{5,6},{6,5},{7,4},{8,11},{9,10},{10,... | collective-permute-start | bytes 196616 | tf_op jit(solution)/shard_map/ppermute | solution.py:293
  15.2 5.0 %collective-permute-start.7 = (f32[64,256]{1,0:T(8,128)S(1)}, f32[64,256]{1,0:T(8,128)S(1)}, u32[]{:S(2)}, u32[]{:S(2)}) collective-permute-start(f32[64,256]{1,0:T(8,128)S(1)} %get-tuple-element.63), channel_id=1, source_target_pairs={{0,2},{1,3},{2,0},{3,1},{4,6},{5,7},{6,4},{7,5},{8,10},{9,11},{10,... | collective-permute-start | bytes 196616 | tf_op jit(solution)/shard_map/ppermute | solution.py:293
  17.6 2.5 %collective-permute-start.8 = (f32[64,256]{1,0:T(8,128)S(1)}, f32[64,256]{1,0:T(8,128)S(1)}, u32[]{:S(2)}, u32[]{:S(2)}) collective-permute-start(f32[64,256]{1,0:T(8,128)S(1)} %get-tuple-element.67), channel_id=1, source_target_pairs={{0,1},{1,0},{2,3},{3,2},{4,5},{5,4},{6,7},{7,6},{8,9},{9,8},{10,11... | collective-permute-start | bytes 196616 | tf_op jit(solution)/shard_map/ppermute | solution.py:293

commit v5 on v4

--- a/solution.py
+++ b/solution.py
@@ -157,13 +157,10 @@
     sources = take(ns)
     begin, out = take(count), take(count)
     facing, back, fwd_tile, adj_tile = take(2), take(2), take(2), take(2)
-    total, stack, geo, scale_q = refs
+    stack, geo, scale_q = refs
     own = out[0].shape[1]
     cases = out[0].shape[0] // 2
     per = own // BLK
-    for t in range(count):
-        total[t] = begin[t][...]
-
     def match(slot, source):
         slab = source[2 * cases : 2 * cases + SLAB, :]
         right = jnp.concatenate([slab, slab, slab, jnp.ones_like(slab)], axis=0)
@@ -218,11 +215,13 @@
                         woven[done]()
                         done += 1
 
-    def collect(slot, source):
+    def collect(slot, source, onto):
         def piece(t, which):
             lines = slice(cases, 2 * cases) if which else slice(0, cases)
             tile = (adj_tile if which else fwd_tile)[slot][t * own : (t + 1) * own, :]
-            total[t, lines, :] += lax.dot_general(source[lines, :], tile, NT, preferred_element_type=jnp.float32)
+            out[t][lines, :] = onto[t][lines, :] + lax.dot_general(
+                source[lines, :], tile, NT, preferred_element_type=jnp.float32
+            )
 
         return [functools.partial(piece, t, which) for t in range(count) for which in (0, 1)]
 
@@ -237,27 +236,26 @@
                 measure((number + 1) % 2, sources[number + 1])
                 late = late + match((number + 1) % 2, sources[number + 1])
             build(k, number % 2, late)
-            late = collect(number % 2, sources[number])
+            late = collect(number % 2, sources[number], out if number else begin)
         for piece in late:
             piece()
     else:
         for i in range(ns):
             stack[i] = sources[i][...]
+        for t in range(count):
+            out[t][...] = begin[t][...]
 
         def step(i, _):
             source = stack.at[i]
             measure(0, source)
             for piece in match(0, source):
                 piece()
-            build(numbers[0] + i * (numbers[1] - numbers[0]), 0)
-            for piece in collect(0, source):
+            build(lax.rem(numbers[0] - 1 + i, ns) + 1, 0)
+            for piece in collect(0, source, out):
                 piece()
             return 0
 
         lax.fori_loop(0, ns, step, 0)
-    for t in range(count):
-        out[t][...] = total[t]
-
 
 def join_kernel(*refs):
     total = refs[0][...]
@@ -394,7 +392,6 @@
                 scratch_shapes=[
                     *[pltpu.VMEM((count * own, own), f32)] * 4,
                     *[pltpu.VMEM((count * own, own), jnp.bfloat16)] * 4,
-                    pltpu.VMEM((count, 2 * cases, own), f32),
                     pltpu.VMEM((ns if ns > 4 else 1, rows, own), jnp.bfloat16),
                     pltpu.VMEM((2, 8, own), f32),
                     pltpu.VMEM((2, blocks, own), f32),
@@ -411,7 +408,7 @@
         )
 
     shapes = prepare(targets[:2]) + prepare(targets[2:])
-    rest = tuple(range(nz - 1, 0, -1))
+    rest = tuple(range(nz // 2, nz)) + tuple(range(1, nz // 2))
     begun = []
     for first in range(0, nr, 2):
         begun += add((first, first + 1), (0,), [zero if first else source, zero])

time: 21 us -> 21 us (level)
  starting transfers between devices: 9.47 us -> 9.25 us
    ppermute x9, starting transfers between devices: 9.47 us -> 9.25 us  [swap(): lax.ppermute(x, axis, [(i, i ^ other) for i in range(lax.axis_size(axis))])]
  transfers between devices with their start and end apart: 9 -> 9, of which waited for: 3 -> 3; matrix products, arithmetic and copies ran while one was open for 0% -> 0% of each run, Pallas kernels for 21% -> 20%
where the time goes in v5:
time: 21 us; the launch traced here: 20.8 us
  starting transfers between devices  9.25 us (44%)
  Pallas kernels  7.69 us (37%)
  waiting for transfers between devices  3.1 us (15%)
  between operations  0.72 us (3%)
    ppermute x9, starting transfers between devices, swap(): lax.ppermute(x, axis, [(i, i ^ other) for i in range(lax.axis_size(axis))])  9.25 us
    pallas_call x4, Pallas kernels, add(): pl.pallas_call(functools.partial(sum_kernel, slots=slots, blocks=blocks,...  4.6 us
    ppermute x9, waiting for transfers between devices, swap(): lax.ppermute(x, axis, [(i, i ^ other) for i in range(lax.axis_size(axis))])  3.1 us
    pallas_call x1, Pallas kernels, local(): pl.pallas_call(functools.partial(pack_kernel, nr=nr, nz=nz, held=len(give...  1.21 us
    pallas_call x2, Pallas kernels, prepare(): pl.pallas_call(functools.partial(prepare_kernel, count=count), out_shape=...  0.77 us
    pallas_call x1, Pallas kernels, local(): pl.pallas_call(functools.partial(finish_kernel, nr=len(pieces)), out_shap...  0.64 us
    pallas_call x1, Pallas kernels, local(): pl.pallas_call(source_kernel, out_shape=jax.ShapeDtypeStruct((2 * cases,...  0.45 us
  transfers between devices with their start and end apart: 9, of which 3 were waited for; matrix products, arithmetic and copies ran while one was open for 0% of the time, Pallas kernels for 20%

profile of v5, /device:TPU:0, one launch (start us, length us, event | category | flops | bytes accessed | tf_op | source)
XLA Modules:
  0.0 20.8 jit_solution(11517173233297195386)
XLA Ops:
  0.6 1.2 %shard_map.130 = (bf16[32,256]{1,0:T(8,128)(2,1)S(1)}, bf16[96,256]{1,0:T(8,128)(2,1)S(1)}, bf16[96,256]{1,0:T(8,128)(2,1)S(1)}, bf16[96,256]{1,0:T(8,128)(2,1)S...) custom-call(s32[8,32]{1,0:T(8,128)} %refs_0_.1, ...), custom_call_target="tpu_custom_call" | custom-call | tf_op jit(solution)/shard_map/pallas_call | solution.py:332
  1.9 0.5 %collective-permute-start.5 = (bf16[32,256]{1,0:T(8,128)(2,1)S(1)}, bf16[32,256]{1,0:T(8,128)(2,1)S(1)}, u32[]{:S(2)}, u32[]{:S(2)}) collective-permute-start(bf16[32,256]{1,0:T(8,128)(2,1)S(1)} %get-tuple-element.41.refs_1_), channel_id=1, source_target_pairs={{0,1},{1,0},{2,3},{3,2},{4,5},{5,4},{6,7},{7,6},{8,9},{9,8},{10,11... | collective-permute-start | bytes 49160 | tf_op jit(solution)/shard_map/ppermute | solution.py:291
  2.4 2.6 %collective-permute-start = (bf16[32,256]{1,0:T(8,128)(2,1)S(1)}, bf16[32,256]{1,0:T(8,128)(2,1)S(1)}, u32[]{:S(2)}, u32[]{:S(2)}) collective-permute-start(bf16[32,256]{1,0:T(8,128)(2,1)S(1)} %get-tuple-element.41.refs_1_), channel_id=1, source_target_pairs={{0,2},{1,3},{2,0},{3,1},{4,6},{5,7},{6,4},{7,5},{8,10},{9,11},{10,... | collective-permute-start | bytes 49160 | tf_op jit(solution)/shard_map/ppermute | solution.py:291
  4.9 2.6 %collective-permute-start.2 = (bf16[96,256]{1,0:T(8,128)(2,1)S(1)}, bf16[96,256]{1,0:T(8,128)(2,1)S(1)}, u32[]{:S(2)}, u32[]{:S(2)}) collective-permute-start(bf16[96,256]{1,0:T(8,128)(2,1)S(1)} %get-tuple-element.46), channel_id=1, source_target_pairs={{0,8},{4,12},{8,0},{12,4},{1,9},{5,13},{9,1},{13,5},{2,10},{6,14},... | collective-permute-start | bytes 147464 | tf_op jit(solution)/shard_map/ppermute | solution.py:291
  7.5 1.3 %collective-permute-start.3 = (bf16[96,256]{1,0:T(8,128)(2,1)S(1)}, bf16[96,256]{1,0:T(8,128)(2,1)S(1)}, u32[]{:S(2)}, u32[]{:S(2)}) collective-permute-start(bf16[96,256]{1,0:T(8,128)(2,1)S(1)} %get-tuple-element.47), channel_id=1, source_target_pairs={{0,12},{4,8},{8,4},{12,0},{1,13},{5,9},{9,5},{13,1},{2,14},{6,10},... | collective-permute-start | bytes 147464 | tf_op jit(solution)/shard_map/ppermute | solution.py:291
  8.9 0.2 %collective-permute-start.4 = (bf16[96,256]{1,0:T(8,128)(2,1)S(1)}, bf16[96,256]{1,0:T(8,128)(2,1)S(1)}, u32[]{:S(2)}, u32[]{:S(2)}) collective-permute-start(bf16[96,256]{1,0:T(8,128)(2,1)S(1)} %get-tuple-element.48), channel_id=1, source_target_pairs={{0,4},{4,0},{8,12},{12,8},{1,5},{5,1},{9,13},{13,9},{2,6},{6,2},{1... | collective-permute-start | bytes 147464 | tf_op jit(solution)/shard_map/ppermute | solution.py:291
  9.1 0.5 %shard_map.135.refs_6_ = f32[64,256]{1,0:T(8,128)S(1)} custom-call(s32[1,2048]{1,0:T(1,128)S(1)} %get-tuple-element.58.ids, f32[32,2048]{1,0:T(8,128)S(1)} %get-tuple-element.59.weights), custom_call_target="tpu_custom_call" | custom-call | flops 550000000 | tf_op jit(solution)/shard_map/pallas_call | solution.py:358
  9.6 0.0 collective-permute-done.refs_1_
  9.6 0.1 collective-permute-start.1
  9.7 0.0 collective-permute-done.5.refs_2_
  9.7 0.4 %shard_map.134 = (bf16[256,256]{1,0:T(8,128)(2,1)S(1)}, bf16[256,256]{1,0:T(8,128)(2,1)S(1)}, f32[256,512]{1,0:T(8,128)S(1)}, f32[256,512]{1,0:T(8,128)S(1)}) custom-call(bf16[32,768]{1,0:T(8,128)(2,1)S(1)} %get-tuple-element.40.refs_0_, bf16[32,256]{1,0:T(8,128)(2,1)S(1)} %get-tuple-element.41.refs_1_, bf16[32,256]{1,0:T(8,128)(2,1)S(1)} %collective-permute-done.5.refs_2_), custom_call_target="tpu_custom_call" | custom-call | flops 440000000 | tf_op jit(solution)/shard_map/pallas_call | solution.py:374
  10.1 0.7 %shard_map.136 = (f32[64,256]{1,0:T(8,128)S(1)}, f32[64,256]{1,0:T(8,128)S(1)}) custom-call(f32[32,256]{1,0:T(8,128)S(1)} %get-tuple-element.39.refs_0_, bf16[256,256]{1,0:T(8,128)(2,1)S(1)} %get-tuple-element.54.refs_1_, bf16[256,256]{1,0:T(8,128)(2,1)S(1)} %get-tuple-element.55.refs_2_, f32[256,512]{1,0:T(8,128)S(1)} %get-tuple-element.56.refs_3_, ...), custom_call_target="tpu_custom_call" | custom-call | flops 660000000 | tf_op jit(solution)/shard_map/pallas_call | solution.py:387
  10.8 0.0 collective-permute-done.1.refs_2_
  10.8 0.4 %shard_map.131 = (bf16[256,256]{1,0:T(8,128)(2,1)S(1)}, bf16[256,256]{1,0:T(8,128)(2,1)S(1)}, f32[256,512]{1,0:T(8,128)S(1)}, f32[256,512]{1,0:T(8,128)S(1)}) custom-call(bf16[32,768]{1,0:T(8,128)(2,1)S(1)} %get-tuple-element.40.refs_0_, bf16[32,256]{1,0:T(8,128)(2,1)S(1)} %collective-permute-done.refs_1_, bf16[32,256]{1,0:T(8,128)(2,1)S(1)} %collective-permute-done.1.refs_2_), custom_call_target="tpu_custom_call" | custom-call | flops 440000000 | tf_op jit(solution)/shard_map/pallas_call | solution.py:374
  11.2 0.7 %shard_map.132 = (f32[64,256]{1,0:T(8,128)S(1)}, f32[64,256]{1,0:T(8,128)S(1)}) custom-call(f32[32,256]{1,0:T(8,128)S(1)} %get-tuple-element.39.refs_0_, bf16[256,256]{1,0:T(8,128)(2,1)S(1)} %get-tuple-element.42.refs_1_, bf16[256,256]{1,0:T(8,128)(2,1)S(1)} %get-tuple-element.43.refs_2_, f32[256,512]{1,0:T(8,128)S(1)} %get-tuple-element.44.refs_3_, ...), custom_call_target="tpu_custom_call" | custom-call | flops 660000000 | tf_op jit(solution)/shard_map/pallas_call | solution.py:387
  12.0 0.0 collective-permute-done.2.refs_5_
  12.0 1.5 %collective-permute-done.3.refs_6_ = bf16[96,256]{1,0:T(8,128)(2,1)S(1)} collective-permute-done((bf16[96,256]{1,0:T(8,128)(2,1)S(1)}, bf16[96,256]{1,0:T(8,128)(2,1)S(1)}, u32[]{:S(2)}, u32[]{:S(2)}) %collective-permute-start.3) | collective-permute-done | bytes 49184 | tf_op jit(solution)/shard_map/ppermute | solution.py:291
  13.5 0.0 collective-permute-done.4.refs_7_
  13.5 1.6 %shard_map.133 = (f32[64,256]{1,0:T(8,128)S(1)}, f32[64,256]{1,0:T(8,128)S(1)}) custom-call(f32[32,256]{1,0:T(8,128)S(1)} %get-tuple-element.39.refs_0_, bf16[256,256]{1,0:T(8,128)(2,1)S(1)} %get-tuple-element.42.refs_1_, bf16[256,256]{1,0:T(8,128)(2,1)S(1)} %get-tuple-element.43.refs_2_, f32[256,512]{1,0:T(8,128)S(1)} %get-tuple-element.44.refs_3_, ...), custom_call_target="tpu_custom_call" | custom-call | flops 1980000000 | tf_op jit(solution)/shard_map/pallas_call | solution.py:387
  15.1 0.0 collective-permute-start.6
  15.1 0.6 %collective-permute-start.7 = (f32[64,256]{1,0:T(8,128)S(1)}, f32[64,256]{1,0:T(8,128)S(1)}, u32[]{:S(2)}, u32[]{:S(2)}) collective-permute-start(f32[64,256]{1,0:T(8,128)S(1)} %get-tuple-element.63), channel_id=1, source_target_pairs={{0,2},{1,3},{2,0},{3,1},{4,6},{5,7},{6,4},{7,5},{8,10},{9,11},{10,... | collective-permute-start | bytes 196616 | tf_op jit(solution)/shard_map/ppermute | solution.py:291
  15.7 1.6 %shard_map.138 = (f32[64,256]{1,0:T(8,128)S(1)}, f32[64,256]{1,0:T(8,128)S(1)}) custom-call(f32[32,256]{1,0:T(8,128)S(1)} %get-tuple-element.39.refs_0_, bf16[256,256]{1,0:T(8,128)(2,1)S(1)} %get-tuple-element.54.refs_1_, bf16[256,256]{1,0:T(8,128)(2,1)S(1)} %get-tuple-element.55.refs_2_, f32[256,512]{1,0:T(8,128)S(1)} %get-tuple-element.56.refs_3_, ...), custom_call_target="tpu_custom_call" | custom-call | flops 1980000000 | tf_op jit(solution)/shard_map/pallas_call | solution.py:387
  17.3 1.3 %collective-permute-start.8 = (f32[64,256]{1,0:T(8,128)S(1)}, f32[64,256]{1,0:T(8,128)S(1)}, u32[]{:S(2)}, u32[]{:S(2)}) collective-permute-start(f32[64,256]{1,0:T(8,128)S(1)} %get-tuple-element.67), channel_id=1, source_target_pairs={{0,1},{1,0},{2,3},{3,2},{4,5},{5,4},{6,7},{7,6},{8,9},{9,8},{10,11... | collective-permute-start | bytes 196616 | tf_op jit(solution)/shard_map/ppermute | solution.py:291
  18.6 0.3 %collective-permute-done.6.refs_0_ = f32[64,256]{1,0:T(8,128)S(1)} collective-permute-done((f32[64,256]{1,0:T(8,128)S(1)}, f32[64,256]{1,0:T(8,128)S(1)}, u32[]{:S(2)}, u32[]{:S(2)}) %collective-permute-start.6) | collective-permute-done | bytes 65568 | tf_op jit(solution)/shard_map/ppermute | solution.py:291
  18.9 1.2 %collective-permute-done.7.refs_1_ = f32[64,256]{1,0:T(8,128)S(1)} collective-permute-done((f32[64,256]{1,0:T(8,128)S(1)}, f32[64,256]{1,0:T(8,128)S(1)}, u32[]{:S(2)}, u32[]{:S(2)}) %collective-permute-start.7) | collective-permute-done | bytes 65568 | tf_op jit(solution)/shard_map/ppermute | solution.py:291
  20.1 0.0 collective-permute-done.8.refs_4_
  20.1 0.6 %shard_map.139 = (f32[32,256]{1,0:T(8,128)}, f32[32,256]{1,0:T(8,128)}, f32[1,256]{1,0:T(1,128)}) custom-call(f32[1,256]{1,0:T(1,128)S(1)} %get-tuple-element.37.refs_0_, f32[32,256]{1,0:T(8,128)S(1)} %get-tuple-element.38.refs_1_, f32[64,256]{1,0:T(8,128)S(1)} %shard_map.137.refs_2_, f32[64,256]{1,0:T(8,128)S(1)} %get-tuple-element.66.refs_3_, ...), custom_call_target="tpu_custom_call" | custom-call | tf_op jit(solution)/shard_map/pallas_call | solution.py:430
  (2 shorter events, 0.0 us)
Async XLA Ops:
  1.9 7.8 %collective-permute-start.5 = (bf16[32,256]{1,0:T(8,128)(2,1)S(1)}, bf16[32,256]{1,0:T(8,128)(2,1)S(1)}, u32[]{:S(2)}, u32[]{:S(2)}) collective-permute-start(bf16[32,256]{1,0:T(8,128)(2,1)S(1)} %get-tuple-element.41.refs_1_), channel_id=1, source_target_pairs={{0,1},{1,0},{2,3},{3,2},{4,5},{5,4},{6,7},{7,6},{8,9},{9,8},{10,11... | collective-permute-start | bytes 49160 | tf_op jit(solution)/shard_map/ppermute | solution.py:291
  2.4 7.2 %collective-permute-start = (bf16[32,256]{1,0:T(8,128)(2,1)S(1)}, bf16[32,256]{1,0:T(8,128)(2,1)S(1)}, u32[]{:S(2)}, u32[]{:S(2)}) collective-permute-start(bf16[32,256]{1,0:T(8,128)(2,1)S(1)} %get-tuple-element.41.refs_1_), channel_id=1, source_target_pairs={{0,2},{1,3},{2,0},{3,1},{4,6},{5,7},{6,4},{7,5},{8,10},{9,11},{10,... | collective-permute-start | bytes 49160 | tf_op jit(solution)/shard_map/ppermute | solution.py:291
  4.9 7.0 %collective-permute-start.2 = (bf16[96,256]{1,0:T(8,128)(2,1)S(1)}, bf16[96,256]{1,0:T(8,128)(2,1)S(1)}, u32[]{:S(2)}, u32[]{:S(2)}) collective-permute-start(bf16[96,256]{1,0:T(8,128)(2,1)S(1)} %get-tuple-element.46), channel_id=1, source_target_pairs={{0,8},{4,12},{8,0},{12,4},{1,9},{5,13},{9,1},{13,5},{2,10},{6,14},... | collective-permute-start | bytes 147464 | tf_op jit(solution)/shard_map/ppermute | solution.py:291
  7.5 6.0 %collective-permute-start.3 = (bf16[96,256]{1,0:T(8,128)(2,1)S(1)}, bf16[96,256]{1,0:T(8,128)(2,1)S(1)}, u32[]{:S(2)}, u32[]{:S(2)}) collective-permute-start(bf16[96,256]{1,0:T(8,128)(2,1)S(1)} %get-tuple-element.47), channel_id=1, source_target_pairs={{0,12},{4,8},{8,4},{12,0},{1,13},{5,9},{9,5},{13,1},{2,14},{6,10},... | collective-permute-start | bytes 147464 | tf_op jit(solution)/shard_map/ppermute | solution.py:291
  8.9 4.6 %collective-permute-start.4 = (bf16[96,256]{1,0:T(8,128)(2,1)S(1)}, bf16[96,256]{1,0:T(8,128)(2,1)S(1)}, u32[]{:S(2)}, u32[]{:S(2)}) collective-permute-start(bf16[96,256]{1,0:T(8,128)(2,1)S(1)} %get-tuple-element.48), channel_id=1, source_target_pairs={{0,4},{4,0},{8,12},{12,8},{1,5},{5,1},{9,13},{13,9},{2,6},{6,2},{1... | collective-permute-start | bytes 147464 | tf_op jit(solution)/shard_map/ppermute | solution.py:291
  9.6 1.2 %collective-permute-start.1 = (bf16[32,256]{1,0:T(8,128)(2,1)S(1)}, bf16[32,256]{1,0:T(8,128)(2,1)S(1)}, u32[]{:S(2)}, u32[]{:S(2)}) collective-permute-start(bf16[32,256]{1,0:T(8,128)(2,1)S(1)} %collective-permute-done.refs_1_), channel_id=1, source_target_pairs={{0,1},{1,0},{2,3},{3,2},{4,5},{5,4},{6,7},{7,6},{8,9},{9,8},{10,11... | collective-permute-start | bytes 49160 | tf_op jit(solution)/shard_map/ppermute | solution.py:291
  15.1 3.8 %collective-permute-start.6 = (f32[64,256]{1,0:T(8,128)S(1)}, f32[64,256]{1,0:T(8,128)S(1)}, u32[]{:S(2)}, u32[]{:S(2)}) collective-permute-start(f32[64,256]{1,0:T(8,128)S(1)} %get-tuple-element.62), channel_id=1, source_target_pairs={{0,3},{1,2},{2,1},{3,0},{4,7},{5,6},{6,5},{7,4},{8,11},{9,10},{10,... | collective-permute-start | bytes 196616 | tf_op jit(solution)/shard_map/ppermute | solution.py:291
  15.1 5.0 %collective-permute-start.7 = (f32[64,256]{1,0:T(8,128)S(1)}, f32[64,256]{1,0:T(8,128)S(1)}, u32[]{:S(2)}, u32[]{:S(2)}) collective-permute-start(f32[64,256]{1,0:T(8,128)S(1)} %get-tuple-element.63), channel_id=1, source_target_pairs={{0,2},{1,3},{2,0},{3,1},{4,6},{5,7},{6,4},{7,5},{8,10},{9,11},{10,... | collective-permute-start | bytes 196616 | tf_op jit(solution)/shard_map/ppermute | solution.py:291
  17.3 2.8 %collective-permute-start.8 = (f32[64,256]{1,0:T(8,128)S(1)}, f32[64,256]{1,0:T(8,128)S(1)}, u32[]{:S(2)}, u32[]{:S(2)}) collective-permute-start(f32[64,256]{1,0:T(8,128)S(1)} %get-tuple-element.67), channel_id=1, source_target_pairs={{0,1},{1,0},{2,3},{3,2},{4,5},{5,4},{6,7},{7,6},{8,9},{9,8},{10,11... | collective-permute-start | bytes 196616 | tf_op jit(solution)/shard_map/ppermute | solution.py:291

commit v6 on v5

--- a/solution.py
+++ b/solution.py
@@ -11,6 +11,7 @@
 
 BLK = 128
 GEO = 24
+WORD = 20
 SLAB = 32
 FEAT = 128
 ROWS = 32
@@ -80,20 +81,28 @@
         geo[0, 9 + 3 * number : 12 + 3 * number, :] = b
         geo[0, 18 + number : 19 + number, :] = c
         geo[0, 21 + number : 22 + number, :] = d
+    third = geo[0, WORD : WORD + 1, :]
     sight.wait()
     for k in range(nz):
+        words = [[0.0] * per for _ in range(geo.shape[1] - GEO + 1)]
         for s in range(nr):
             for ib in range(per):
-                row = GEO + s * per + ib
+                block = s * per + ib
                 col = ((me_z ^ k) * nr + (me_r ^ s)) * per + ib
                 spot = (k * nr + s) * per + ib
                 for jb in range(per):
                     lanes = slice(jb * BLK, (jb + 1) * BLK)
-                    sees = seen[me_r * per + jb, col].astype(jnp.float32)
-                    geo[k, row : row + 1, lanes] = jnp.full((1, BLK), sees, jnp.float32)
+                    bit = seen[me_r * per + jb, col].astype(jnp.float32) * float(1 << block % 8)
+                    words[block // 8][jb] = words[block // 8][jb] + bit
                     other = seen[(me_r ^ s) * per + ib, ((me_z ^ k) * nr + me_r) * per + jb]
                     sees = other.astype(jnp.float32) * (1.0 / math.pi)
                     mask_ref[spot : spot + 1, lanes] = jnp.full((1, BLK), sees, jnp.float32)
+        for number in range(-(-nr * per // 8)):
+            row = WORD if nr * per <= 8 else GEO + number
+            for jb in range(per):
+                geo[k, row : row + 1, jb * BLK : (jb + 1) * BLK] = jnp.full((1, BLK), words[number][jb], jnp.float32)
+    word = geo[0, WORD : WORD + 1, :]
+    geo[0, WORD : WORD + 1, :] = third
     shared = geo[0, 0:GEO, :]
     one = jnp.ones((SLAB - GEO, own), jnp.float32)
     target_ref[...] = jnp.concatenate([shared, one], axis=0).astype(jnp.bfloat16)
@@ -104,7 +113,13 @@
     for k in range(nz):
         sources[k][0:cases, :] = value
         sources[k][cases : 2 * cases, :] = weighted
-        sources[k][2 * cases :, :] = jnp.concatenate([shared, geo[k, GEO:, :]], axis=0).astype(jnp.bfloat16)
+        slab = shared
+        if nr * per <= 8:
+            line = lax.broadcasted_iota(jnp.int32, shared.shape, 0)
+            slab = jnp.where(line == WORD, geo[k, WORD : WORD + 1, :] if k else word, shared)
+        else:
+            slab = jnp.concatenate([shared, geo[k, GEO:, :]], axis=0)
+        sources[k][2 * cases :, :] = slab.astype(jnp.bfloat16)
     for copy in copies[6:]:
         copy.wait()
 
@@ -157,12 +172,12 @@
     sources = take(ns)
     begin, out = take(count), take(count)
     facing, back, fwd_tile, adj_tile = take(2), take(2), take(2), take(2)
-    stack, geo, scale_q = refs
+    stack, geo, slabs, scale_q = refs
     own = out[0].shape[1]
     cases = out[0].shape[0] // 2
     per = own // BLK
     def match(slot, source):
-        slab = source[2 * cases : 2 * cases + SLAB, :]
+        slab = slabs[slot, :, :].astype(jnp.bfloat16)
         right = jnp.concatenate([slab, slab, slab, jnp.ones_like(slab)], axis=0)
 
         def piece(t, which):
@@ -178,7 +193,18 @@
         geo[slot, 0:3, :] = exact[0:3] + exact[3:6] + exact[6:9]
         area_q = exact[21:22] + exact[22:23] + exact[23:24]
         geo[slot, 3:4, :] = area_q
-        scale_q[slot] = exact[GEO:] * (area_q * (1.0 / math.pi))
+        flow = (exact[9:12] + exact[12:15] + exact[15:18]) * geo[slot, 0:3, :]
+        offset = -(flow[0:1] + flow[1:2] + flow[2:3])
+        slabs[slot, 0:GEO, :] = exact[0:GEO]
+        slabs[slot, GEO:, :] = jnp.zeros((SLAB - GEO, own), jnp.float32)
+        slabs[slot, WORD : WORD + 1, :] = offset - exact[18:19] - exact[19:20]
+        scaled = area_q * (1.0 / math.pi)
+        for number in range(-(-blocks // 8)):
+            row = WORD if blocks <= 8 else GEO + number
+            bits = min(8, blocks - 8 * number)
+            power = jnp.exp2(-lax.broadcasted_iota(jnp.int32, (bits, own), 0).astype(jnp.float32))
+            half = jnp.floor((exact[row : row + 1] + 0.5) * power)
+            scale_q[slot, 8 * number : 8 * number + bits, :] = (half - 2.0 * jnp.floor(half * 0.5)) * scaled
 
     def build(k, slot, woven=()):
         spots, spot = count * own // ROWS, 0
@@ -314,7 +340,8 @@
     small = pltpu.CompilerParams(vmem_limit_bytes=4 << 20)
     f32 = jnp.float32
     blocks = nr * per
-    rows = 2 * cases + GEO + blocks
+    extra = 0 if blocks <= 8 else -(-blocks // 64) * 8
+    rows = 2 * cases + GEO + extra
     given = (
         positions,
         angles,
@@ -343,7 +370,7 @@
             pltpu.VMEM((1, own), f32),
             pltpu.VMEM((cases, own), f32),
             pltpu.VMEM((cases, own), f32),
-            pltpu.VMEM((nz, GEO + blocks, own), f32),
+            pltpu.VMEM((nz, GEO + extra, own), f32),
             pltpu.SMEM(visibility.shape, jnp.int32),
             pltpu.SemaphoreType.DMA((len(given),)),
             pltpu.SemaphoreType.DMA,
@@ -394,6 +421,7 @@
                     *[pltpu.VMEM((count * own, own), jnp.bfloat16)] * 4,
                     pltpu.VMEM((ns if ns > 4 else 1, rows, own), jnp.bfloat16),
                     pltpu.VMEM((2, 8, own), f32),
+                    pltpu.VMEM((2, SLAB, own), f32),
                     pltpu.VMEM((2, blocks, own), f32),
                 ],
                 compiler_params=pltpu.CompilerParams(vmem_limit_bytes=12 << 20),

time: 21 us -> 20.9 us (level)
  transfers between devices with their start and end apart: 9 -> 9, of which waited for: 3 -> 3; matrix products, arithmetic and copies ran while one was open for 0% -> 0% of each run, Pallas kernels for 20% -> 21%
where the time goes in v6:
time: 20.9 us; the launch traced here: 20.8 us
  starting transfers between devices  9.24 us (44%)
  Pallas kernels  7.84 us (38%)
  waiting for transfers between devices  2.94 us (14%)
  between operations  0.73 us (3%)
    ppermute x9, starting transfers between devices, swap(): lax.ppermute(x, axis, [(i, i ^ other) for i in range(lax.axis_size(axis))])  9.24 us
    pallas_call x4, Pallas kernels, add(): pl.pallas_call(functools.partial(sum_kernel, slots=slots, blocks=blocks,...  4.7 us
    ppermute x9, waiting for transfers between devices, swap(): lax.ppermute(x, axis, [(i, i ^ other) for i in range(lax.axis_size(axis))])  2.94 us
    pallas_call x1, Pallas kernels, local(): pl.pallas_call(functools.partial(pack_kernel, nr=nr, nz=nz, held=len(give...  1.26 us
    pallas_call x2, Pallas kernels, prepare(): pl.pallas_call(functools.partial(prepare_kernel, count=count), out_shape=...  0.78 us
    pallas_call x1, Pallas kernels, local(): pl.pallas_call(functools.partial(finish_kernel, nr=len(pieces)), out_shap...  0.64 us
    pallas_call x1, Pallas kernels, local(): pl.pallas_call(source_kernel, out_shape=jax.ShapeDtypeStruct((2 * cases,...  0.45 us
  transfers between devices with their start and end apart: 9, of which 3 were waited for; matrix products, arithmetic and copies ran while one was open for 0% of the time, Pallas kernels for 21%

profile of v6, /device:TPU:0, one launch (start us, length us, event | category | flops | bytes accessed | tf_op | source)
XLA Modules:
  0.0 20.8 jit_solution(6720023530577274088)
XLA Ops:
  0.6 1.3 %shard_map.130 = (bf16[32,256]{1,0:T(8,128)(2,1)S(1)}, bf16[88,256]{1,0:T(8,128)(2,1)S(1)}, bf16[88,256]{1,0:T(8,128)(2,1)S(1)}, bf16[88,256]{1,0:T(8,128)(2,1)S...) custom-call(s32[8,32]{1,0:T(8,128)} %refs_0_.1, ...), custom_call_target="tpu_custom_call" | custom-call | tf_op jit(solution)/shard_map/pallas_call | solution.py:359
  1.9 0.5 %collective-permute-start.5 = (bf16[32,256]{1,0:T(8,128)(2,1)S(1)}, bf16[32,256]{1,0:T(8,128)(2,1)S(1)}, u32[]{:S(2)}, u32[]{:S(2)}) collective-permute-start(bf16[32,256]{1,0:T(8,128)(2,1)S(1)} %get-tuple-element.41.refs_1_), channel_id=1, source_target_pairs={{0,1},{1,0},{2,3},{3,2},{4,5},{5,4},{6,7},{7,6},{8,9},{9,8},{10,11... | collective-permute-start | bytes 49160 | tf_op jit(solution)/shard_map/ppermute | solution.py:317
  2.4 2.6 %collective-permute-start = (bf16[32,256]{1,0:T(8,128)(2,1)S(1)}, bf16[32,256]{1,0:T(8,128)(2,1)S(1)}, u32[]{:S(2)}, u32[]{:S(2)}) collective-permute-start(bf16[32,256]{1,0:T(8,128)(2,1)S(1)} %get-tuple-element.41.refs_1_), channel_id=1, source_target_pairs={{0,2},{1,3},{2,0},{3,1},{4,6},{5,7},{6,4},{7,5},{8,10},{9,11},{10,... | collective-permute-start | bytes 49160 | tf_op jit(solution)/shard_map/ppermute | solution.py:317
  5.0 2.6 %collective-permute-start.2 = (bf16[88,256]{1,0:T(8,128)(2,1)S(1)}, bf16[88,256]{1,0:T(8,128)(2,1)S(1)}, u32[]{:S(2)}, u32[]{:S(2)}) collective-permute-start(bf16[88,256]{1,0:T(8,128)(2,1)S(1)} %get-tuple-element.46), channel_id=1, source_target_pairs={{0,8},{4,12},{8,0},{12,4},{1,9},{5,13},{9,1},{13,5},{2,10},{6,14},... | collective-permute-start | bytes 135176 | tf_op jit(solution)/shard_map/ppermute | solution.py:317
  7.6 1.3 %collective-permute-start.3 = (bf16[88,256]{1,0:T(8,128)(2,1)S(1)}, bf16[88,256]{1,0:T(8,128)(2,1)S(1)}, u32[]{:S(2)}, u32[]{:S(2)}) collective-permute-start(bf16[88,256]{1,0:T(8,128)(2,1)S(1)} %get-tuple-element.47), channel_id=1, source_target_pairs={{0,12},{4,8},{8,4},{12,0},{1,13},{5,9},{9,5},{13,1},{2,14},{6,10},... | collective-permute-start | bytes 135176 | tf_op jit(solution)/shard_map/ppermute | solution.py:317
  8.9 0.2 %collective-permute-start.4 = (bf16[88,256]{1,0:T(8,128)(2,1)S(1)}, bf16[88,256]{1,0:T(8,128)(2,1)S(1)}, u32[]{:S(2)}, u32[]{:S(2)}) collective-permute-start(bf16[88,256]{1,0:T(8,128)(2,1)S(1)} %get-tuple-element.48), channel_id=1, source_target_pairs={{0,4},{4,0},{8,12},{12,8},{1,5},{5,1},{9,13},{13,9},{2,6},{6,2},{1... | collective-permute-start | bytes 135176 | tf_op jit(solution)/shard_map/ppermute | solution.py:317
  9.1 0.5 %shard_map.135.refs_6_ = f32[64,256]{1,0:T(8,128)S(1)} custom-call(s32[1,2048]{1,0:T(1,128)S(1)} %get-tuple-element.58.ids, f32[32,2048]{1,0:T(8,128)S(1)} %get-tuple-element.59.weights), custom_call_target="tpu_custom_call" | custom-call | flops 550000000 | tf_op jit(solution)/shard_map/pallas_call | solution.py:385
  9.6 0.0 collective-permute-done.refs_1_
  9.6 0.1 collective-permute-start.1
  9.7 0.0 collective-permute-done.5.refs_2_
  9.7 0.4 %shard_map.134 = (bf16[256,256]{1,0:T(8,128)(2,1)S(1)}, bf16[256,256]{1,0:T(8,128)(2,1)S(1)}, f32[256,512]{1,0:T(8,128)S(1)}, f32[256,512]{1,0:T(8,128)S(1)}) custom-call(bf16[32,768]{1,0:T(8,128)(2,1)S(1)} %get-tuple-element.40.refs_0_, bf16[32,256]{1,0:T(8,128)(2,1)S(1)} %get-tuple-element.41.refs_1_, bf16[32,256]{1,0:T(8,128)(2,1)S(1)} %collective-permute-done.5.refs_2_), custom_call_target="tpu_custom_call" | custom-call | flops 440000000 | tf_op jit(solution)/shard_map/pallas_call | solution.py:401
  10.1 0.7 %shard_map.136 = (f32[64,256]{1,0:T(8,128)S(1)}, f32[64,256]{1,0:T(8,128)S(1)}) custom-call(f32[32,256]{1,0:T(8,128)S(1)} %get-tuple-element.39.refs_0_, bf16[256,256]{1,0:T(8,128)(2,1)S(1)} %get-tuple-element.54.refs_1_, bf16[256,256]{1,0:T(8,128)(2,1)S(1)} %get-tuple-element.55.refs_2_, f32[256,512]{1,0:T(8,128)S(1)} %get-tuple-element.56.refs_3_, ...), custom_call_target="tpu_custom_call" | custom-call | flops 660000000 | tf_op jit(solution)/shard_map/pallas_call | solution.py:414
  10.9 0.0 collective-permute-done.1.refs_2_
  10.9 0.4 %shard_map.131 = (bf16[256,256]{1,0:T(8,128)(2,1)S(1)}, bf16[256,256]{1,0:T(8,128)(2,1)S(1)}, f32[256,512]{1,0:T(8,128)S(1)}, f32[256,512]{1,0:T(8,128)S(1)}) custom-call(bf16[32,768]{1,0:T(8,128)(2,1)S(1)} %get-tuple-element.40.refs_0_, bf16[32,256]{1,0:T(8,128)(2,1)S(1)} %collective-permute-done.refs_1_, bf16[32,256]{1,0:T(8,128)(2,1)S(1)} %collective-permute-done.1.refs_2_), custom_call_target="tpu_custom_call" | custom-call | flops 440000000 | tf_op jit(solution)/shard_map/pallas_call | solution.py:401
  11.3 0.7 %shard_map.132 = (f32[64,256]{1,0:T(8,128)S(1)}, f32[64,256]{1,0:T(8,128)S(1)}) custom-call(f32[32,256]{1,0:T(8,128)S(1)} %get-tuple-element.39.refs_0_, bf16[256,256]{1,0:T(8,128)(2,1)S(1)} %get-tuple-element.42.refs_1_, bf16[256,256]{1,0:T(8,128)(2,1)S(1)} %get-tuple-element.43.refs_2_, f32[256,512]{1,0:T(8,128)S(1)} %get-tuple-element.44.refs_3_, ...), custom_call_target="tpu_custom_call" | custom-call | flops 660000000 | tf_op jit(solution)/shard_map/pallas_call | solution.py:414
  12.0 0.0 collective-permute-done.2.refs_5_
  12.1 1.4 %collective-permute-done.3.refs_6_ = bf16[88,256]{1,0:T(8,128)(2,1)S(1)} collective-permute-done((bf16[88,256]{1,0:T(8,128)(2,1)S(1)}, bf16[88,256]{1,0:T(8,128)(2,1)S(1)}, u32[]{:S(2)}, u32[]{:S(2)}) %collective-permute-start.3) | collective-permute-done | bytes 45088 | tf_op jit(solution)/shard_map/ppermute | solution.py:317
  13.4 0.0 collective-permute-done.4.refs_7_
  13.5 1.6 %shard_map.133 = (f32[64,256]{1,0:T(8,128)S(1)}, f32[64,256]{1,0:T(8,128)S(1)}) custom-call(f32[32,256]{1,0:T(8,128)S(1)} %get-tuple-element.39.refs_0_, bf16[256,256]{1,0:T(8,128)(2,1)S(1)} %get-tuple-element.42.refs_1_, bf16[256,256]{1,0:T(8,128)(2,1)S(1)} %get-tuple-element.43.refs_2_, f32[256,512]{1,0:T(8,128)S(1)} %get-tuple-element.44.refs_3_, ...), custom_call_target="tpu_custom_call" | custom-call | flops 1980000000 | tf_op jit(solution)/shard_map/pallas_call | solution.py:414
  15.1 0.0 collective-permute-start.6
  15.1 0.7 %collective-permute-start.7 = (f32[64,256]{1,0:T(8,128)S(1)}, f32[64,256]{1,0:T(8,128)S(1)}, u32[]{:S(2)}, u32[]{:S(2)}) collective-permute-start(f32[64,256]{1,0:T(8,128)S(1)} %get-tuple-element.63), channel_id=1, source_target_pairs={{0,2},{1,3},{2,0},{3,1},{4,6},{5,7},{6,4},{7,5},{8,10},{9,11},{10,... | collective-permute-start | bytes 196616 | tf_op jit(solution)/shard_map/ppermute | solution.py:317
  15.8 1.6 %shard_map.138 = (f32[64,256]{1,0:T(8,128)S(1)}, f32[64,256]{1,0:T(8,128)S(1)}) custom-call(f32[32,256]{1,0:T(8,128)S(1)} %get-tuple-element.39.refs_0_, bf16[256,256]{1,0:T(8,128)(2,1)S(1)} %get-tuple-element.54.refs_1_, bf16[256,256]{1,0:T(8,128)(2,1)S(1)} %get-tuple-element.55.refs_2_, f32[256,512]{1,0:T(8,128)S(1)} %get-tuple-element.56.refs_3_, ...), custom_call_target="tpu_custom_call" | custom-call | flops 1980000000 | tf_op jit(solution)/shard_map/pallas_call | solution.py:414
  17.4 1.1 %collective-permute-start.8 = (f32[64,256]{1,0:T(8,128)S(1)}, f32[64,256]{1,0:T(8,128)S(1)}, u32[]{:S(2)}, u32[]{:S(2)}) collective-permute-start(f32[64,256]{1,0:T(8,128)S(1)} %get-tuple-element.67), channel_id=1, source_target_pairs={{0,1},{1,0},{2,3},{3,2},{4,5},{5,4},{6,7},{7,6},{8,9},{9,8},{10,11... | collective-permute-start | bytes 196616 | tf_op jit(solution)/shard_map/ppermute | solution.py:317
  18.6 0.3 %collective-permute-done.6.refs_0_ = f32[64,256]{1,0:T(8,128)S(1)} collective-permute-done((f32[64,256]{1,0:T(8,128)S(1)}, f32[64,256]{1,0:T(8,128)S(1)}, u32[]{:S(2)}, u32[]{:S(2)}) %collective-permute-start.6) | collective-permute-done | bytes 65568 | tf_op jit(solution)/shard_map/ppermute | solution.py:317
  18.9 1.2 %collective-permute-done.7.refs_1_ = f32[64,256]{1,0:T(8,128)S(1)} collective-permute-done((f32[64,256]{1,0:T(8,128)S(1)}, f32[64,256]{1,0:T(8,128)S(1)}, u32[]{:S(2)}, u32[]{:S(2)}) %collective-permute-start.7) | collective-permute-done | bytes 65568 | tf_op jit(solution)/shard_map/ppermute | solution.py:317
  20.1 0.0 collective-permute-done.8.refs_4_
  20.1 0.6 %shard_map.139 = (f32[32,256]{1,0:T(8,128)}, f32[32,256]{1,0:T(8,128)}, f32[1,256]{1,0:T(1,128)}) custom-call(f32[1,256]{1,0:T(1,128)S(1)} %get-tuple-element.37.refs_0_, f32[32,256]{1,0:T(8,128)S(1)} %get-tuple-element.38.refs_1_, f32[64,256]{1,0:T(8,128)S(1)} %shard_map.137.refs_2_, f32[64,256]{1,0:T(8,128)S(1)} %get-tuple-element.66.refs_3_, ...), custom_call_target="tpu_custom_call" | custom-call | tf_op jit(solution)/shard_map/pallas_call | solution.py:458
  (2 shorter events, 0.0 us)
Async XLA Ops:
  1.9 7.8 %collective-permute-start.5 = (bf16[32,256]{1,0:T(8,128)(2,1)S(1)}, bf16[32,256]{1,0:T(8,128)(2,1)S(1)}, u32[]{:S(2)}, u32[]{:S(2)}) collective-permute-start(bf16[32,256]{1,0:T(8,128)(2,1)S(1)} %get-tuple-element.41.refs_1_), channel_id=1, source_target_pairs={{0,1},{1,0},{2,3},{3,2},{4,5},{5,4},{6,7},{7,6},{8,9},{9,8},{10,11... | collective-permute-start | bytes 49160 | tf_op jit(solution)/shard_map/ppermute | solution.py:317
  2.4 7.2 %collective-permute-start = (bf16[32,256]{1,0:T(8,128)(2,1)S(1)}, bf16[32,256]{1,0:T(8,128)(2,1)S(1)}, u32[]{:S(2)}, u32[]{:S(2)}) collective-permute-start(bf16[32,256]{1,0:T(8,128)(2,1)S(1)} %get-tuple-element.41.refs_1_), channel_id=1, source_target_pairs={{0,2},{1,3},{2,0},{3,1},{4,6},{5,7},{6,4},{7,5},{8,10},{9,11},{10,... | collective-permute-start | bytes 49160 | tf_op jit(solution)/shard_map/ppermute | solution.py:317
  5.0 7.1 %collective-permute-start.2 = (bf16[88,256]{1,0:T(8,128)(2,1)S(1)}, bf16[88,256]{1,0:T(8,128)(2,1)S(1)}, u32[]{:S(2)}, u32[]{:S(2)}) collective-permute-start(bf16[88,256]{1,0:T(8,128)(2,1)S(1)} %get-tuple-element.46), channel_id=1, source_target_pairs={{0,8},{4,12},{8,0},{12,4},{1,9},{5,13},{9,1},{13,5},{2,10},{6,14},... | collective-permute-start | bytes 135176 | tf_op jit(solution)/shard_map/ppermute | solution.py:317
  7.6 5.9 %collective-permute-start.3 = (bf16[88,256]{1,0:T(8,128)(2,1)S(1)}, bf16[88,256]{1,0:T(8,128)(2,1)S(1)}, u32[]{:S(2)}, u32[]{:S(2)}) collective-permute-start(bf16[88,256]{1,0:T(8,128)(2,1)S(1)} %get-tuple-element.47), channel_id=1, source_target_pairs={{0,12},{4,8},{8,4},{12,0},{1,13},{5,9},{9,5},{13,1},{2,14},{6,10},... | collective-permute-start | bytes 135176 | tf_op jit(solution)/shard_map/ppermute | solution.py:317
  8.9 4.5 %collective-permute-start.4 = (bf16[88,256]{1,0:T(8,128)(2,1)S(1)}, bf16[88,256]{1,0:T(8,128)(2,1)S(1)}, u32[]{:S(2)}, u32[]{:S(2)}) collective-permute-start(bf16[88,256]{1,0:T(8,128)(2,1)S(1)} %get-tuple-element.48), channel_id=1, source_target_pairs={{0,4},{4,0},{8,12},{12,8},{1,5},{5,1},{9,13},{13,9},{2,6},{6,2},{1... | collective-permute-start | bytes 135176 | tf_op jit(solution)/shard_map/ppermute | solution.py:317
  9.6 1.3 %collective-permute-start.1 = (bf16[32,256]{1,0:T(8,128)(2,1)S(1)}, bf16[32,256]{1,0:T(8,128)(2,1)S(1)}, u32[]{:S(2)}, u32[]{:S(2)}) collective-permute-start(bf16[32,256]{1,0:T(8,128)(2,1)S(1)} %collective-permute-done.refs_1_), channel_id=1, source_target_pairs={{0,1},{1,0},{2,3},{3,2},{4,5},{5,4},{6,7},{7,6},{8,9},{9,8},{10,11... | collective-permute-start | bytes 49160 | tf_op jit(solution)/shard_map/ppermute | solution.py:317
  15.1 3.8 %collective-permute-start.6 = (f32[64,256]{1,0:T(8,128)S(1)}, f32[64,256]{1,0:T(8,128)S(1)}, u32[]{:S(2)}, u32[]{:S(2)}) collective-permute-start(f32[64,256]{1,0:T(8,128)S(1)} %get-tuple-element.62), channel_id=1, source_target_pairs={{0,3},{1,2},{2,1},{3,0},{4,7},{5,6},{6,5},{7,4},{8,11},{9,10},{10,... | collective-permute-start | bytes 196616 | tf_op jit(solution)/shard_map/ppermute | solution.py:317
  15.1 5.0 %collective-permute-start.7 = (f32[64,256]{1,0:T(8,128)S(1)}, f32[64,256]{1,0:T(8,128)S(1)}, u32[]{:S(2)}, u32[]{:S(2)}) collective-permute-start(f32[64,256]{1,0:T(8,128)S(1)} %get-tuple-element.63), channel_id=1, source_target_pairs={{0,2},{1,3},{2,0},{3,1},{4,6},{5,7},{6,4},{7,5},{8,10},{9,11},{10,... | collective-permute-start | bytes 196616 | tf_op jit(solution)/shard_map/ppermute | solution.py:317
  17.4 2.7 %collective-permute-start.8 = (f32[64,256]{1,0:T(8,128)S(1)}, f32[64,256]{1,0:T(8,128)S(1)}, u32[]{:S(2)}, u32[]{:S(2)}) collective-permute-start(f32[64,256]{1,0:T(8,128)S(1)} %get-tuple-element.67), channel_id=1, source_target_pairs={{0,1},{1,0},{2,3},{3,2},{4,5},{5,4},{6,7},{7,6},{8,9},{9,8},{10,11... | collective-permute-start | bytes 196616 | tf_op jit(solution)/shard_map/ppermute | solution.py:317

commit v7 on v6

--- a/solution.py
+++ b/solution.py
@@ -276,7 +276,7 @@
             measure(0, source)
             for piece in match(0, source):
                 piece()
-            build(lax.rem(numbers[0] - 1 + i, ns) + 1, 0)
+            build(numbers[0] - i, 0)
             for piece in collect(0, source, out):
                 piece()
             return 0
@@ -436,7 +436,7 @@
         )
 
     shapes = prepare(targets[:2]) + prepare(targets[2:])
-    rest = tuple(range(nz // 2, nz)) + tuple(range(1, nz // 2))
+    rest = tuple(range(nz - 1, 0, -1))
     begun = []
     for first in range(0, nr, 2):
         begun += add((first, first + 1), (0,), [zero if first else source, zero])

time: 20.9 us -> 21 us (level)
    ppermute x9, starting transfers between devices: 9.24 us -> 9.45 us  [swap(): lax.ppermute(x, axis, [(i, i ^ other) for i in range(lax.axis_size(axis))])]
where the time goes in v7:
time: 21 us; the launch traced here: 20.8 us
  starting transfers between devices  9.45 us (45%)
  Pallas kernels  7.85 us (37%)
  waiting for transfers between devices  2.8 us (13%)
  between operations  0.73 us (3%)
    ppermute x9, starting transfers between devices, swap(): lax.ppermute(x, axis, [(i, i ^ other) for i in range(lax.axis_size(axis))])  9.45 us
    pallas_call x4, Pallas kernels, add(): pl.pallas_call(functools.partial(sum_kernel, slots=slots, blocks=blocks,...  4.71 us
    ppermute x9, waiting for transfers between devices, swap(): lax.ppermute(x, axis, [(i, i ^ other) for i in range(lax.axis_size(axis))])  2.8 us
    pallas_call x1, Pallas kernels, local(): pl.pallas_call(functools.partial(pack_kernel, nr=nr, nz=nz, held=len(give...  1.26 us
    pallas_call x2, Pallas kernels, prepare(): pl.pallas_call(functools.partial(prepare_kernel, count=count), out_shape=...  0.78 us
    pallas_call x1, Pallas kernels, local(): pl.pallas_call(functools.partial(finish_kernel, nr=len(pieces)), out_shap...  0.64 us
    pallas_call x1, Pallas kernels, local(): pl.pallas_call(source_kernel, out_shape=jax.ShapeDtypeStruct((2 * cases,...  0.45 us
  transfers between devices with their start and end apart: 9, of which 3 were waited for; matrix products, arithmetic and copies ran while one was open for 0% of the time, Pallas kernels for 21%

profile of v7, /device:TPU:0, one launch (start us, length us, event | category | flops | bytes accessed | tf_op | source)
XLA Modules:
  0.0 20.8 jit_solution(6090752333143672464)
XLA Ops:
  0.6 1.3 %shard_map.130 = (bf16[32,256]{1,0:T(8,128)(2,1)S(1)}, bf16[88,256]{1,0:T(8,128)(2,1)S(1)}, bf16[88,256]{1,0:T(8,128)(2,1)S(1)}, bf16[88,256]{1,0:T(8,128)(2,1)S...) custom-call(s32[8,32]{1,0:T(8,128)} %refs_0_.1, ...), custom_call_target="tpu_custom_call" | custom-call | tf_op jit(solution)/shard_map/pallas_call | solution.py:359
  1.9 0.5 %collective-permute-start.5 = (bf16[32,256]{1,0:T(8,128)(2,1)S(1)}, bf16[32,256]{1,0:T(8,128)(2,1)S(1)}, u32[]{:S(2)}, u32[]{:S(2)}) collective-permute-start(bf16[32,256]{1,0:T(8,128)(2,1)S(1)} %get-tuple-element.41.refs_1_), channel_id=1, source_target_pairs={{0,1},{1,0},{2,3},{3,2},{4,5},{5,4},{6,7},{7,6},{8,9},{9,8},{10,11... | collective-permute-start | bytes 49160 | tf_op jit(solution)/shard_map/ppermute | solution.py:317
  2.4 2.6 %collective-permute-start = (bf16[32,256]{1,0:T(8,128)(2,1)S(1)}, bf16[32,256]{1,0:T(8,128)(2,1)S(1)}, u32[]{:S(2)}, u32[]{:S(2)}) collective-permute-start(bf16[32,256]{1,0:T(8,128)(2,1)S(1)} %get-tuple-element.41.refs_1_), channel_id=1, source_target_pairs={{0,2},{1,3},{2,0},{3,1},{4,6},{5,7},{6,4},{7,5},{8,10},{9,11},{10,... | collective-permute-start | bytes 49160 | tf_op jit(solution)/shard_map/ppermute | solution.py:317
  5.0 3.6 %collective-permute-start.2 = (bf16[88,256]{1,0:T(8,128)(2,1)S(1)}, bf16[88,256]{1,0:T(8,128)(2,1)S(1)}, u32[]{:S(2)}, u32[]{:S(2)}) collective-permute-start(bf16[88,256]{1,0:T(8,128)(2,1)S(1)} %get-tuple-element.46), channel_id=1, source_target_pairs={{0,12},{4,8},{8,4},{12,0},{1,13},{5,9},{9,5},{13,1},{2,14},{6,10},... | collective-permute-start | bytes 135176 | tf_op jit(solution)/shard_map/ppermute | solution.py:317
  8.6 0.0 collective-permute-start.3
  8.6 0.8 %collective-permute-start.4 = (bf16[88,256]{1,0:T(8,128)(2,1)S(1)}, bf16[88,256]{1,0:T(8,128)(2,1)S(1)}, u32[]{:S(2)}, u32[]{:S(2)}) collective-permute-start(bf16[88,256]{1,0:T(8,128)(2,1)S(1)} %get-tuple-element.48), channel_id=1, source_target_pairs={{0,4},{4,0},{8,12},{12,8},{1,5},{5,1},{9,13},{13,9},{2,6},{6,2},{1... | collective-permute-start | bytes 135176 | tf_op jit(solution)/shard_map/ppermute | solution.py:317
  9.4 0.5 %shard_map.135.refs_6_ = f32[64,256]{1,0:T(8,128)S(1)} custom-call(s32[1,2048]{1,0:T(1,128)S(1)} %get-tuple-element.58.ids, f32[32,2048]{1,0:T(8,128)S(1)} %get-tuple-element.59.weights), custom_call_target="tpu_custom_call" | custom-call | flops 550000000 | tf_op jit(solution)/shard_map/pallas_call | solution.py:385
  9.8 0.0 collective-permute-done.refs_1_
  9.9 0.1 collective-permute-start.1
  9.9 0.0 collective-permute-done.5.refs_2_
  9.9 0.4 %shard_map.134 = (bf16[256,256]{1,0:T(8,128)(2,1)S(1)}, bf16[256,256]{1,0:T(8,128)(2,1)S(1)}, f32[256,512]{1,0:T(8,128)S(1)}, f32[256,512]{1,0:T(8,128)S(1)}) custom-call(bf16[32,768]{1,0:T(8,128)(2,1)S(1)} %get-tuple-element.40.refs_0_, bf16[32,256]{1,0:T(8,128)(2,1)S(1)} %get-tuple-element.41.refs_1_, bf16[32,256]{1,0:T(8,128)(2,1)S(1)} %collective-permute-done.5.refs_2_), custom_call_target="tpu_custom_call" | custom-call | flops 440000000 | tf_op jit(solution)/shard_map/pallas_call | solution.py:401
  10.3 0.7 %shard_map.136 = (f32[64,256]{1,0:T(8,128)S(1)}, f32[64,256]{1,0:T(8,128)S(1)}) custom-call(f32[32,256]{1,0:T(8,128)S(1)} %get-tuple-element.39.refs_0_, bf16[256,256]{1,0:T(8,128)(2,1)S(1)} %get-tuple-element.54.refs_1_, bf16[256,256]{1,0:T(8,128)(2,1)S(1)} %get-tuple-element.55.refs_2_, f32[256,512]{1,0:T(8,128)S(1)} %get-tuple-element.56.refs_3_, ...), custom_call_target="tpu_custom_call" | custom-call | flops 660000000 | tf_op jit(solution)/shard_map/pallas_call | solution.py:414
  11.1 0.0 collective-permute-done.1.refs_2_
  11.1 0.4 %shard_map.131 = (bf16[256,256]{1,0:T(8,128)(2,1)S(1)}, bf16[256,256]{1,0:T(8,128)(2,1)S(1)}, f32[256,512]{1,0:T(8,128)S(1)}, f32[256,512]{1,0:T(8,128)S(1)}) custom-call(bf16[32,768]{1,0:T(8,128)(2,1)S(1)} %get-tuple-element.40.refs_0_, bf16[32,256]{1,0:T(8,128)(2,1)S(1)} %collective-permute-done.refs_1_, bf16[32,256]{1,0:T(8,128)(2,1)S(1)} %collective-permute-done.1.refs_2_), custom_call_target="tpu_custom_call" | custom-call | flops 440000000 | tf_op jit(solution)/shard_map/pallas_call | solution.py:401
  11.5 0.7 %shard_map.132 = (f32[64,256]{1,0:T(8,128)S(1)}, f32[64,256]{1,0:T(8,128)S(1)}) custom-call(f32[32,256]{1,0:T(8,128)S(1)} %get-tuple-element.39.refs_0_, bf16[256,256]{1,0:T(8,128)(2,1)S(1)} %get-tuple-element.42.refs_1_, bf16[256,256]{1,0:T(8,128)(2,1)S(1)} %get-tuple-element.43.refs_2_, f32[256,512]{1,0:T(8,128)S(1)} %get-tuple-element.44.refs_3_, ...), custom_call_target="tpu_custom_call" | custom-call | flops 660000000 | tf_op jit(solution)/shard_map/pallas_call | solution.py:414
  12.3 0.0 collective-permute-done.2.refs_5_
  12.3 1.3 %collective-permute-done.3.refs_6_ = bf16[88,256]{1,0:T(8,128)(2,1)S(1)} collective-permute-done((bf16[88,256]{1,0:T(8,128)(2,1)S(1)}, bf16[88,256]{1,0:T(8,128)(2,1)S(1)}, u32[]{:S(2)}, u32[]{:S(2)}) %collective-permute-start.3) | collective-permute-done | bytes 45088 | tf_op jit(solution)/shard_map/ppermute | solution.py:317
  13.5 0.0 collective-permute-done.4.refs_7_
  13.5 1.6 %shard_map.133 = (f32[64,256]{1,0:T(8,128)S(1)}, f32[64,256]{1,0:T(8,128)S(1)}) custom-call(f32[32,256]{1,0:T(8,128)S(1)} %get-tuple-element.39.refs_0_, bf16[256,256]{1,0:T(8,128)(2,1)S(1)} %get-tuple-element.42.refs_1_, bf16[256,256]{1,0:T(8,128)(2,1)S(1)} %get-tuple-element.43.refs_2_, f32[256,512]{1,0:T(8,128)S(1)} %get-tuple-element.44.refs_3_, ...), custom_call_target="tpu_custom_call" | custom-call | flops 1980000000 | tf_op jit(solution)/shard_map/pallas_call | solution.py:414
  15.1 0.0 collective-permute-start.6
  15.2 0.9 %collective-permute-start.7 = (f32[64,256]{1,0:T(8,128)S(1)}, f32[64,256]{1,0:T(8,128)S(1)}, u32[]{:S(2)}, u32[]{:S(2)}) collective-permute-start(f32[64,256]{1,0:T(8,128)S(1)} %get-tuple-element.63), channel_id=1, source_target_pairs={{0,2},{1,3},{2,0},{3,1},{4,6},{5,7},{6,4},{7,5},{8,10},{9,11},{10,... | collective-permute-start | bytes 196616 | tf_op jit(solution)/shard_map/ppermute | solution.py:317
  16.0 1.6 %shard_map.138 = (f32[64,256]{1,0:T(8,128)S(1)}, f32[64,256]{1,0:T(8,128)S(1)}) custom-call(f32[32,256]{1,0:T(8,128)S(1)} %get-tuple-element.39.refs_0_, bf16[256,256]{1,0:T(8,128)(2,1)S(1)} %get-tuple-element.54.refs_1_, bf16[256,256]{1,0:T(8,128)(2,1)S(1)} %get-tuple-element.55.refs_2_, f32[256,512]{1,0:T(8,128)S(1)} %get-tuple-element.56.refs_3_, ...), custom_call_target="tpu_custom_call" | custom-call | flops 1980000000 | tf_op jit(solution)/shard_map/pallas_call | solution.py:414
  17.7 1.0 %collective-permute-start.8 = (f32[64,256]{1,0:T(8,128)S(1)}, f32[64,256]{1,0:T(8,128)S(1)}, u32[]{:S(2)}, u32[]{:S(2)}) collective-permute-start(f32[64,256]{1,0:T(8,128)S(1)} %get-tuple-element.67), channel_id=1, source_target_pairs={{0,1},{1,0},{2,3},{3,2},{4,5},{5,4},{6,7},{7,6},{8,9},{9,8},{10,11... | collective-permute-start | bytes 196616 | tf_op jit(solution)/shard_map/ppermute | solution.py:317
  18.7 0.5 %collective-permute-done.6.refs_0_ = f32[64,256]{1,0:T(8,128)S(1)} collective-permute-done((f32[64,256]{1,0:T(8,128)S(1)}, f32[64,256]{1,0:T(8,128)S(1)}, u32[]{:S(2)}, u32[]{:S(2)}) %collective-permute-start.6) | collective-permute-done | bytes 65568 | tf_op jit(solution)/shard_map/ppermute | solution.py:317
  19.2 1.0 %collective-permute-done.7.refs_1_ = f32[64,256]{1,0:T(8,128)S(1)} collective-permute-done((f32[64,256]{1,0:T(8,128)S(1)}, f32[64,256]{1,0:T(8,128)S(1)}, u32[]{:S(2)}, u32[]{:S(2)}) %collective-permute-start.7) | collective-permute-done | bytes 65568 | tf_op jit(solution)/shard_map/ppermute | solution.py:317
  20.2 0.0 collective-permute-done.8.refs_4_
  20.2 0.6 %shard_map.139 = (f32[32,256]{1,0:T(8,128)}, f32[32,256]{1,0:T(8,128)}, f32[1,256]{1,0:T(1,128)}) custom-call(f32[1,256]{1,0:T(1,128)S(1)} %get-tuple-element.37.refs_0_, f32[32,256]{1,0:T(8,128)S(1)} %get-tuple-element.38.refs_1_, f32[64,256]{1,0:T(8,128)S(1)} %shard_map.137.refs_2_, f32[64,256]{1,0:T(8,128)S(1)} %get-tuple-element.66.refs_3_, ...), custom_call_target="tpu_custom_call" | custom-call | tf_op jit(solution)/shard_map/pallas_call | solution.py:458
  (2 shorter events, 0.0 us)
Async XLA Ops:
  1.9 8.0 %collective-permute-start.5 = (bf16[32,256]{1,0:T(8,128)(2,1)S(1)}, bf16[32,256]{1,0:T(8,128)(2,1)S(1)}, u32[]{:S(2)}, u32[]{:S(2)}) collective-permute-start(bf16[32,256]{1,0:T(8,128)(2,1)S(1)} %get-tuple-element.41.refs_1_), channel_id=1, source_target_pairs={{0,1},{1,0},{2,3},{3,2},{4,5},{5,4},{6,7},{7,6},{8,9},{9,8},{10,11... | collective-permute-start | bytes 49160 | tf_op jit(solution)/shard_map/ppermute | solution.py:317
  2.4 7.4 %collective-permute-start = (bf16[32,256]{1,0:T(8,128)(2,1)S(1)}, bf16[32,256]{1,0:T(8,128)(2,1)S(1)}, u32[]{:S(2)}, u32[]{:S(2)}) collective-permute-start(bf16[32,256]{1,0:T(8,128)(2,1)S(1)} %get-tuple-element.41.refs_1_), channel_id=1, source_target_pairs={{0,2},{1,3},{2,0},{3,1},{4,6},{5,7},{6,4},{7,5},{8,10},{9,11},{10,... | collective-permute-start | bytes 49160 | tf_op jit(solution)/shard_map/ppermute | solution.py:317
  5.0 7.3 %collective-permute-start.2 = (bf16[88,256]{1,0:T(8,128)(2,1)S(1)}, bf16[88,256]{1,0:T(8,128)(2,1)S(1)}, u32[]{:S(2)}, u32[]{:S(2)}) collective-permute-start(bf16[88,256]{1,0:T(8,128)(2,1)S(1)} %get-tuple-element.46), channel_id=1, source_target_pairs={{0,12},{4,8},{8,4},{12,0},{1,13},{5,9},{9,5},{13,1},{2,14},{6,10},... | collective-permute-start | bytes 135176 | tf_op jit(solution)/shard_map/ppermute | solution.py:317
  8.6 4.9 %collective-permute-start.3 = (bf16[88,256]{1,0:T(8,128)(2,1)S(1)}, bf16[88,256]{1,0:T(8,128)(2,1)S(1)}, u32[]{:S(2)}, u32[]{:S(2)}) collective-permute-start(bf16[88,256]{1,0:T(8,128)(2,1)S(1)} %get-tuple-element.47), channel_id=1, source_target_pairs={{0,8},{4,12},{8,0},{12,4},{1,9},{5,13},{9,1},{13,5},{2,10},{6,14},... | collective-permute-start | bytes 135176 | tf_op jit(solution)/shard_map/ppermute | solution.py:317
  8.6 4.9 %collective-permute-start.4 = (bf16[88,256]{1,0:T(8,128)(2,1)S(1)}, bf16[88,256]{1,0:T(8,128)(2,1)S(1)}, u32[]{:S(2)}, u32[]{:S(2)}) collective-permute-start(bf16[88,256]{1,0:T(8,128)(2,1)S(1)} %get-tuple-element.48), channel_id=1, source_target_pairs={{0,4},{4,0},{8,12},{12,8},{1,5},{5,1},{9,13},{13,9},{2,6},{6,2},{1... | collective-permute-start | bytes 135176 | tf_op jit(solution)/shard_map/ppermute | solution.py:317
  9.9 1.3 %collective-permute-start.1 = (bf16[32,256]{1,0:T(8,128)(2,1)S(1)}, bf16[32,256]{1,0:T(8,128)(2,1)S(1)}, u32[]{:S(2)}, u32[]{:S(2)}) collective-permute-start(bf16[32,256]{1,0:T(8,128)(2,1)S(1)} %collective-permute-done.refs_1_), channel_id=1, source_target_pairs={{0,1},{1,0},{2,3},{3,2},{4,5},{5,4},{6,7},{7,6},{8,9},{9,8},{10,11... | collective-permute-start | bytes 49160 | tf_op jit(solution)/shard_map/ppermute | solution.py:317
  15.1 4.0 %collective-permute-start.6 = (f32[64,256]{1,0:T(8,128)S(1)}, f32[64,256]{1,0:T(8,128)S(1)}, u32[]{:S(2)}, u32[]{:S(2)}) collective-permute-start(f32[64,256]{1,0:T(8,128)S(1)} %get-tuple-element.62), channel_id=1, source_target_pairs={{0,3},{1,2},{2,1},{3,0},{4,7},{5,6},{6,5},{7,4},{8,11},{9,10},{10,... | collective-permute-start | bytes 196616 | tf_op jit(solution)/shard_map/ppermute | solution.py:317
  15.2 5.0 %collective-permute-start.7 = (f32[64,256]{1,0:T(8,128)S(1)}, f32[64,256]{1,0:T(8,128)S(1)}, u32[]{:S(2)}, u32[]{:S(2)}) collective-permute-start(f32[64,256]{1,0:T(8,128)S(1)} %get-tuple-element.63), channel_id=1, source_target_pairs={{0,2},{1,3},{2,0},{3,1},{4,6},{5,7},{6,4},{7,5},{8,10},{9,11},{10,... | collective-permute-start | bytes 196616 | tf_op jit(solution)/shard_map/ppermute | solution.py:317
  17.7 2.5 %collective-permute-start.8 = (f32[64,256]{1,0:T(8,128)S(1)}, f32[64,256]{1,0:T(8,128)S(1)}, u32[]{:S(2)}, u32[]{:S(2)}) collective-permute-start(f32[64,256]{1,0:T(8,128)S(1)} %get-tuple-element.67), channel_id=1, source_target_pairs={{0,1},{1,0},{2,3},{3,2},{4,5},{5,4},{6,7},{7,6},{8,9},{9,8},{10,11... | collective-permute-start | bytes 196616 | tf_op jit(solution)/shard_map/ppermute | solution.py:317
